TPU v7x, 32 devices: a whole 2x2x4 slice. The times are simulated.
32 devices in a mesh: shard: 2 (over x), ctx: 4 (over y, core), tp: 4 (over z).
Axes of the slice: x: 2, y: 2, z: 4, core: 2. Of those that a mesh axis runs over, the one named last changes fastest.
Arguments:
- tokens: bfloat16 [4, 2048, 1536], P('shard', 'ctx'), may hold values from -6 to 6
- segments: int32 [4, 2048], P('shard', 'ctx'), may hold values from 0 to 15, never falling along the last dimension, each value on 1 to 800 neighbouring positions
- norm_gain: bfloat16 [1536], P('shard'), may hold values from 0.5 to 1.5
- ffn_gain: bfloat16 [1536], P('shard'), may hold values from 0.5 to 1.5
- memory_gain: bfloat16 [16, 96], P('tp', 'shard'), may hold values from 0.5 to 1.5
- memory_rates: bfloat16 [2, 6144], P('shard'), may hold values from 0.19921875 to 0.9765625
- persistent: bfloat16 [64, 1536], P(None, 'shard'), may hold values from -6 to 6
- w_qkv: bfloat16 [3, 1536, 1536], P(None, 'shard', 'tp'), may hold values from -0.15625 to 0.15625
- w_out: bfloat16 [1536, 1536], P('tp', 'shard'), may hold values from -0.625 to 0.625
- w_value: bfloat16 [1536, 1536], P('shard', 'tp'), may hold values from -0.15625 to 0.15625
- w_feature: bfloat16 [1536, 6144], P('shard', 'tp'), may hold values from -0.15625 to 0.15625
- w_gate_up: bfloat16 [2, 1536, 4096], P(None, 'shard', 'tp'), may hold values from -0.15625 to 0.15625
- w_down: bfloat16 [4096, 1536], P('tp', 'shard'), may hold values from -0.09375 to 0.09375
- out_grad: bfloat16 [4, 2048, 1536], P('shard', 'ctx'), may hold values from -6 to 6
Outputs:
- output: bfloat16 [4, 2048, 1536], P('shard', 'ctx')
- input_grad: float32 [4, 2048, 1536], P('shard', 'ctx')
- grad_norm_gain: float32 [1536], P('shard')
- grad_ffn_gain: float32 [1536], P('shard')
- grad_memory_gain: float32 [16, 96], P('tp', 'shard')
- grad_memory_rates: float32 [2, 6144], P('shard', 'tp')
- grad_persistent: float32 [64, 1536], P(None, 'shard')
- grad_w_qkv: float32 [3, 1536, 1536], P(None, 'shard', 'tp')
- grad_w_out: float32 [1536, 1536], P('tp', 'shard')
- grad_w_value: float32 [1536, 1536], P('shard', 'tp')
- grad_w_feature: float32 [1536, 6144], P('shard', 'tp')
- grad_w_gate_up: float32 [2, 1536, 4096], P(None, 'shard', 'tp')
- grad_w_down: float32 [4096, 1536], P('tp', 'shard')
Inputs may be any that keep to these rules, and one draw needn't show every extreme that they name: `segments`: along each sequence the document numbers never fall; a document holds 1 to 800 positions, one exactly that many.
All inputs are finite; a program needn't handle non-finite values.
Results may differ from a plain program's by a relative error of at most 0.02.
Values may be sent and summed in bfloat16 or wider, within the bound.
A program may use at most 512 MiB of HBM per device.

v0:
```python
import jax
import jax.numpy as jnp
from jax import lax
from jax.sharding import PartitionSpec as P

HD = 96
SPAN = 256


EPSILON = 1e-06
MASKED = -1e30
WIDE = jnp.float32
NARROW = jnp.bfloat16


def passed_along(value, axis, steps):
    count = lax.axis_size(axis)
    initial, last = (max(0, -steps), min(count, count - steps))
    return lax.ppermute(value, axis, [(source, source + steps) for source in range(initial, last)])


def norm_rows(values, gain):
    factor = lax.rsqrt(jnp.mean(values * values, axis=-1, keepdims=True) + EPSILON)
    normed = values * factor
    return (normed * gain, normed, factor)


def norm_back(upstream, normed, factor, gain):
    inner = upstream * gain
    return factor * (inner - normed * jnp.mean(inner * normed, axis=-1, keepdims=True))


def silu_slope(values):
    sigmoid = jax.nn.sigmoid(values)
    return sigmoid * (1.0 + values * (1.0 - sigmoid))


def matmul(left, right):
    return jnp.dot(left, right, preferred_element_type=WIDE)


def over_rows(left, right):
    return lax.dot_general(left, right, (((0,), (0,)), ((), ())), preferred_element_type=WIDE)


def by_rows(left, right):
    return lax.dot_general(left, right, (((1,), (1,)), ((), ())), preferred_element_type=WIDE)


def exact_product(left, right):
    return jnp.dot(left, right, precision=lax.Precision.HIGHEST, preferred_element_type=WIDE)


def on_device(
    tokens,
    segments,
    norm_gain,
    ffn_gain,
    memory_gain,
    memory_rates,
    persistent,
    w_qkv,
    w_out,
    w_value,
    w_feature,
    w_gate_up,
    w_down,
    out_grad,
):
    gathered = (
        lax.all_gather(norm_gain, "shard", axis=0, tiled=True),
        lax.all_gather(ffn_gain, "shard", axis=0, tiled=True),
        lax.all_gather(memory_gain, "shard", axis=1, tiled=True),
        lax.all_gather(memory_rates, "shard", axis=0, tiled=True),
        lax.all_gather(persistent, "shard", axis=1, tiled=True),
        lax.all_gather(w_qkv, "shard", axis=1, tiled=True),
        lax.all_gather(w_out, "shard", axis=1, tiled=True),
        lax.all_gather(w_value, "shard", axis=0, tiled=True),
        lax.all_gather(w_feature, "shard", axis=0, tiled=True),
        lax.all_gather(w_gate_up, "shard", axis=1, tiled=True),
        lax.all_gather(w_down, "shard", axis=1, tiled=True),
    )
    (
        gain_in,
        gain_ffn,
        gain_memory,
        rates,
        persist,
        qkv_cols,
        out_rows,
        value_cols,
        feature_cols,
        gate_up_cols,
        down_rows,
    ) = gathered
    groups, local_len, width = tokens.shape
    rows = groups * local_len
    blocks_each = local_len // SPAN
    blocks = groups * blocks_each
    local_width = qkv_cols.shape[2]
    local_heads = local_width // HD
    persist_count = persist.shape[0]
    step = 6.0 / (SPAN + 8)
    scale = HD ** (-0.5)
    gain_in_wide = gain_in.astype(WIDE)
    gain_ffn_wide = gain_ffn.astype(WIDE)
    gain_mem = gain_memory.astype(WIDE)
    retain = rates[0].astype(WIDE)
    moment = rates[1].astype(WIDE)
    residual = tokens.reshape(rows, width).astype(WIDE)
    normed_in, unit_in, factor_in = norm_rows(residual, gain_in_wide)
    input_low = normed_in.astype(NARROW)
    preact = matmul(input_low, feature_cols)
    features = lax.all_gather(jax.nn.silu(preact).astype(NARROW), "tp", axis=1, tiled=True)
    feature_width = features.shape[1]
    key_scale = lax.rsqrt(jnp.sum(jnp.square(features.astype(WIDE)), axis=1) + EPSILON)
    targets = matmul(input_low, value_cols)
    features_seq = features.reshape(groups, blocks_each, SPAN, feature_width)
    scales_seq = key_scale.reshape(groups, blocks_each, SPAN)
    targets_seq = targets.reshape(groups, blocks_each, SPAN, local_width)
    labels = segments.astype(WIDE).reshape(groups, blocks_each, SPAN) + 1.0
    lasts = labels[:, :, -1]

    def masks_for(incoming):
        before = jnp.concatenate([incoming[:, None], lasts[:, :-1]], axis=1)
        keeping = (lasts == before).astype(WIDE)
        writing = (labels == lasts[:, :, None]).astype(WIDE)
        reading = (labels == before[:, :, None]).astype(WIDE)
        return (keeping, writing, reading)

    def chain_forward(memory, velocity, incoming, collect):
        keeping, writing, _ = masks_for(incoming)

        def advance(carry, index):
            memory, velocity = carry
            span_feat = lax.dynamic_index_in_dim(features_seq, index, 1, False)
            span_scale = lax.dynamic_index_in_dim(scales_seq, index, 1, False)[:, :, None]
            span_target = lax.dynamic_index_in_dim(targets_seq, index, 1, False)
            span_write = lax.dynamic_index_in_dim(writing, index, 1, False)
            span_keep = lax.dynamic_index_in_dim(keeping, index, 1, False)[:, None, None]
            recall = span_scale * jnp.einsum(
                "sci,sid->scd", span_feat, memory.astype(NARROW), preferred_element_type=WIDE
            )
            error = span_write[:, :, None] * (span_keep * recall - span_target)
            update = jnp.einsum(
                "sci,scd->sid",
                span_feat,
                (span_scale * error).astype(NARROW),
                preferred_element_type=WIDE,
            )
            new_velocity = span_keep * moment[None, :, None] * velocity - step * update
            new_memory = span_keep * retain[None, :, None] * memory + new_velocity
            if collect:
                return ((new_memory, new_velocity), (recall, memory, velocity))
            return ((new_memory, new_velocity), None)

        return lax.scan(advance, (memory, velocity), jnp.arange(blocks_each))

    empty = jnp.zeros((groups, feature_width, local_width), WIDE)

    def forward_round(turn, state):
        memory, velocity, incoming = state
        final, _ = chain_forward(memory, velocity, incoming, False)
        return passed_along((final[0], final[1], lasts[:, -1]), "ctx", 1)

    memory_in, velocity_in, label_in = lax.fori_loop(
        0, lax.axis_size("ctx") - 1, forward_round, (empty, empty, jnp.zeros((groups,), WIDE))
    )
    _, (recalls, memories, velocities) = chain_forward(memory_in, velocity_in, label_in, True)
    keeping, writing, reading = masks_for(label_in)
    recall_seq = jnp.swapaxes(recalls, 0, 1)
    heads_view = (reading[..., None] * recall_seq).reshape(rows, local_heads, HD)
    head_factor = lax.rsqrt(jnp.mean(heads_view * heads_view, axis=-1, keepdims=True) + EPSILON)
    head_unit = heads_view * head_factor
    retrieved = (head_unit * gain_mem).reshape(rows, local_width).astype(NARROW)
    retrieved_full = lax.all_gather(retrieved, "tp", axis=1, tiled=True)
    query_w = qkv_cols[0]
    key_w = qkv_cols[1]
    value_w = qkv_cols[2]

    def heads(values):
        return values.astype(NARROW).reshape(blocks, SPAN, local_heads, HD)

    def fixed(values):
        shaped = values.astype(NARROW).reshape(1, persist_count, local_heads, HD)
        return jnp.broadcast_to(shaped, (blocks, persist_count, local_heads, HD))

    queries = heads(matmul(input_low, query_w))
    keys = jnp.concatenate(
        [
            fixed(matmul(persist, key_w)),
            heads(matmul(retrieved_full, key_w)),
            heads(matmul(input_low, key_w)),
        ],
        axis=1,
    )
    values_all = jnp.concatenate(
        [
            fixed(matmul(persist, value_w)),
            heads(matmul(retrieved_full, value_w)),
            heads(matmul(input_low, value_w)),
        ],
        axis=1,
    )
    label_rows = labels.reshape(blocks, SPAN)
    read_rows = reading.reshape(blocks, SPAN)
    position = jnp.arange(SPAN)
    causal = position[:, None] >= position[None, :]
    visible_own = causal[None] & (label_rows[:, :, None] == label_rows[:, None, :])
    visible_memory = visible_own & (read_rows[:, None, :] > 0.5)
    visible = jnp.concatenate(
        [jnp.ones((blocks, SPAN, persist_count), jnp.bool_), visible_memory, visible_own], axis=2
    )

    def scores_of():
        raw = jnp.einsum("bthd,bkhd->bhtk", queries, keys, preferred_element_type=WIDE) * scale
        return jnp.where(visible[:, None], raw, MASKED)

    scores = scores_of()
    highest = jnp.max(scores, axis=-1, keepdims=True)
    raised = jnp.exp(scores - highest)
    totals = jnp.sum(raised, axis=-1, keepdims=True)
    logsum = highest + jnp.log(totals)
    probs_low = (raised / totals).astype(NARROW)
    attended = (
        jnp.einsum("bhtk,bkhd->bthd", probs_low, values_all, preferred_element_type=WIDE)
        .astype(NARROW)
        .reshape(rows, local_width)
    )
    mixed = lax.psum(matmul(attended, out_rows), "tp")
    hidden = residual + mixed
    normed_mid, unit_mid, factor_mid = norm_rows(hidden, gain_ffn_wide)
    mid_low = normed_mid.astype(NARROW)
    gate = matmul(mid_low, gate_up_cols[0])
    upper = matmul(mid_low, gate_up_cols[1])
    activ = (jax.nn.silu(gate) * upper).astype(NARROW)
    branch = lax.psum(matmul(activ, down_rows).astype(jnp.bfloat16), "tp").astype(jnp.float32)
    output = (hidden + branch).astype(NARROW).reshape(groups, local_len, width)
    upstream_low = out_grad.reshape(rows, width)
    upstream = upstream_low.astype(WIDE)
    grad_down = over_rows(activ, upstream_low)
    grad_act = by_rows(upstream_low, down_rows)
    grad_gate = (grad_act * upper * silu_slope(gate)).astype(NARROW)
    grad_upper = (grad_act * jax.nn.silu(gate)).astype(NARROW)
    grad_gate_up = jnp.stack([over_rows(mid_low, grad_gate), over_rows(mid_low, grad_upper)])
    grad_mid = lax.psum(
        by_rows(grad_gate, gate_up_cols[0]) + by_rows(grad_upper, gate_up_cols[1]), "tp"
    )
    grad_gain_ffn = jnp.sum(grad_mid * unit_mid, axis=0)
    grad_hidden = upstream + norm_back(grad_mid, unit_mid, factor_mid, gain_ffn_wide)
    grad_mixed = grad_hidden.astype(NARROW)
    grad_out_rows = over_rows(attended, grad_mixed)
    grad_attended = (
        by_rows(grad_mixed, out_rows).astype(NARROW).reshape(blocks, SPAN, local_heads, HD)
    )
    probs = jnp.exp(scores_of() - logsum)
    grad_probs = jnp.einsum(
        "bthd,bkhd->bhtk", grad_attended, values_all, preferred_element_type=WIDE
    )
    grad_values = jnp.einsum(
        "bhtk,bthd->bkhd", probs.astype(NARROW), grad_attended, preferred_element_type=WIDE
    )
    grad_scores = (
        probs * (grad_probs - jnp.sum(grad_probs * probs, axis=-1, keepdims=True))
    ).astype(NARROW)
    grad_queries = (
        (jnp.einsum("bhtk,bkhd->bthd", grad_scores, keys, preferred_element_type=WIDE) * scale)
        .astype(NARROW)
        .reshape(rows, local_width)
    )
    grad_keys = (
        jnp.einsum("bhtk,bthd->bkhd", grad_scores, queries, preferred_element_type=WIDE) * scale
    )

    def split_keys(grads):
        fixed_part = jnp.sum(grads[:, :persist_count], axis=0).reshape(persist_count, local_width)
        memory_part = (
            grads[:, persist_count : persist_count + SPAN].astype(NARROW).reshape(rows, local_width)
        )
        token_part = grads[:, persist_count + SPAN :].astype(NARROW).reshape(rows, local_width)
        return (fixed_part, memory_part, token_part)

    key_fixed, key_memory, key_token = split_keys(grad_keys)
    value_fixed, value_memory, value_token = split_keys(grad_values)
    persist_wide = persist.astype(WIDE)
    grad_query_w = over_rows(input_low, grad_queries)
    grad_key_w = (
        over_rows(input_low, key_token)
        + over_rows(retrieved_full, key_memory)
        + exact_product(persist_wide.T, key_fixed)
    )
    grad_value_proj = (
        over_rows(input_low, value_token)
        + over_rows(retrieved_full, value_memory)
        + exact_product(persist_wide.T, value_fixed)
    )
    grad_qkv = jnp.stack([grad_query_w, grad_key_w, grad_value_proj])
    grad_persist = exact_product(key_fixed, key_w.astype(WIDE).T) + exact_product(
        value_fixed, value_w.astype(WIDE).T
    )
    grad_input = (
        by_rows(grad_queries, query_w) + by_rows(key_token, key_w) + by_rows(value_token, value_w)
    )
    grad_retrieved = lax.psum_scatter(
        by_rows(key_memory, key_w) + by_rows(value_memory, value_w),
        "tp",
        scatter_dimension=1,
        tiled=True,
    )
    grad_heads = grad_retrieved.reshape(rows, local_heads, HD)
    grad_gain_memory = jnp.sum(grad_heads * head_unit, axis=0)
    inner = grad_heads * gain_mem
    grad_masked = head_factor * (
        inner - head_unit * jnp.mean(inner * head_unit, axis=-1, keepdims=True)
    )
    grad_read = reading[..., None] * grad_masked.reshape(groups, blocks_each, SPAN, local_width)

    def chain_backward(grad_memory, grad_velocity, collect):

        def retreat(carry, index):
            grad_memory, grad_velocity, grad_retain, grad_moment = carry
            memory = lax.dynamic_index_in_dim(memories, index, 0, False)
            velocity = lax.dynamic_index_in_dim(velocities, index, 0, False)
            span_feat = lax.dynamic_index_in_dim(features_seq, index, 1, False)
            span_scale = lax.dynamic_index_in_dim(scales_seq, index, 1, False)[:, :, None]
            span_target = lax.dynamic_index_in_dim(targets_seq, index, 1, False)
            span_write = lax.dynamic_index_in_dim(writing, index, 1, False)[:, :, None]
            span_keep = lax.dynamic_index_in_dim(keeping, index, 1, False)[:, None, None]
            span_grad = lax.dynamic_index_in_dim(grad_read, index, 1, False)
            memory_low = memory.astype(NARROW)
            raw_recall = jnp.einsum(
                "sci,sid->scd", span_feat, memory_low, preferred_element_type=WIDE
            )
            error = span_write * (span_keep * span_scale * raw_recall - span_target)
            grad_total = grad_velocity + grad_memory
            grad_update = (-step * grad_total).astype(NARROW)
            grad_scaled = jnp.einsum(
                "sci,sid->scd", span_feat, grad_update, preferred_element_type=WIDE
            )
            grad_error = span_scale * grad_scaled
            grad_recall = span_grad + span_write * span_keep * grad_error
            grad_raw = (span_scale * grad_recall).astype(NARROW)
            grad_feat = jnp.einsum(
                "scd,sid->sci",
                (span_scale * error).astype(NARROW),
                grad_update,
                preferred_element_type=WIDE,
            ) + jnp.einsum("scd,sid->sci", grad_raw, memory_low, preferred_element_type=WIDE)
            grad_scale = jnp.sum(error * grad_scaled + raw_recall * grad_recall, axis=2)
            grad_target = -span_write * grad_error
            grad_retain = grad_retain + jnp.sum(span_keep * grad_memory * memory, axis=(0, 2))
            grad_moment = grad_moment + jnp.sum(span_keep * grad_total * velocity, axis=(0, 2))
            next_memory = span_keep * retain[None, :, None] * grad_memory + jnp.einsum(
                "sci,scd->sid", span_feat, grad_raw, preferred_element_type=WIDE
            )
            next_velocity = span_keep * moment[None, :, None] * grad_total
            if collect:
                return (
                    (next_memory, next_velocity, grad_retain, grad_moment),
                    (grad_feat, grad_target, grad_scale),
                )
            return ((next_memory, next_velocity, grad_retain, grad_moment), None)

        zero_rates = jnp.zeros((feature_width,), WIDE)
        return lax.scan(
            retreat,
            (grad_memory, grad_velocity, zero_rates, zero_rates),
            jnp.arange(blocks_each),
            reverse=True,
        )

    def backward_round(turn, state):
        result, _ = chain_backward(state[0], state[1], False)
        return passed_along((result[0], result[1]), "ctx", -1)

    grad_mem_in, grad_vel_in = lax.fori_loop(
        0, lax.axis_size("ctx") - 1, backward_round, (empty, empty)
    )
    final, (grad_feats, grad_targets, grad_scales) = chain_backward(grad_mem_in, grad_vel_in, True)
    grad_feat_rows = jnp.swapaxes(grad_feats, 0, 1).reshape(rows, feature_width)
    scale_rows = jnp.swapaxes(grad_scales, 0, 1).reshape(rows)
    grad_feat_rows = grad_feat_rows - (key_scale * key_scale * key_scale * scale_rows)[
        :, None
    ] * features.astype(WIDE)
    grad_feat_own, grad_rates = (
        lax.psum_scatter(grad_feat_rows, "tp", scatter_dimension=1, tiled=True),
        lax.psum_scatter(jnp.stack([final[2], final[3]]), "tp", scatter_dimension=1, tiled=True),
    )
    grad_pre = (grad_feat_own * silu_slope(preact)).astype(NARROW)
    grad_feature_w = over_rows(input_low, grad_pre)
    grad_target_low = jnp.swapaxes(grad_targets, 0, 1).reshape(rows, local_width).astype(NARROW)
    grad_target_w = over_rows(input_low, grad_target_low)
    grad_input = grad_input + by_rows(grad_pre, feature_cols) + by_rows(grad_target_low, value_cols)
    grad_input, grad_persist = lax.psum((grad_input, grad_persist), "tp")
    grad_gain_in = jnp.sum(grad_input * unit_in, axis=0)
    grad_tokens = grad_hidden + norm_back(grad_input, unit_in, factor_in, gain_in_wide)
    local_grads = (
        grad_gain_in,
        grad_gain_ffn,
        grad_gain_memory,
        grad_rates,
        grad_persist,
        grad_qkv,
        grad_out_rows,
        grad_target_w,
        grad_feature_w,
        grad_gate_up,
        grad_down,
    )
    summed = lax.psum(
        (
            local_grads[0],
            local_grads[1],
            local_grads[2],
            local_grads[3],
            local_grads[4],
            local_grads[5],
            local_grads[6],
            local_grads[7],
            local_grads[8],
            local_grads[9],
            local_grads[10],
        ),
        "ctx",
    )
    shared = (
        lax.psum_scatter(summed[0], "shard", scatter_dimension=0, tiled=True),
        lax.psum_scatter(summed[1], "shard", scatter_dimension=0, tiled=True),
        lax.psum_scatter(summed[2], "shard", scatter_dimension=1, tiled=True),
        lax.psum_scatter(summed[3], "shard", scatter_dimension=0, tiled=True),
        lax.psum_scatter(summed[4], "shard", scatter_dimension=1, tiled=True),
        lax.psum_scatter(summed[5], "shard", scatter_dimension=1, tiled=True),
        lax.psum_scatter(summed[6], "shard", scatter_dimension=1, tiled=True),
        lax.psum_scatter(summed[7], "shard", scatter_dimension=0, tiled=True),
        lax.psum_scatter(summed[8], "shard", scatter_dimension=0, tiled=True),
        lax.psum_scatter(summed[9], "shard", scatter_dimension=1, tiled=True),
        lax.psum_scatter(summed[10], "shard", scatter_dimension=1, tiled=True),
    )
    return (
        output,
        grad_tokens.reshape(groups, local_len, width),
        shared[0],
        shared[1],
        shared[2],
        shared[3],
        shared[4],
        shared[5],
        shared[6],
        shared[7],
        shared[8],
        shared[9],
        shared[10],
    )


def solution(mesh):
    placed = (
        P("shard", "ctx", None),
        P("shard", "ctx"),
        P("shard"),
        P("shard"),
        P("tp", "shard"),
        P("shard", None),
        P(None, "shard"),
        P(None, "shard", "tp"),
        P("tp", "shard"),
        P("shard", "tp"),
        P("shard", "tp"),
        P(None, "shard", "tp"),
        P("tp", "shard"),
        P("shard", "ctx", None),
    )
    return jax.shard_map(
        on_device,
        mesh=mesh,
        in_specs=placed,
        out_specs=(
            P("shard", "ctx", None),
            P("shard", "ctx", None),
            P("shard"),
            P("shard"),
            P("tp", "shard"),
            P("shard", "tp"),
            P(None, "shard"),
            P(None, "shard", "tp"),
            P("tp", "shard"),
            P("shard", "tp"),
            P("shard", "tp"),
            P(None, "shard", "tp"),
            P("tp", "shard"),
        ),
        check_vma=False,
    )
```

profile of v0, /device:TPU:1, one launch (start us, length us, event | category | flops | bytes accessed | tf_op | source)
XLA Modules:
  0.0 6653.7 jit_solution(1468046182782887614)
XLA Ops:
  103.0 216.6 %all-gather.17.cloned.1.call-done = bf16[1024,6144]{1,0:T(8,128)(2,1)} async-done(((bf16[1024,1536]{1,0:T(8,128)(2,1)}), bf16[1024,6144]{1,0:T(8,128)(2,1)}) %all-gather.17.cloned.1.call-update) | async-done | bytes 12582928 | tf_op jit(solution)/shard_map/all_gather | solution.py:114
  353.4 1518.5 %while.127 = (s32[]{:T(128)}, f32[2,6144,384]{2,1,0:T(8,128)}, f32[2,6144,384]{2,1,0:T(8,128)}, f32[2]{0:T(128)S(1)}, f32[2,2,1]{1,0,2:T(2,128)S(1)}, /*index=5*...) while((s32[]{:T(128)}, f32[2,6144,384]{2,1,0:T(8,128)}, ...), condition=%wide.region_5.6_spmd, body=%wide.region_2.5_spmd.sunk | while | flops 4861356032 | bytes 335321280 | solution.py:166
  441.2 201.0 %collective-permute-done.2 = f32[2,6144,384]{2,1,0:T(8,128)} collective-permute-done((f32[2,6144,384]{2,1,0:T(8,128)}, f32[2,6144,384]{2,1,0:T(8,128)}, u32[]{:S(2)}, u32[]{:S(2)}) %collective-permute-start.2) | collective-permute-done | bytes 18874400 | tf_op jit(solution)/shard_map/while/body/eval_jaxpr/ppermute | solution.py:19
  656.7 187.7 %collective-permute-done.3 = f32[2,6144,384]{2,1,0:T(8,128)} collective-permute-done((f32[2,6144,384]{2,1,0:T(8,128)}, f32[2,6144,384]{2,1,0:T(8,128)}, u32[]{:S(2)}, u32[]{:S(2)}) %collective-permute-start.3) | collective-permute-done | bytes 18874400 | tf_op jit(solution)/shard_map/while/body/eval_jaxpr/ppermute | solution.py:19
  947.6 201.1 %collective-permute-done.2 = f32[2,6144,384]{2,1,0:T(8,128)} collective-permute-done((f32[2,6144,384]{2,1,0:T(8,128)}, f32[2,6144,384]{2,1,0:T(8,128)}, u32[]{:S(2)}, u32[]{:S(2)}) %collective-permute-start.2) | collective-permute-done | bytes 18874400 | tf_op jit(solution)/shard_map/while/body/eval_jaxpr/ppermute | solution.py:19
  1163.2 187.7 %collective-permute-done.3 = f32[2,6144,384]{2,1,0:T(8,128)} collective-permute-done((f32[2,6144,384]{2,1,0:T(8,128)}, f32[2,6144,384]{2,1,0:T(8,128)}, u32[]{:S(2)}, u32[]{:S(2)}) %collective-permute-start.3) | collective-permute-done | bytes 18874400 | tf_op jit(solution)/shard_map/while/body/eval_jaxpr/ppermute | solution.py:19
  1454.1 201.1 %collective-permute-done.2 = f32[2,6144,384]{2,1,0:T(8,128)} collective-permute-done((f32[2,6144,384]{2,1,0:T(8,128)}, f32[2,6144,384]{2,1,0:T(8,128)}, u32[]{:S(2)}, u32[]{:S(2)}) %collective-permute-start.2) | collective-permute-done | bytes 18874400 | tf_op jit(solution)/shard_map/while/body/eval_jaxpr/ppermute | solution.py:19
  1669.7 187.7 %collective-permute-done.3 = f32[2,6144,384]{2,1,0:T(8,128)} collective-permute-done((f32[2,6144,384]{2,1,0:T(8,128)}, f32[2,6144,384]{2,1,0:T(8,128)}, u32[]{:S(2)}, u32[]{:S(2)}) %collective-permute-start.3) | collective-permute-done | bytes 18874400 | tf_op jit(solution)/shard_map/while/body/eval_jaxpr/ppermute | solution.py:19
  1873.0 172.5 %while.128 = (s32[]{:T(128)}, f32[2,6144,384]{2,1,0:T(8,128)}, f32[2,6144,384]{2,1,0:T(8,128)}, f32[2,2,256,384]{2,0,1,3:T(2,128)}, f32[2,2,6144,384]{3,2,1,0:T(...) while((s32[]{:T(128)}, f32[2,6144,384]{2,1,0:T(8,128)}, ...), condition=%wide.region_7.8_spmd, body=%wide.region_6.7_spmd.sunk | while | flops 4861353984 | bytes 188219632 | solution.py:157
  2172.9 216.8 %all-reduce.13.cloned.1.call-done = f32[1024,1536]{1,0:T(8,128)} async-done(((f32[1024,1536]{1,0:T(8,128)}), f32[1024,1536]{1,0:T(8,128)}) %all-reduce.13.cloned.1.call-update) | async-done | bytes 6291472 | tf_op jit(solution)/shard_map/psum | solution.py:230
  2548.9 214.5 %all-reduce.17.cloned.1.call-done = f32[1024,1536]{1,0:T(8,128)} async-done(((f32[1024,1536]{1,0:T(8,128)}), f32[1024,1536]{1,0:T(8,128)}) %all-reduce.17.cloned.1.call-update) | async-done | bytes 6291472 | tf_op jit(solution)/shard_map/psum | solution.py:246
  3082.3 1667.8 %while.130 = (s32[]{:T(128)}, f32[2,6144,384]{2,1,0:T(8,128)}, f32[2,6144,384]{2,1,0:T(8,128)}, f32[2,2]{0,1:T(2,128)S(1)}, f32[6144]{0:T(1024)S(1)}, /*index=5*...) while((s32[]{:T(128)}, f32[2,6144,384]{2,1,0:T(8,128)}, ...), condition=%wide.region_22.23_spmd, body=%wide.region_19.22_spmd.sunk | while | flops 4865876480 | bytes 486274688 | solution.py:376
  3082.3 131.6 %while.133 = (s32[]{:T(128)}, f32[2,6144,384]{2,1,0:T(8,128)}, f32[2,6144,384]{2,1,0:T(8,128)}, s32[2]{0:T(128)S(1)}, f32[2,2]{0,1:T(2,128)S(1)}, /*index=5*/f32...) while((s32[]{:T(128)}, f32[2,6144,384]{2,1,0:T(8,128)}, ...), condition=%wide.region_21.21_spmd, body=%wide.region_20.20_spmd.sunk | while | flops 4865876480 | bytes 259781888 | solution.py:365
  3218.5 202.9 %collective-permute-done = f32[2,6144,384]{2,1,0:T(8,128)} collective-permute-done((f32[2,6144,384]{2,1,0:T(8,128)}, f32[2,6144,384]{2,1,0:T(8,128)}, u32[]{:S(2)}, u32[]{:S(2)}) %collective-permute-start) | collective-permute-done | bytes 18874400 | tf_op jit(solution)/shard_map/while/body/eval_jaxpr/ppermute | solution.py:19
  3436.0 187.6 %collective-permute-done.1 = f32[2,6144,384]{2,1,0:T(8,128)} collective-permute-done((f32[2,6144,384]{2,1,0:T(8,128)}, f32[2,6144,384]{2,1,0:T(8,128)}, u32[]{:S(2)}, u32[]{:S(2)}) %collective-permute-start.1) | collective-permute-done | bytes 18874400 | tf_op jit(solution)/shard_map/while/body/eval_jaxpr/ppermute | solution.py:19
  3773.8 203.6 %collective-permute-done = f32[2,6144,384]{2,1,0:T(8,128)} collective-permute-done((f32[2,6144,384]{2,1,0:T(8,128)}, f32[2,6144,384]{2,1,0:T(8,128)}, u32[]{:S(2)}, u32[]{:S(2)}) %collective-permute-start) | collective-permute-done | bytes 18874400 | tf_op jit(solution)/shard_map/while/body/eval_jaxpr/ppermute | solution.py:19
  3991.9 187.6 %collective-permute-done.1 = f32[2,6144,384]{2,1,0:T(8,128)} collective-permute-done((f32[2,6144,384]{2,1,0:T(8,128)}, f32[2,6144,384]{2,1,0:T(8,128)}, u32[]{:S(2)}, u32[]{:S(2)}) %collective-permute-start.1) | collective-permute-done | bytes 18874400 | tf_op jit(solution)/shard_map/while/body/eval_jaxpr/ppermute | solution.py:19
  4329.6 203.6 %collective-permute-done = f32[2,6144,384]{2,1,0:T(8,128)} collective-permute-done((f32[2,6144,384]{2,1,0:T(8,128)}, f32[2,6144,384]{2,1,0:T(8,128)}, u32[]{:S(2)}, u32[]{:S(2)}) %collective-permute-start) | collective-permute-done | bytes 18874400 | tf_op jit(solution)/shard_map/while/body/eval_jaxpr/ppermute | solution.py:19
  4547.8 187.6 %collective-permute-done.1 = f32[2,6144,384]{2,1,0:T(8,128)} collective-permute-done((f32[2,6144,384]{2,1,0:T(8,128)}, f32[2,6144,384]{2,1,0:T(8,128)}, u32[]{:S(2)}, u32[]{:S(2)}) %collective-permute-start.1) | collective-permute-done | bytes 18874400 | tf_op jit(solution)/shard_map/while/body/eval_jaxpr/ppermute | solution.py:19
  4763.9 240.7 %while.131 = (s32[]{:T(128)}, f32[2,6144,384]{2,1,0:T(8,128)}, f32[2,6144,384]{2,1,0:T(8,128)}, f32[6144]{0:T(1024)S(1)}, f32[6144]{0:T(1024)S(1)}, /*index=5*/f...) while((s32[]{:T(128)}, f32[2,6144,384]{2,1,0:T(8,128)}, ...), condition=%wide.region_27.28_spmd.clone, body=%wide.region_23.27_spmd.clone.sunk | while | flops 12152574976 | bytes 297363328 | solution.py:365
  5134.8 320.8 %reduce-scatter.18.cloned.1.call-done = f32[1024,1536]{1,0:T(8,128)} async-done(((f32[1024,6144]{1,0:T(8,128)}), f32[1024,1536]{1,0:T(8,128)}) %reduce-scatter.18.cloned.1.call-update) | async-done | bytes 6291472 | tf_op jit(solution)/shard_map/reduce_scatter | solution.py:386
  5714.4 146.9 %reduce-scatter.28.cloned.1.call-done = f32[2,768,1024]{2,1,0:T(8,128)} async-done(((f32[2,1536,1024]{2,1,0:T(8,128)}), f32[2,768,1024]{2,1,0:T(8,128)}) %reduce-scatter.28.cloned.1.call-update) | async-done | bytes 6291472 | tf_op jit(solution)/shard_map/reduce_scatter | solution.py:436
  5861.3 232.1 %all-reduce.19.cloned.1.call-done = (f32[1024,1536]{1,0:T(8,128)}, f32[64,768]{1,0:T(8,128)}) async-done(((f32[1024,1536]{1,0:T(8,128)}, f32[64,768]{1,0:T(8,128)}), (f32[1024,1536]{1,0:T(8,128)}, f32[64,768]{1,0:T(8,128)})) %all-reduce.19.cloned.1.call-update) | async-done | bytes 6488080 | tf_op jit(solution)/shard_map/psum | solution.py:394
  6314.9 313.7 %all-reduce.21.cloned.1.call-done = (f32[64,768]{1,0:T(8,128)}, f32[3,768,384]{2,1,0:T(8,128)}, f32[384,768]{1,0:T(8,128)}, f32[768,384]{1,0:T(8,128)}, f32[768,...) async-done(((f32[64,768]{1,0:T(8,128)}, f32[3,768,384]{2,1,0:T(8,128)}, f32[384,768]{1,0:T(8,128)}, f32[768,384]{1,0:T(8,128)}, f32[768,1536]{1,0:T(8,128)}, ...) | async-done | bytes 20250640 | tf_op jit(solution)/shard_map/psum | solution.py:410
  (770 shorter events, 3111.3 us)
Async XLA Ops:
  84.9 1988.5 %all-gather.13.cloned.1.call-start = ((), (), s32[]{:S(2)}) async-start(), calls=%async_computation.11 | async-start | bytes 5308416 | tf_op jit(solution)/shard_map/all_gather | solution.py:76
  89.7 2038.6 %all-gather.21.cloned.1.call-start = ((), (), s32[]{:S(2)}) async-start(), calls=%async_computation.15 | async-start | bytes 3932160 | tf_op jit(solution)/shard_map/all_gather | solution.py:176
  439.2 405.3 %collective-permute-start.3 = (f32[2,6144,384]{2,1,0:T(8,128)}, f32[2,6144,384]{2,1,0:T(8,128)}, u32[]{:S(2)}, u32[]{:S(2)}) collective-permute-start(f32[2,6144,384]{2,1,0:T(8,128)} %get-tuple-element.2058), channel_id=1, source_target_pairs={{0,4},{4,8},{8,12},{1,5},{5,9},{9,13},{2,6},{6,10},{10,14},{3,7},{... | collective-permute-start | bytes 56623112 | tf_op jit(solution)/shard_map/while/body/eval_jaxpr/ppermute | solution.py:19
  945.6 405.3 %collective-permute-start.3 = (f32[2,6144,384]{2,1,0:T(8,128)}, f32[2,6144,384]{2,1,0:T(8,128)}, u32[]{:S(2)}, u32[]{:S(2)}) collective-permute-start(f32[2,6144,384]{2,1,0:T(8,128)} %get-tuple-element.2058), channel_id=1, source_target_pairs={{0,4},{4,8},{8,12},{1,5},{5,9},{9,13},{2,6},{6,10},{10,14},{3,7},{... | collective-permute-start | bytes 56623112 | tf_op jit(solution)/shard_map/while/body/eval_jaxpr/ppermute | solution.py:19
  1452.1 405.3 %collective-permute-start.3 = (f32[2,6144,384]{2,1,0:T(8,128)}, f32[2,6144,384]{2,1,0:T(8,128)}, u32[]{:S(2)}, u32[]{:S(2)}) collective-permute-start(f32[2,6144,384]{2,1,0:T(8,128)} %get-tuple-element.2058), channel_id=1, source_target_pairs={{0,4},{4,8},{8,12},{1,5},{5,9},{9,13},{2,6},{6,10},{10,14},{3,7},{... | collective-permute-start | bytes 56623112 | tf_op jit(solution)/shard_map/while/body/eval_jaxpr/ppermute | solution.py:19
  2168.8 348.2 %all-gather.27.cloned.1.call-start = ((), (), s32[]{:S(2)}) async-start(), calls=%async_computation.19 | async-start | bytes 4718592 | tf_op jit(solution)/shard_map/all_gather | solution.py:81
  2169.5 593.8 %all-reduce.17.cloned.1.call-start = ((), (), s32[]{:S(2)}) async-start(), calls=%async_computation.21 | async-start | bytes 12582912 | tf_op jit(solution)/shard_map/psum | solution.py:246
  2540.4 346.0 %all-reduce.15.cloned.1.call-start = ((), (), s32[]{:S(2)}) async-start(), calls=%async_computation.20 | async-start | bytes 6291456 | tf_op jit(solution)/shard_map/psum | solution.py:237
  2548.1 504.2 %reduce-scatter.16.cloned.1.call-start = ((), (), s32[]{:S(2)}) async-start(), calls=%async_computation.22 | async-start | bytes 7864320 | tf_op jit(solution)/shard_map/reduce_scatter | solution.py:304
  2942.3 2513.4 %reduce-scatter.18.cloned.1.call-start = ((), (), s32[]{:S(2)}) async-start(), calls=%async_computation.23 | async-start | bytes 31457280 | tf_op jit(solution)/shard_map/reduce_scatter | solution.py:386
  3216.6 407.1 %collective-permute-start.1 = (f32[2,6144,384]{2,1,0:T(8,128)}, f32[2,6144,384]{2,1,0:T(8,128)}, u32[]{:S(2)}, u32[]{:S(2)}) collective-permute-start(f32[2,6144,384]{2,1,0:T(8,128)} %get-tuple-element.2093), channel_id=1, source_target_pairs={{4,0},{8,4},{12,8},{5,1},{9,5},{13,9},{6,2},{10,6},{14,10},{7,3},{... | collective-permute-start | bytes 56623112 | tf_op jit(solution)/shard_map/while/body/eval_jaxpr/ppermute | solution.py:19
  3771.8 407.7 %collective-permute-start.1 = (f32[2,6144,384]{2,1,0:T(8,128)}, f32[2,6144,384]{2,1,0:T(8,128)}, u32[]{:S(2)}, u32[]{:S(2)}) collective-permute-start(f32[2,6144,384]{2,1,0:T(8,128)} %get-tuple-element.2093), channel_id=1, source_target_pairs={{4,0},{8,4},{12,8},{5,1},{9,5},{13,9},{6,2},{10,6},{14,10},{7,3},{... | collective-permute-start | bytes 56623112 | tf_op jit(solution)/shard_map/while/body/eval_jaxpr/ppermute | solution.py:19
  4327.7 407.7 %collective-permute-start.1 = (f32[2,6144,384]{2,1,0:T(8,128)}, f32[2,6144,384]{2,1,0:T(8,128)}, u32[]{:S(2)}, u32[]{:S(2)}) collective-permute-start(f32[2,6144,384]{2,1,0:T(8,128)} %get-tuple-element.2093), channel_id=1, source_target_pairs={{4,0},{8,4},{12,8},{5,1},{9,5},{13,9},{6,2},{10,6},{14,10},{7,3},{... | collective-permute-start | bytes 56623112 | tf_op jit(solution)/shard_map/while/body/eval_jaxpr/ppermute | solution.py:19
  5042.3 439.3 %reduce-scatter.32.cloned.1.call-start = ((), (), s32[]{:S(2)}) async-start(), calls=%async_computation.30 | async-start | bytes 589824 | tf_op jit(solution)/shard_map/reduce_scatter | solution.py:431
  5048.3 461.4 %reduce-scatter.22.cloned.1.call-start = ((), (), s32[]{:S(2)}) async-start(), calls=%async_computation.25 | async-start | bytes 3538944 | tf_op jit(solution)/shard_map/reduce_scatter | solution.py:433
  5054.7 534.4 %reduce-scatter.30.cloned.1.call-start = ((), (), s32[]{:S(2)}) async-start(), calls=%async_computation.29 | async-start | bytes 9437184 | tf_op jit(solution)/shard_map/reduce_scatter | solution.py:437
  5063.3 613.6 %reduce-scatter.20.cloned.1.call-start = ((), (), s32[]{:S(2)}) async-start(), calls=%async_computation.24 | async-start | bytes 10616832 | tf_op jit(solution)/shard_map/reduce_scatter | solution.py:432
  5088.2 626.2 %reduce-scatter.24.cloned.1.call-start = ((), (), s32[]{:S(2)}) async-start(), calls=%async_computation.26 | async-start | bytes 3538944 | tf_op jit(solution)/shard_map/reduce_scatter | solution.py:434
  5093.6 767.7 %reduce-scatter.28.cloned.1.call-start = ((), (), s32[]{:S(2)}) async-start(), calls=%async_computation.28 | async-start | bytes 18874368 | tf_op jit(solution)/shard_map/reduce_scatter | solution.py:436
  5119.8 973.6 %all-reduce.19.cloned.1.call-start = ((), (), s32[]{:S(2)}) async-start(), calls=%async_computation.33 | async-start | bytes 12976128 | tf_op jit(solution)/shard_map/psum | solution.py:394
  5481.6 723.8 %reduce-scatter.26.cloned.1.call-start = ((), (), s32[]{:S(2)}) async-start(), calls=%async_computation.27 | async-start | bytes 14155776 | tf_op jit(solution)/shard_map/reduce_scatter | solution.py:435
  5493.2 724.6 %reduce-scatter.36.cloned.1.call-start = ((), (), s32[]{:S(2)}) async-start(), calls=%async_computation.32 | async-start | bytes 73728
  5497.5 783.7 %reduce-scatter.34.cloned.1.call-start = ((), (), s32[]{:S(2)}) async-start(), calls=%async_computation.31 | async-start | bytes 3932160
  5499.9 1128.8 %all-reduce.21.cloned.1.call-start = ((), (), s32[]{:S(2)}) async-start(), calls=%async_computation.34 | async-start | bytes 40501248 | tf_op jit(solution)/shard_map/psum | solution.py:410
  (171 other events, 8666.9 us)
Sparse Core Ops, SparseCore 0:
  9.5 64.5 all-gather.14
  75.6 23.2 all-gather.18
  101.1 218.5 all-gather.16
  321.1 47.1 all-gather.12
  2066.2 61.9 all-gather.20
  2129.6 21.3 all-gather.22
  2168.2 221.4 all-reduce.12
  2391.2 79.2 all-gather.24
  2472.1 44.8 all-gather.26
  2540.5 222.8 all-reduce.16
  2766.3 119.9 all-reduce.14
  2942.4 109.8 reduce-scatter.15
  5042.4 413.2 reduce-scatter.17
  5457.8 15.0 reduce-scatter.31
  5474.9 34.7 reduce-scatter.21
  5511.9 77.1 reduce-scatter.29
  5591.2 85.6 reduce-scatter.19
  5679.6 34.7 reduce-scatter.23
  5716.7 144.5 reduce-scatter.27
  5864.2 229.2 all-reduce.18
  6095.8 109.5 reduce-scatter.25
  6208.1 9.6 reduce-scatter.35
  6220.6 60.5 reduce-scatter.33
  6284.4 344.2 all-reduce.20
where the time goes:
time: 6670 us; the launch traced here: 6650 us
  waiting for transfers between devices  4800 us (72%)
  matrix products  874 us (13%)
  local copies, waits for them, and re-layouts  521 us (8%)
  other arithmetic  332 us (5%)
    ppermute x13, waiting for transfers between devices, passed_along(): lax.ppermute(value, axis, [(source, source + steps) for source in range(i...  2340 us
    reduce_scatter x1, waiting for transfers between devices, on_device(): lax.psum_scatter(grad_feat_rows, 'tp', scatter_dimension=1, tiled=True)  321 us
    psum x1, waiting for transfers between devices, on_device(): lax.psum((local_grads[0], local_grads[1], local_grads[2], local_grads[3],...  314 us
    while x83, local copies, waits for them, and re-layouts  238 us
    psum x1, waiting for transfers between devices, on_device(): grad_input, grad_persist = lax.psum((grad_input, grad_persist), 'tp')  232 us
    dot_general x8, matrix products, advance(): jnp.einsum('sci,scd->sid', span_feat, (span_scale * error).astype(NARROW)...  217 us
    psum x1, waiting for transfers between devices, on_device(): mixed = lax.psum(matmul(attended, out_rows), 'tp')  217 us
    all_gather x1, waiting for transfers between devices, on_device(): lax.all_gather(jax.nn.silu(preact).astype(NARROW), 'tp', axis=1, tiled=True)  217 us
  transfers between devices with their start and end apart: 37, of which 33 were waited for; matrix products, arithmetic and copies ran while one was open for 13% of the time, Pallas kernels for 0%

commit v1 on v0

v1 whole, which is shorter than its diff:
```python
import jax
import jax.numpy as jnp
from jax import lax
from jax.sharding import PartitionSpec as P

HD = 96
SPAN = 256
LIMIT = 800
LAGS = (LIMIT + SPAN - 2) // SPAN


EPSILON = 1e-06
MASKED = -1e30
WIDE = jnp.float32
NARROW = jnp.bfloat16


def passed_along(value, axis, steps):
    count = lax.axis_size(axis)
    initial, last = (max(0, -steps), min(count, count - steps))
    return lax.ppermute(value, axis, [(source, source + steps) for source in range(initial, last)])


def norm_rows(values, gain):
    factor = lax.rsqrt(jnp.mean(values * values, axis=-1, keepdims=True) + EPSILON)
    normed = values * factor
    return (normed * gain, normed, factor)


def norm_back(upstream, normed, factor, gain):
    inner = upstream * gain
    return factor * (inner - normed * jnp.mean(inner * normed, axis=-1, keepdims=True))


def silu_slope(values):
    sigmoid = jax.nn.sigmoid(values)
    return sigmoid * (1.0 + values * (1.0 - sigmoid))


def matmul(left, right):
    return jnp.dot(left, right, preferred_element_type=WIDE)


def over_rows(left, right):
    return lax.dot_general(left, right, (((0,), (0,)), ((), ())), preferred_element_type=WIDE)


def by_rows(left, right):
    return lax.dot_general(left, right, (((1,), (1,)), ((), ())), preferred_element_type=WIDE)


def exact_product(left, right):
    return jnp.dot(left, right, precision=lax.Precision.HIGHEST, preferred_element_type=WIDE)


def batched(spec, left, right):
    return jnp.einsum(spec, left, right, preferred_element_type=WIDE)


def on_device(
    tokens,
    segments,
    norm_gain,
    ffn_gain,
    memory_gain,
    memory_rates,
    persistent,
    w_qkv,
    w_out,
    w_value,
    w_feature,
    w_gate_up,
    w_down,
    out_grad,
):
    def whole(array, axis):
        return lax.all_gather(array, "shard", axis=axis, tiled=True)

    feature_cols = whole(w_feature, 0)
    value_cols = whole(w_value, 0)
    qkv_cols = whole(w_qkv, 1)
    out_rows = whole(w_out, 1)
    gate_up_cols = whole(w_gate_up, 1)
    down_rows = whole(w_down, 1)
    persist = whole(persistent, 1)
    gain_in_wide = whole(norm_gain, 0).astype(WIDE)
    gain_ffn_wide = whole(ffn_gain, 0).astype(WIDE)
    gain_mem = whole(memory_gain, 1).astype(WIDE)
    rates = whole(memory_rates, 0)

    groups, local_len, width = tokens.shape
    rows = groups * local_len
    blocks_each = local_len // SPAN
    blocks = groups * blocks_each
    local_width = qkv_cols.shape[2]
    local_units = feature_cols.shape[1]
    local_heads = local_width // HD
    persist_count = persist.shape[0]
    parts, ranks = (lax.axis_size("ctx"), lax.axis_size("tp"))
    part, rank = (lax.axis_index("ctx"), lax.axis_index("tp"))
    total_blocks = parts * blocks_each
    reach = -(-LAGS // blocks_each)
    step = 6.0 / (SPAN + 8)
    scale = HD ** (-0.5)
    sub = rows // ranks

    def own_rows(array):
        return lax.dynamic_slice_in_dim(array, rank * sub, sub, 0)

    def scattered(array):
        return lax.psum_scatter(
            array.astype(NARROW), "tp", scatter_dimension=0, tiled=True
        ).astype(WIDE)

    def collected(array):
        return lax.all_gather(array.astype(NARROW), "tp", axis=0, tiled=True)

    flat_tokens = tokens.reshape(rows, width)
    all_tokens = lax.all_gather(tokens, "ctx", axis=1, tiled=True)
    all_labels = lax.all_gather(segments, "ctx", axis=1, tiled=True).astype(WIDE) + 1.0
    block_lasts = all_labels.reshape(groups, total_blocks, SPAN)[:, :, -1]
    own_units = lax.dynamic_slice_in_dim(rates.astype(WIDE), rank * local_units, local_units, 1)
    retain, moment = (own_units[0], own_units[1])
    decays = [jnp.ones_like(retain)]
    for lag in range(1, LAGS):
        decays.append(retain * decays[-1] + moment**lag)

    input_low = norm_rows(flat_tokens.astype(WIDE), gain_in_wide)[0].astype(NARROW)
    preact = matmul(input_low, feature_cols)
    features = jax.nn.silu(preact).astype(NARROW)
    all_low = norm_rows(
        all_tokens.reshape(groups * parts * local_len, width).astype(WIDE), gain_in_wide
    )[0].astype(NARROW)
    all_features = (
        jax.nn.silu(matmul(all_low, feature_cols))
        .astype(NARROW)
        .reshape(groups, total_blocks, SPAN, local_units)
    )
    squares = jnp.sum(jnp.square(features.astype(WIDE)), axis=1)
    key_scale = lax.rsqrt(lax.psum(squares, "tp") + EPSILON)
    scales = key_scale.reshape(groups, blocks_each, SPAN, 1)
    targets = matmul(input_low, value_cols).reshape(groups, blocks_each, SPAN, local_width)
    first = part * blocks_each

    def block_of(index):
        return lax.dynamic_index_in_dim(
            all_features, jnp.clip(index, 0, total_blocks - 1), 1, False
        )

    def last_of(index):
        found = lax.dynamic_index_in_dim(
            block_lasts, jnp.clip(index, 0, total_blocks - 1), 1, False
        )
        return jnp.where(index >= 0, found, 0.0)

    own_features = features.reshape(groups, blocks_each, SPAN, local_units)
    weighted = [
        (own_features.astype(WIDE) * decay).astype(NARROW) for decay in decays
    ]
    products = []
    linked = []
    for own in range(blocks_each):
        row = []
        links = []
        for lag in range(LAGS):
            source = first + own - 1 - lag
            row.append(batched("sth,suh->stu", weighted[lag][:, own], block_of(source)))
            links.append((source >= 0) & (last_of(source) == last_of(first + own - 1)))
        products.append(jnp.stack(row, axis=1))
        linked.append(jnp.stack(links, axis=1))
    products = jnp.stack(products, axis=1).astype(NARROW)
    linked = jnp.stack(linked, axis=1)
    mixing = lax.psum(products, "tp")
    mixing = jnp.where(linked[..., None, None], mixing, jnp.zeros_like(mixing))

    labels = segments.astype(WIDE).reshape(groups, blocks_each, SPAN) + 1.0
    lasts = labels[:, :, -1]
    before = jnp.stack([last_of(first + own - 1) for own in range(blocks_each)], axis=1)
    keeping = (lasts == before).astype(WIDE)[:, :, None, None]
    writing = (labels == lasts[:, :, None]).astype(WIDE)[..., None]
    reading = (labels == before[:, :, None]).astype(WIDE)

    halo = jnp.zeros((groups, reach * blocks_each, SPAN, local_width), NARROW)

    def advance(halo):
        known = [halo[:, index] for index in range(reach * blocks_each)]
        recalls = []
        errors = []
        for own in range(blocks_each):
            total = 0.0
            for lag in range(LAGS):
                total = total + batched(
                    "stu,sud->std", mixing[:, own, lag], known[reach * blocks_each + own - 1 - lag]
                )
            recall = -step * scales[:, own] * total
            error = writing[:, own] * (keeping[:, own] * recall - targets[:, own])
            recalls.append(recall)
            errors.append(error)
            known.append((scales[:, own] * error).astype(NARROW))
        return (jnp.stack(recalls, 1), jnp.stack(errors, 1), jnp.stack(known[-blocks_each:], 1))

    for turn in range(parts):
        recall_seq, errors, scaled_errors = advance(halo)
        if turn < parts - 1:
            halo = jnp.concatenate(
                [passed_along(scaled_errors, "ctx", hop) for hop in range(reach, 0, -1)], axis=1
            )

    heads_view = (reading[..., None] * recall_seq).reshape(rows, local_heads, HD)
    head_factor = lax.rsqrt(jnp.mean(heads_view * heads_view, axis=-1, keepdims=True) + EPSILON)
    head_unit = heads_view * head_factor
    retrieved = (head_unit * gain_mem).reshape(rows, local_width).astype(NARROW)
    retrieved_full = lax.all_gather(retrieved, "tp", axis=1, tiled=True)
    query_w = qkv_cols[0]
    key_w = qkv_cols[1]
    value_w = qkv_cols[2]

    def heads(values):
        return values.astype(NARROW).reshape(blocks, SPAN, local_heads, HD)

    def fixed(values):
        shaped = values.astype(NARROW).reshape(1, persist_count, local_heads, HD)
        return jnp.broadcast_to(shaped, (blocks, persist_count, local_heads, HD))

    queries = heads(matmul(input_low, query_w))
    keys = jnp.concatenate(
        [
            fixed(matmul(persist, key_w)),
            heads(matmul(retrieved_full, key_w)),
            heads(matmul(input_low, key_w)),
        ],
        axis=1,
    )
    values_all = jnp.concatenate(
        [
            fixed(matmul(persist, value_w)),
            heads(matmul(retrieved_full, value_w)),
            heads(matmul(input_low, value_w)),
        ],
        axis=1,
    )
    label_rows = labels.reshape(blocks, SPAN)
    read_rows = reading.reshape(blocks, SPAN)
    position = jnp.arange(SPAN)
    causal = position[:, None] >= position[None, :]
    visible_own = causal[None] & (label_rows[:, :, None] == label_rows[:, None, :])
    visible_memory = visible_own & (read_rows[:, None, :] > 0.5)
    visible = jnp.concatenate(
        [jnp.ones((blocks, SPAN, persist_count), jnp.bool_), visible_memory, visible_own], axis=2
    )

    def scores_of():
        raw = batched("bthd,bkhd->bhtk", queries, keys) * scale
        return jnp.where(visible[:, None], raw, MASKED)

    scores = scores_of()
    highest = jnp.max(scores, axis=-1, keepdims=True)
    raised = jnp.exp(scores - highest)
    totals = jnp.sum(raised, axis=-1, keepdims=True)
    logsum = highest + jnp.log(totals)
    probs_low = (raised / totals).astype(NARROW)
    attended = (
        batched("bhtk,bkhd->bthd", probs_low, values_all).astype(NARROW).reshape(rows, local_width)
    )
    residual = own_rows(flat_tokens).astype(WIDE)
    hidden = residual + scattered(matmul(attended, out_rows))
    normed_mid, unit_mid, factor_mid = norm_rows(hidden, gain_ffn_wide)
    mid_low = collected(normed_mid)
    gate = matmul(mid_low, gate_up_cols[0])
    upper = matmul(mid_low, gate_up_cols[1])
    activ = (jax.nn.silu(gate) * upper).astype(NARROW)
    branch = scattered(matmul(activ, down_rows))
    output = collected(hidden + branch).reshape(groups, local_len, width)
    upstream_low = out_grad.reshape(rows, width)
    upstream = own_rows(upstream_low).astype(WIDE)
    grad_down = over_rows(activ, upstream_low)
    grad_act = by_rows(upstream_low, down_rows)
    grad_gate = (grad_act * upper * silu_slope(gate)).astype(NARROW)
    grad_upper = (grad_act * jax.nn.silu(gate)).astype(NARROW)
    grad_gate_up = jnp.stack([over_rows(mid_low, grad_gate), over_rows(mid_low, grad_upper)])
    grad_mid = scattered(by_rows(grad_gate, gate_up_cols[0]) + by_rows(grad_upper, gate_up_cols[1]))
    grad_gain_ffn = jnp.sum(grad_mid * unit_mid, axis=0)
    grad_hidden = upstream + norm_back(grad_mid, unit_mid, factor_mid, gain_ffn_wide)
    grad_mixed = collected(grad_hidden)
    grad_out_rows = over_rows(attended, grad_mixed)
    grad_attended = (
        by_rows(grad_mixed, out_rows).astype(NARROW).reshape(blocks, SPAN, local_heads, HD)
    )
    probs = jnp.exp(scores_of() - logsum)
    grad_probs = batched("bthd,bkhd->bhtk", grad_attended, values_all)
    grad_values = batched("bhtk,bthd->bkhd", probs.astype(NARROW), grad_attended)
    grad_scores = (
        probs * (grad_probs - jnp.sum(grad_probs * probs, axis=-1, keepdims=True))
    ).astype(NARROW)
    grad_queries = (
        (batched("bhtk,bkhd->bthd", grad_scores, keys) * scale)
        .astype(NARROW)
        .reshape(rows, local_width)
    )
    grad_keys = batched("bhtk,bthd->bkhd", grad_scores, queries) * scale

    def split_keys(grads):
        fixed_part = jnp.sum(grads[:, :persist_count], axis=0).reshape(persist_count, local_width)
        memory_part = (
            grads[:, persist_count : persist_count + SPAN].astype(NARROW).reshape(rows, local_width)
        )
        token_part = grads[:, persist_count + SPAN :].astype(NARROW).reshape(rows, local_width)
        return (fixed_part, memory_part, token_part)

    key_fixed, key_memory, key_token = split_keys(grad_keys)
    value_fixed, value_memory, value_token = split_keys(grad_values)
    persist_wide = persist.astype(WIDE)
    grad_query_w = over_rows(input_low, grad_queries)
    grad_key_w = (
        over_rows(input_low, key_token)
        + over_rows(retrieved_full, key_memory)
        + exact_product(persist_wide.T, key_fixed)
    )
    grad_value_proj = (
        over_rows(input_low, value_token)
        + over_rows(retrieved_full, value_memory)
        + exact_product(persist_wide.T, value_fixed)
    )
    grad_qkv = jnp.stack([grad_query_w, grad_key_w, grad_value_proj])
    grad_persist = exact_product(key_fixed, key_w.astype(WIDE).T) + exact_product(
        value_fixed, value_w.astype(WIDE).T
    )
    grad_input = (
        by_rows(grad_queries, query_w) + by_rows(key_token, key_w) + by_rows(value_token, value_w)
    )
    grad_retrieved = lax.psum_scatter(
        (by_rows(key_memory, key_w) + by_rows(value_memory, value_w)).astype(NARROW),
        "tp",
        scatter_dimension=1,
        tiled=True,
    ).astype(WIDE)
    grad_heads = grad_retrieved.reshape(rows, local_heads, HD)
    grad_gain_memory = jnp.sum(grad_heads * head_unit, axis=0)
    inner = grad_heads * gain_mem
    grad_masked = head_factor * (
        inner - head_unit * jnp.mean(inner * head_unit, axis=-1, keepdims=True)
    )
    grad_read = reading[..., None] * grad_masked.reshape(groups, blocks_each, SPAN, local_width)

    def retreat(later):
        known = [later[:, index] for index in range(blocks_each)]
        known = known[:0] + [0.0] * (reach * blocks_each) + known
        grad_errors = [None] * blocks_each
        grad_recalls = [None] * blocks_each
        raws = [None] * blocks_each
        for own in range(blocks_each - 1, -1, -1):
            grad_scaled = -step * known[reach * blocks_each + own]
            grad_error = scales[:, own] * grad_scaled
            grad_recall = grad_read[:, own] + writing[:, own] * keeping[:, own] * grad_error
            raw = (scales[:, own] * grad_recall).astype(NARROW)
            grad_errors[own] = grad_error
            grad_recalls[own] = grad_recall
            raws[own] = raw
            for lag in range(LAGS):
                place = reach * blocks_each + own - 1 - lag
                known[place] = known[place] + batched("stu,std->sud", mixing[:, own, lag], raw)
        sent = jnp.stack(known[: reach * blocks_each], 1).astype(NARROW)
        return (jnp.stack(grad_errors, 1), jnp.stack(grad_recalls, 1), jnp.stack(raws, 1), sent)

    later = jnp.zeros((groups, blocks_each, SPAN, local_width), WIDE)
    for turn in range(parts):
        grad_errors, grad_recalls, raws, sent = retreat(later)
        if turn < parts - 1:
            later = 0.0
            for hop in range(1, reach + 1):
                start = (reach - hop) * blocks_each
                later = later + passed_along(
                    sent[:, start : start + blocks_each], "ctx", -hop
                ).astype(WIDE)

    grad_targets = (-writing * grad_errors).astype(NARROW).reshape(rows, local_width)
    scale_part = jnp.sum(grad_recalls * recall_seq + errors * grad_errors, axis=3).reshape(rows)
    scale_sum = lax.psum(scale_part, "tp")
    known = [halo[:, index] for index in range(reach * blocks_each)]
    known = known + [scaled_errors[:, own] for own in range(blocks_each)]
    grad_mixing = []
    for own in range(blocks_each):
        row = []
        for lag in range(LAGS):
            link = linked[:, own, lag][:, None, None]
            product = batched(
                "std,sud->stu", raws[:, own], known[reach * blocks_each + own - 1 - lag]
            )
            row.append(jnp.where(link, -step * product, 0.0))
        grad_mixing.append(jnp.stack(row, axis=1))
    grad_mixing = lax.psum(jnp.stack(grad_mixing, axis=1).astype(NARROW), "tp")
    needed = {}
    for hop in range(1, reach + 1):
        pairs = [
            (own, lag)
            for own in range(blocks_each)
            for lag in range(LAGS)
            if -(-(1 + lag - own) // blocks_each) == hop
        ]
        moved = passed_along(
            jnp.stack([grad_mixing[:, own, lag] for own, lag in pairs], axis=1), "ctx", -hop
        )
        for place, (own, lag) in enumerate(pairs):
            needed[(hop * blocks_each + own, lag)] = moved[:, place]
    for own in range(blocks_each):
        for lag in range(LAGS):
            needed[(own, lag)] = grad_mixing[:, own, lag]
    grad_features = []
    grad_decays = [0.0] * LAGS
    for own in range(blocks_each):
        total = 0.0
        mine = own_features[:, own].astype(WIDE)
        for lag in range(LAGS):
            from_reads = batched("stu,suh->sth", needed[(own, lag)], block_of(first + own - 1 - lag))
            grad_decays[lag] = grad_decays[lag] + jnp.sum(mine * from_reads, axis=(0, 1))
            later = own + 1 + lag
            from_writes = batched("stu,sth->suh", needed[(later, lag)], block_of(first + later))
            total = total + decays[lag] * (from_reads + from_writes)
        grad_features.append(total)
    grad_features = jnp.stack(grad_features, 1).reshape(rows, local_units)
    grad_features = grad_features - (key_scale * key_scale * scale_sum)[:, None] * features.astype(
        WIDE
    )
    grad_retain = 0.0
    grad_moment = 0.0
    retain_slope = jnp.zeros_like(retain)
    for lag in range(1, LAGS):
        retain_slope = retain * retain_slope + decays[lag - 1]
        moment_slope = 0.0
        for power in range(1, lag + 1):
            moment_slope = moment_slope + power * retain ** (lag - power) * moment ** (power - 1)
        grad_retain = grad_retain + retain_slope * grad_decays[lag]
        grad_moment = grad_moment + moment_slope * grad_decays[lag]
    grad_rates = jnp.stack([grad_retain, grad_moment])

    grad_pre = (grad_features * silu_slope(preact)).astype(NARROW)
    grad_feature_w = over_rows(input_low, grad_pre)
    grad_target_w = over_rows(input_low, grad_targets)
    grad_input = grad_input + by_rows(grad_pre, feature_cols) + by_rows(grad_targets, value_cols)
    grad_input = scattered(grad_input)
    _, unit_in, factor_in = norm_rows(residual, gain_in_wide)
    grad_gain_in = jnp.sum(grad_input * unit_in, axis=0)
    grad_tokens = collected(
        grad_hidden + norm_back(grad_input, unit_in, factor_in, gain_in_wide)
    ).astype(WIDE)

    def shared(array, axis):
        halves = lax.psum_scatter(
            array.astype(NARROW), "shard", scatter_dimension=axis, tiled=True
        )
        return lax.psum(halves, "ctx").astype(WIDE)

    def small(array, axis, axes):
        summed = lax.psum(array, axes)
        size = summed.shape[axis] // lax.axis_size("shard")
        return lax.dynamic_slice_in_dim(summed, lax.axis_index("shard") * size, size, axis)

    return (
        output,
        grad_tokens.reshape(groups, local_len, width),
        small(grad_gain_in, 0, ("shard", "ctx", "tp")),
        small(grad_gain_ffn, 0, ("shard", "ctx", "tp")),
        small(grad_gain_memory, 1, ("shard", "ctx")),
        small(grad_rates, 0, ("shard", "ctx")),
        small(grad_persist, 1, ("shard", "ctx", "tp")),
        shared(grad_qkv, 1),
        shared(grad_out_rows, 1),
        shared(grad_target_w, 0),
        shared(grad_feature_w, 0),
        shared(grad_gate_up, 1),
        shared(grad_down, 1),
    )


def solution(mesh):
    placed = (
        P("shard", "ctx", None),
        P("shard", "ctx"),
        P("shard"),
        P("shard"),
        P("tp", "shard"),
        P("shard", None),
        P(None, "shard"),
        P(None, "shard", "tp"),
        P("tp", "shard"),
        P("shard", "tp"),
        P("shard", "tp"),
        P(None, "shard", "tp"),
        P("tp", "shard"),
        P("shard", "ctx", None),
    )
    return jax.shard_map(
        on_device,
        mesh=mesh,
        in_specs=placed,
        out_specs=(
            P("shard", "ctx", None),
            P("shard", "ctx", None),
            P("shard"),
            P("shard"),
            P("tp", "shard"),
            P("shard", "tp"),
            P(None, "shard"),
            P(None, "shard", "tp"),
            P("tp", "shard"),
            P("shard", "tp"),
            P("shard", "tp"),
            P(None, "shard", "tp"),
            P("tp", "shard"),
        ),
        check_vma=False,
    )
```

time: 6670 us -> 2220 us (0.33)
  waiting for transfers between devices: 4800 us -> 1490 us
  matrix products: 874 us -> 312 us
  local copies, waits for them, and re-layouts: 521 us -> 107 us
  other arithmetic: 332 us -> 123 us
  blocking collectives: 39.5 us -> 112 us
    ppermute x13 -> x14, waiting for transfers between devices: 2340 us -> 112 us  [passed_along(): lax.ppermute(value, axis, [(source, source + steps) for source in range(i...]
    psum x5 -> x4, waiting for transfers between devices: 1090 us -> 436 us  [the longest x1 175 us: shared(): return lax.psum(halves, 'ctx').astype(WIDE)]
    dot_general x44 -> x95, matrix products: 678 us -> 99.1 us  [batched(): return jnp.einsum(spec, left, right, preferred_element_type=WIDE)]
    reduce_scatter x9 -> x10, waiting for transfers between devices: 900 us -> 436 us  [the longest x6 283 us: shared(): lax.psum_scatter(array.astype(NARROW), 'shard', scatter_dimension=axis, t...]
    while x88 -> x0, local copies, waits for them, and re-layouts: 251 us -> none
    mul x34 -> x3, other arithmetic: 156 us -> 0.68 us  [the longest x1 0.67 us: retreat(): writing[:, own] * keeping[:, own] * grad_error]
    dynamic_update_slice x8 -> x0, local copies, waits for them, and re-layouts: 86.6 us -> none  [the longest x6 86.6 us: chain_forward(): return lax.scan(advance, (memory, velocity), jnp.arange(blocks_each))]
    psum x1 -> x4, blocking collectives: 13.7 us -> 85.3 us  [the longest x2 66 us: small(): summed = lax.psum(array, axes)]
  transfers between devices with their start and end apart: 37 -> 41, of which waited for: 33 -> 36; matrix products, arithmetic and copies ran while one was open for 13% -> 15% of each run, Pallas kernels for 0% -> 0%
where the time goes in v1:
time: 2220 us; the launch traced here: 2200 us
  waiting for transfers between devices  1490 us (67%)
  matrix products  312 us (14%)
  other arithmetic  123 us (6%)
  blocking collectives  112 us (5%)
  local copies, waits for them, and re-layouts  107 us (5%)
  starting transfers between devices  45.6 us (2%)
    reduce_scatter x6, waiting for transfers between devices, shared(): lax.psum_scatter(array.astype(NARROW), 'shard', scatter_dimension=axis, t...  283 us
    all_gather x4, waiting for transfers between devices, collected(): return lax.all_gather(array.astype(NARROW), 'tp', axis=0, tiled=True)  187 us
    psum x1, waiting for transfers between devices, shared(): return lax.psum(halves, 'ctx').astype(WIDE)  175 us
    all_gather x6, waiting for transfers between devices, whole(): return lax.all_gather(array, 'shard', axis=axis, tiled=True)  158 us
    reduce_scatter x4, waiting for transfers between devices, scattered(): lax.psum_scatter(array.astype(NARROW), 'tp', scatter_dimension=0, tiled=T...  152 us
    psum x1, waiting for transfers between devices, small(): summed = lax.psum(array, axes)  133 us
    ppermute x14, waiting for transfers between devices, passed_along(): lax.ppermute(value, axis, [(source, source + steps) for source in range(i...  112 us
    dot_general x95, matrix products, batched(): return jnp.einsum(spec, left, right, preferred_element_type=WIDE)  99.1 us
  transfers between devices with their start and end apart: 41, of which 36 were waited for; matrix products, arithmetic and copies ran while one was open for 15% of the time, Pallas kernels for 0%

profile of v1, /device:TPU:1, one launch (start us, length us, event | category | flops | bytes accessed | tf_op | source)
XLA Modules:
  0.0 2203.5 jit_solution(12139713608318112963)
XLA Ops:
  26.9 47.5 %all-gather.19.cloned.1.call-done = bf16[1536,1536]{1,0:T(8,128)(2,1)} async-done(((bf16[768,1536]{1,0:T(8,128)(2,1)}), bf16[1536,1536]{1,0:T(8,128)(2,1)}) %all-gather.19.cloned.1.call-update) | async-done | bytes 4718608 | tf_op jit(solution)/shard_map/all_gather | solution.py:77
  91.8 67.1 %all-gather.21.cloned.1.call-done = bf16[2,2048,1536]{2,1,0:T(8,128)(2,1)} async-done(((bf16[2,512,1536]{2,1,0:T(8,128)(2,1)}), bf16[2,2048,1536]{2,1,0:T(8,128)(2,1)}) %all-gather.21.cloned.1.call-update) | async-done | bytes 12582928 | tf_op jit(solution)/shard_map/all_gather | solution.py:119
  177.8 26.1 %multiply_convert_fusion = bf16[4096,1536]{1,0:T(8,128)(2,1)S(1)} fusion(bf16[4096,1536]{1,0:T(8,128)(2,1)} %fusion.1, bf16[1536,1536]{1,0:T(8,128)(2,1)} %all-gather.19.cloned.1.call-done), kind=kOutput, calls=%fused_computation.3 | convolution fusion | flops 19358810112 | bytes 29884416 | tf_op jit(solution)/shard_map/dot_general | solution.py:41
  231.8 70.0 %all-reduce.8.cloned.1.call-done = bf16[2,2,4,256,256]{4,3,0,2,1:T(8,128)(2,1)} async-done(((bf16[2,2,4,256,256]{4,3,0,2,1:T(8,128)(2,1)}), bf16[2,2,4,256,256]{4,3,0,2,1:T(8,128)(2,1)}) %all-reduce.8.cloned.1.call-update) | async-done | bytes 2097168 | tf_op jit(solution)/shard_map/psum | solution.py:173
  458.9 30.0 %all-gather.25.cloned.1.call-done = bf16[1024,1536]{1,0:T(8,128)(2,1)} async-done(((bf16[1024,384]{1,0:T(8,128)(2,1)}), bf16[1024,1536]{1,0:T(8,128)(2,1)}) %all-gather.25.cloned.1.call-update) | async-done | bytes 3145744 | tf_op jit(solution)/shard_map/all_gather | solution.py:213
  533.3 53.7 %reduce-scatter.14.cloned.1.call-done = bf16[256,1536]{1,0:T(8,128)(2,1)} async-done(((bf16[1024,1536]{1,0:T(8,128)(2,1)}), bf16[256,1536]{1,0:T(8,128)(2,1)}) %reduce-scatter.14.cloned.1.call-update) | async-done | bytes 786448 | tf_op jit(solution)/shard_map/reduce_scatter | solution.py:111
  591.6 77.5 %all-gather.31.cloned.1.call-done = bf16[2,1536,1024]{2,1,0:T(8,128)(2,1)} async-done(((bf16[2,768,1024]{2,1,0:T(8,128)(2,1)}), bf16[2,1536,1024]{2,1,0:T(8,128)(2,1)}) %all-gather.31.cloned.1.call-update) | async-done | bytes 6291472 | tf_op jit(solution)/shard_map/all_gather | solution.py:77
  669.0 65.5 %all-gather.29.cloned.1.call-done = bf16[1024,1536]{1,0:T(8,128)(2,1)} async-done(((bf16[256,1536]{1,0:T(8,128)(2,1)}), bf16[1024,1536]{1,0:T(8,128)(2,1)}) %all-gather.29.cloned.1.call-update) | async-done | bytes 3145744 | tf_op jit(solution)/shard_map/all_gather | solution.py:116
  748.0 31.6 %all-gather.33.cloned.1.call-done = bf16[1024,1536]{1,0:T(8,128)(2,1)} async-done(((bf16[1024,768]{1,0:T(8,128)(2,1)}), bf16[1024,1536]{1,0:T(8,128)(2,1)}) %all-gather.33.cloned.1.call-update) | async-done | bytes 3145744 | tf_op jit(solution)/shard_map/all_gather | solution.py:77
  804.9 60.3 %reduce-scatter.18.cloned.1.call-done = bf16[256,1536]{1,0:T(8,128)(2,1)} async-done(((bf16[1024,1536]{1,0:T(8,128)(2,1)}), bf16[256,1536]{1,0:T(8,128)(2,1)}) %reduce-scatter.18.cloned.1.call-update) | async-done | bytes 786448 | tf_op jit(solution)/shard_map/reduce_scatter | solution.py:111
  872.6 62.9 %all-gather.37.cloned.1.call-done = bf16[1024,1536]{1,0:T(8,128)(2,1)} async-done(((bf16[256,1536]{1,0:T(8,128)(2,1)}), bf16[1024,1536]{1,0:T(8,128)(2,1)}) %all-gather.37.cloned.1.call-update) | async-done | bytes 3145744 | tf_op jit(solution)/shard_map/all_gather | solution.py:116
  987.6 54.0 %reduce-scatter.34.cloned.1.call-done = bf16[384,1024]{1,0:T(8,128)(2,1)} async-done(((bf16[1536,1024]{1,0:T(8,128)(2,1)}), bf16[384,1024]{1,0:T(8,128)(2,1)}) %reduce-scatter.34.cloned.1.call-update) | async-done | bytes 786448
  1193.3 57.9 %all-reduce.10.cloned.1.call-done = bf16[2,2,4,256,256]{4,3,0,2,1:T(8,128)(2,1)} async-done(((bf16[2,2,4,256,256]{4,3,0,2,1:T(8,128)(2,1)}), bf16[2,2,4,256,256]{4,3,0,2,1:T(8,128)(2,1)}) %all-reduce.10.cloned.1.call-update) | async-done | bytes 2097168 | tf_op jit(solution)/shard_map/psum | solution.py:391
  1407.8 38.4 %reduce-scatter.16.cloned.1.call-done = bf16[256,1536]{1,0:T(8,128)(2,1)} async-done(((bf16[1024,1536]{1,0:T(8,128)(2,1)}), bf16[256,1536]{1,0:T(8,128)(2,1)}) %reduce-scatter.16.cloned.1.call-update) | async-done | bytes 786448 | tf_op jit(solution)/shard_map/reduce_scatter | solution.py:111
  1451.3 40.6 %reduce-scatter.32.cloned.1.call-done = bf16[1024,768]{1,0:T(8,128)(2,1)} async-done(((bf16[1024,1536]{1,0:T(8,128)(2,1)}), bf16[1024,768]{1,0:T(8,128)(2,1)}) %reduce-scatter.32.cloned.1.call-update) | async-done | bytes 1572880 | tf_op jit(solution)/shard_map/reduce_scatter | solution.py:448
  1491.8 80.0 %reduce-scatter.30.cloned.1.call-done = bf16[2,768,1024]{2,1,0:T(8,128)(2,1)} async-done(((bf16[2,1536,1024]{2,1,0:T(8,128)(2,1)}), bf16[2,768,1024]{2,1,0:T(8,128)(2,1)}) %reduce-scatter.30.cloned.1.call-update) | async-done | bytes 3145744 | tf_op jit(solution)/shard_map/reduce_scatter | solution.py:448
  1571.9 24.5 %reduce-scatter.24.cloned.1.call-done = bf16[384,768]{1,0:T(8,128)(2,1)} async-done(((bf16[384,1536]{1,0:T(8,128)(2,1)}), bf16[384,768]{1,0:T(8,128)(2,1)}) %reduce-scatter.24.cloned.1.call-update) | async-done | bytes 589840 | tf_op jit(solution)/shard_map/reduce_scatter | solution.py:448
  1596.4 50.6 %reduce-scatter.22.cloned.1.call-done = bf16[3,768,384]{2,1,0:T(8,128)(2,1)} async-done(((bf16[3,1536,384]{2,1,0:T(8,128)(2,1)}), bf16[3,768,384]{2,1,0:T(8,128)(2,1)}) %reduce-scatter.22.cloned.1.call-update) | async-done | bytes 1769488 | tf_op jit(solution)/shard_map/reduce_scatter | solution.py:448
  1647.0 24.7 %reduce-scatter.26.cloned.1.call-done = bf16[768,384]{1,0:T(8,128)(2,1)} async-done(((bf16[1536,384]{1,0:T(8,128)(2,1)}), bf16[768,384]{1,0:T(8,128)(2,1)}) %reduce-scatter.26.cloned.1.call-update) | async-done | bytes 589840 | tf_op jit(solution)/shard_map/reduce_scatter | solution.py:448
  1671.7 63.0 %reduce-scatter.28.cloned.1.call-done = bf16[768,1536]{1,0:T(8,128)(2,1)} async-done(((bf16[1536,1536]{1,0:T(8,128)(2,1)}), bf16[768,1536]{1,0:T(8,128)(2,1)}) %reduce-scatter.28.cloned.1.call-update) | async-done | bytes 2359312 | tf_op jit(solution)/shard_map/reduce_scatter | solution.py:448
  1734.8 133.1 %all-reduce.12.cloned.1.call-done = f32[64,1536]{1,0:T(8,128)} async-done(((f32[64,1536]{1,0:T(8,128)}), f32[64,1536]{1,0:T(8,128)}) %all-reduce.12.cloned.1.call-update) | async-done | bytes 393232 | tf_op jit(solution)/shard_map/psum | solution.py:454
  1893.5 45.0 %all-reduce = (f32[1536]{0:T(1024)S(1)}, f32[1536]{0:T(1024)S(1)}) all-reduce(f32[1536]{0:T(1024)S(1)} %get-tuple-element.15, f32[1536]{0:T(1024)S(1)} %copy-done.123), channel_id=1, replica_groups=mesh['shard'=2,'ctx'=4,'tp'=4] {'shard','ctx','tp'}, use_global_device_ids=true, to_apply=%region_23.24 | all-reduce | flops 3072 | bytes 24576 | tf_op jit(solution)/shard_map/psum | solution.py:454
  1939.9 58.4 %all-gather.39.cloned.1.call-done = bf16[1024,1536]{1,0:T(8,128)(2,1)} async-done(((bf16[256,1536]{1,0:T(8,128)(2,1)}), bf16[1024,1536]{1,0:T(8,128)(2,1)}) %all-gather.39.cloned.1.call-update) | async-done | bytes 3145744 | tf_op jit(solution)/shard_map/all_gather | solution.py:116
  2003.8 175.4 %all-reduce.14.cloned.1.call-done = (bf16[3,768,384]{2,1,0:T(8,128)(2,1)}, bf16[384,768]{1,0:T(8,128)(2,1)}, bf16[768,384]{1,0:T(8,128)(2,1)}, bf16[768,1536]{1,...) async-done(((bf16[3,768,384]{2,1,0:T(8,128)(2,1)}, bf16[384,768]{1,0:T(8,128)(2,1)}, bf16[768,384]{1,0:T(8,128)(2,1)}, ...) | async-done | bytes 10027024 | tf_op jit(solution)/shard_map/psum | solution.py:451
  (778 shorter events, 747.9 us)
Async XLA Ops:
  8.0 150.9 %all-gather.21.cloned.1.call-start = ((), (), s32[]{:S(2)}) async-start(), calls=%async_computation.13 | async-start | bytes 15728640 | tf_op jit(solution)/shard_map/all_gather | solution.py:119
  8.7 207.8 %all-gather.23.cloned.1.call-start = ((), (), s32[]{:S(2)}) async-start(), calls=%async_computation.15 | async-start | bytes 1769472 | tf_op jit(solution)/shard_map/all_gather | solution.py:77
  9.4 292.4 %all-reduce.8.cloned.1.call-start = ((), (), s32[]{:S(2)}) async-start(), calls=%async_computation.14 | async-start | bytes 4194304 | tf_op jit(solution)/shard_map/psum | solution.py:173
  216.1 207.5 %all-gather.17.cloned.1.call-start = ((), (), s32[]{:S(2)}) async-start(), calls=%async_computation.11 | async-start | bytes 5308416 | tf_op jit(solution)/shard_map/all_gather | solution.py:77
  409.6 177.4 %reduce-scatter.14.cloned.1.call-start = ((), (), s32[]{:S(2)}) async-start(), calls=%async_computation.18 | async-start | bytes 3932160 | tf_op jit(solution)/shard_map/reduce_scatter | solution.py:111
  527.9 141.1 %all-gather.31.cloned.1.call-start = ((), (), s32[]{:S(2)}) async-start(), calls=%async_computation.20 | async-start | bytes 9437184 | tf_op jit(solution)/shard_map/all_gather | solution.py:77
  528.7 205.9 %all-gather.29.cloned.1.call-start = ((), (), s32[]{:S(2)}) async-start(), calls=%async_computation.19 | async-start | bytes 3932160 | tf_op jit(solution)/shard_map/all_gather | solution.py:116
  590.8 188.8 %all-gather.33.cloned.1.call-start = ((), (), s32[]{:S(2)}) async-start(), calls=%async_computation.21 | async-start | bytes 4718592 | tf_op jit(solution)/shard_map/all_gather | solution.py:77
  591.5 273.7 %reduce-scatter.18.cloned.1.call-start = ((), (), s32[]{:S(2)}) async-start(), calls=%async_computation.24 | async-start | bytes 3932160 | tf_op jit(solution)/shard_map/reduce_scatter | solution.py:111
  804.9 130.6 %all-gather.37.cloned.1.call-start = ((), (), s32[]{:S(2)}) async-start(), calls=%async_computation.25 | async-start | bytes 3932160 | tf_op jit(solution)/shard_map/all_gather | solution.py:116
  871.8 169.8 %reduce-scatter.34.cloned.1.call-start = ((), (), s32[]{:S(2)}) async-start(), calls=%async_computation.36 | async-start | bytes 3932160
  982.6 268.6 %all-reduce.10.cloned.1.call-start = ((), (), s32[]{:S(2)}) async-start(), calls=%async_computation.26 | async-start | bytes 4194304 | tf_op jit(solution)/shard_map/psum | solution.py:391
  1162.8 243.1 %reduce-scatter.20.cloned.1.call-start = ((), (), s32[]{:S(2)}) async-start(), calls=%async_computation.27 | async-start | bytes 3932160 | tf_op jit(solution)/shard_map/reduce_scatter | solution.py:111
  1325.0 121.2 %reduce-scatter.16.cloned.1.call-start = ((), (), s32[]{:S(2)}) async-start(), calls=%async_computation.22 | async-start | bytes 3932160 | tf_op jit(solution)/shard_map/reduce_scatter | solution.py:111
  1333.4 158.5 %reduce-scatter.32.cloned.1.call-start = ((), (), s32[]{:S(2)}) async-start(), calls=%async_computation.35 | async-start | bytes 4718592 | tf_op jit(solution)/shard_map/reduce_scatter | solution.py:448
  1341.9 230.0 %reduce-scatter.30.cloned.1.call-start = ((), (), s32[]{:S(2)}) async-start(), calls=%async_computation.34 | async-start | bytes 9437184 | tf_op jit(solution)/shard_map/reduce_scatter | solution.py:448
  1356.3 240.1 %reduce-scatter.24.cloned.1.call-start = ((), (), s32[]{:S(2)}) async-start(), calls=%async_computation.31 | async-start | bytes 1769472 | tf_op jit(solution)/shard_map/reduce_scatter | solution.py:448
  1365.2 281.9 %reduce-scatter.22.cloned.1.call-start = ((), (), s32[]{:S(2)}) async-start(), calls=%async_computation.30 | async-start | bytes 5308416 | tf_op jit(solution)/shard_map/reduce_scatter | solution.py:448
  1383.3 288.5 %reduce-scatter.26.cloned.1.call-start = ((), (), s32[]{:S(2)}) async-start(), calls=%async_computation.32 | async-start | bytes 1769472 | tf_op jit(solution)/shard_map/reduce_scatter | solution.py:448
  1389.4 345.3 %reduce-scatter.28.cloned.1.call-start = ((), (), s32[]{:S(2)}) async-start(), calls=%async_computation.33 | async-start | bytes 7077888 | tf_op jit(solution)/shard_map/reduce_scatter | solution.py:448
  1398.7 469.3 %all-reduce.12.cloned.1.call-start = ((), (), s32[]{:S(2)}) async-start(), calls=%async_computation.29 | async-start | bytes 786432 | tf_op jit(solution)/shard_map/psum | solution.py:454
  1405.9 534.0 %all-gather.35.cloned.1.call-start = ((), (), s32[]{:S(2)}) async-start(), calls=%async_computation.23 | async-start | bytes 3932160 | tf_op jit(solution)/shard_map/all_gather | solution.py:116
  1450.6 547.6 %all-gather.39.cloned.1.call-start = ((), (), s32[]{:S(2)}) async-start(), calls=%async_computation.28 | async-start | bytes 3932160 | tf_op jit(solution)/shard_map/all_gather | solution.py:116
  1451.2 728.0 %all-reduce.14.cloned.1.call-start = ((), (), s32[]{:S(2)}) async-start(), calls=%async_computation.37 | async-start | bytes 20054016 | tf_op jit(solution)/shard_map/psum | solution.py:451
  (189 other events, 6542.1 us)
Sparse Core Ops, SparseCore 0:
  9.5 64.8 all-gather.18
  75.9 82.8 all-gather.20
  160.4 22.1 all-gather.22
  216.2 85.5 all-reduce.7
  371.0 52.6 all-gather.16
  425.6 63.2 all-gather.24
  528.0 58.8 reduce-scatter.13
  588.5 80.4 all-gather.30
  671.0 63.4 all-gather.28
  736.1 43.5 all-gather.32
  805.0 60.1 reduce-scatter.17
  871.9 63.5 all-gather.36
  982.8 58.7 reduce-scatter.33
  1163.0 88.2 all-reduce.9
  1325.1 57.9 reduce-scatter.19
  1385.8 60.3 reduce-scatter.15
  1448.3 43.5 reduce-scatter.31
  1494.7 77.1 reduce-scatter.29
  1599.3 47.7 reduce-scatter.21
  1674.6 60.0 reduce-scatter.27
  1739.9 128.0 all-reduce.11
  1870.1 64.1 all-gather.34
  1936.2 61.9 all-gather.38
  2001.2 177.8 all-reduce.13
  (3 shorter events, 64.8 us)

commit v2 on v1

v2 whole, which is shorter than its diff:
```python
import jax
import jax.numpy as jnp
from jax import lax
from jax.sharding import PartitionSpec as P

HD = 96
SPAN = 256
LIMIT = 800
LAGS = (LIMIT + SPAN - 2) // SPAN
STREAMS = 1


EPSILON = 1e-06
MASKED = -1e30
WIDE = jnp.float32
NARROW = jnp.bfloat16


def passed_along(value, axis, pairs):
    return lax.ppermute(value, axis, pairs)


def flipped(value, axis, bit):
    return lax.ppermute(value, axis, [(i, i ^ bit) for i in range(lax.axis_size(axis))])


def either(first, one, other):
    return jnp.where(first, one, other), jnp.where(first, other, one)


def pick(array, place, axis):
    return lax.dynamic_index_in_dim(array, place, axis, keepdims=False)


def after(value, *others):
    return lax.optimization_barrier((value, *others))[0]


def norm_rows(values, gain):
    factor = lax.rsqrt(jnp.mean(values * values, axis=-1, keepdims=True) + EPSILON)
    normed = values * factor
    return (normed * gain, normed, factor)


def norm_back(upstream, normed, factor, gain):
    inner = upstream * gain
    return factor * (inner - normed * jnp.mean(inner * normed, axis=-1, keepdims=True))


def silu_slope(values):
    sigmoid = jax.nn.sigmoid(values)
    return sigmoid * (1.0 + values * (1.0 - sigmoid))


def matmul(left, right):
    return jnp.dot(left, right, preferred_element_type=WIDE)


def over_rows(left, right):
    return lax.dot_general(left, right, (((0,), (0,)), ((), ())), preferred_element_type=WIDE)


def by_rows(left, right):
    return lax.dot_general(left, right, (((1,), (1,)), ((), ())), preferred_element_type=WIDE)


def exact_product(left, right):
    return jnp.dot(left, right, precision=lax.Precision.HIGHEST, preferred_element_type=WIDE)


def batched(spec, left, right):
    return jnp.einsum(spec, left, right, preferred_element_type=WIDE)


def on_device(
    tokens,
    segments,
    norm_gain,
    ffn_gain,
    memory_gain,
    memory_rates,
    persistent,
    w_qkv,
    w_out,
    w_value,
    w_feature,
    w_gate_up,
    w_down,
    out_grad,
):
    parts, ranks = (lax.axis_size("ctx"), lax.axis_size("tp"))
    part, rank = (lax.axis_index("ctx"), lax.axis_index("tp"))
    half_index = lax.axis_index("shard")
    first_half = half_index == 0
    odd_part = part % 2 == 1
    groups, local_len, width = tokens.shape
    blocks_each = local_len // SPAN
    reach = -(-LAGS // blocks_each)
    step = 6.0 / (SPAN + 8)
    scale = HD ** (-0.5)

    def joined(own, other, axis):
        return jnp.concatenate(either(first_half, own, other), axis=axis)

    pair_tokens = flipped(tokens, "ctx", 1)
    far_tokens = flipped(tokens, "ctx", 2)
    diagonal_tokens = flipped(far_tokens, "ctx", 1)
    feature_other = flipped(w_feature, "shard", 1)
    smalls = [norm_gain, ffn_gain, memory_gain, memory_rates, persistent]
    small_flat = jnp.concatenate([item.reshape(-1) for item in smalls])
    small_other = flipped(small_flat, "shard", 1)
    small_others = []
    start = 0
    for item in smalls:
        small_others.append(small_other[start : start + item.size].reshape(item.shape))
        start += item.size
    value_other, qkv_other = [
        flipped(after(item, feature_other), "shard", 1) for item in (w_value, w_qkv)
    ]
    out_other, gate_up_other = [
        flipped(after(item, value_other, qkv_other), "shard", 1) for item in (w_out, w_gate_up)
    ]
    down_other = flipped(after(w_down, out_other, gate_up_other), "shard", 1)

    gain_in_wide = joined(norm_gain, small_others[0], 0).astype(WIDE)
    gain_ffn_wide = joined(ffn_gain, small_others[1], 0).astype(WIDE)
    gain_mem = joined(memory_gain, small_others[2], 1).astype(WIDE)
    rates = joined(memory_rates, small_others[3], 0)
    persist = joined(persistent, small_others[4], 1)
    feature_cols = joined(w_feature, feature_other, 0)
    value_cols = joined(w_value, value_other, 0)
    qkv_cols = joined(w_qkv, qkv_other, 1)
    out_rows = joined(w_out, out_other, 1)
    gate_up_cols = joined(w_gate_up, gate_up_other, 1)
    down_rows = joined(w_down, down_other, 1)
    local_width = qkv_cols.shape[2]
    local_units = feature_cols.shape[1]
    local_heads = local_width // HD
    persist_count = persist.shape[0]
    query_w = qkv_cols[0]
    key_w = qkv_cols[1]
    value_w = qkv_cols[2]

    def scattered(array):
        return lax.psum_scatter(
            array.astype(NARROW), "tp", scatter_dimension=0, tiled=True
        ).astype(WIDE)

    def collected(array):
        return lax.all_gather(array.astype(NARROW), "tp", axis=0, tiled=True)

    own_units = lax.dynamic_slice_in_dim(rates.astype(WIDE), rank * local_units, local_units, 1)
    retain, moment = (own_units[0], own_units[1])
    decays = [jnp.ones_like(retain)]
    for lag in range(1, LAGS):
        decays.append(retain * decays[-1] + moment**lag)

    labels_all = segments.astype(WIDE).reshape(groups, blocks_each, SPAN) + 1.0
    lasts_all = labels_all[:, :, -1]
    block_lasts = lax.all_gather(lasts_all, "ctx", axis=1, tiled=True)
    total_blocks = parts * blocks_each
    first = part * blocks_each

    def last_of(index):
        found = lax.dynamic_index_in_dim(
            block_lasts, jnp.clip(index, 0, total_blocks - 1), 1, False
        )
        return jnp.where(index >= 0, found, 0.0)

    before_all = jnp.stack([last_of(first + own - 1) for own in range(blocks_each)], axis=1)
    linked_all = []
    for own in range(blocks_each):
        links = []
        for lag in range(LAGS - 1, -1, -1):
            source = first + own - 1 - lag
            link = (source >= 0) & (last_of(source) == last_of(first + own - 1))
            links.append(jnp.broadcast_to(link[:, None, None], (groups, 1, SPAN)))
        linked_all.append(jnp.concatenate(links, axis=2))
    linked_all = jnp.stack(linked_all, axis=1)

    def place_of(own, lag):
        return divmod(own - 1 - lag, blocks_each)

    fixed_keys = matmul(persist, key_w).astype(NARROW).reshape(1, persist_count, local_heads, HD)
    fixed_values = (
        matmul(persist, value_w).astype(NARROW).reshape(1, persist_count, local_heads, HD)
    )
    position = jnp.arange(SPAN)
    causal = position[:, None] >= position[None, :]

    count = groups // STREAMS
    rows = count * local_len
    blocks = count * blocks_each
    sub = rows // ranks

    def own_rows(array):
        return lax.dynamic_slice_in_dim(array, rank * sub, sub, 0)

    class Stream:
        pass

    def begin(one, index):
        def mine(array):
            return array[index * count : (index + 1) * count]

        one.flat = mine(tokens).reshape(rows, width)
        one.upstream_low = mine(out_grad).reshape(rows, width)
        one.labels = mine(labels_all)
        one.lasts = mine(lasts_all)
        one.before = mine(before_all)
        one.linked = mine(linked_all)
        one.keeping = (one.lasts == one.before).astype(WIDE)[:, :, None, None]
        one.writing = (one.labels == one.lasts[:, :, None]).astype(WIDE)[..., None]
        one.reading = (one.labels == one.before[:, :, None]).astype(WIDE)

        def features_of(piece):
            low = norm_rows(piece.astype(WIDE), gain_in_wide)[0].astype(NARROW)
            return low, matmul(low.reshape(rows, width), feature_cols)

        def shaped(values):
            return values.reshape(count, blocks_each, SPAN, local_units)

        low, one.preact = features_of(mine(tokens))
        one.input_low = low.reshape(rows, width)
        one.features = jax.nn.silu(one.preact).astype(NARROW)
        close = [mine(pair_tokens), mine(diagonal_tokens)]
        one.around = {0: shaped(one.features)}
        for delta, piece in (
            (-1, jnp.where(odd_part, close[0], close[1])),
            (1, jnp.where(odd_part, close[1], close[0])),
            (2, mine(far_tokens)),
        ):
            one.around[delta] = shaped(jax.nn.silu(features_of(piece)[1]).astype(NARROW))
        one.around[-2] = one.around[2]
        squares = jnp.sum(jnp.square(one.features.astype(WIDE)), axis=1)
        squares = jnp.sum(lax.all_gather(squares, "tp", axis=0), axis=0)
        one.key_scale = lax.rsqrt(squares + EPSILON)
        one.scales = one.key_scale.reshape(count, blocks_each, SPAN, 1)
        one.targets = matmul(one.input_low, value_cols).reshape(
            count, blocks_each, SPAN, local_width
        )
        weighted = [(one.around[0].astype(WIDE) * decay).astype(NARROW) for decay in decays]
        products = []
        for own in range(blocks_each):
            row = []
            for lag in range(LAGS - 1, -1, -1):
                delta, place = place_of(own, lag)
                row.append(
                    batched("sth,suh->stu", weighted[lag][:, own], one.around[delta][:, place])
                )
            products.append(jnp.concatenate(row, axis=2))
        products = jnp.stack(products, axis=1).astype(NARROW)
        mixing = lax.psum(products, "tp")
        one.mixing = jnp.where(one.linked, mixing, jnp.zeros_like(mixing))

    def span_of(own):
        start = (reach * blocks_each - LAGS + own) * SPAN
        return slice(start, start + LAGS * SPAN)

    def remember(one):
        halos = [
            jnp.zeros((count, blocks_each * SPAN, local_width), NARROW) for _ in range(reach)
        ]
        pending = {}
        for turn in range(parts):
            for hop in range(1, reach + 1):
                if (turn - hop, hop) in pending:
                    halos[reach - hop] = halos[reach - hop] + pending[(turn - hop, hop)]
            known = jnp.concatenate(halos, axis=1)
            recalls = []
            errors = []
            for own in range(blocks_each):
                total = batched("stu,sud->std", one.mixing[:, own], known[:, span_of(own)])
                recall = -step * one.scales[:, own] * total
                error = one.writing[:, own] * (
                    one.keeping[:, own] * recall - one.targets[:, own]
                )
                recalls.append(recall)
                errors.append(error)
                known = jnp.concatenate(
                    [known, (one.scales[:, own] * error).astype(NARROW)], axis=1
                )
            for hop in range(1, reach + 1):
                if turn + hop < parts:
                    pending[(turn, hop)] = passed_along(
                        known[:, reach * blocks_each * SPAN :], "ctx", [(turn, turn + hop)]
                    )
        one.known = known
        one.recall = jnp.stack(recalls, 1)
        one.errors = jnp.stack(errors, 1)
        heads_view = (one.reading[..., None] * one.recall).reshape(rows, local_heads, HD)
        one.head_factor = lax.rsqrt(
            jnp.mean(heads_view * heads_view, axis=-1, keepdims=True) + EPSILON
        )
        one.head_unit = heads_view * one.head_factor
        retrieved = (one.head_unit * gain_mem).reshape(rows, local_width).astype(NARROW)
        one.retrieved_full = lax.all_gather(retrieved, "tp", axis=1, tiled=True)

    def heads(values):
        return values.astype(NARROW).reshape(blocks, SPAN, local_heads, HD)

    def fixed(values):
        return jnp.broadcast_to(values, (blocks, persist_count, local_heads, HD))

    def scores_of(one):
        raw = batched("bthd,bkhd->bhtk", one.queries, one.keys) * scale
        return jnp.where(one.visible[:, None], raw, MASKED)

    def attend(one):
        one.queries = heads(matmul(one.input_low, query_w))
        one.keys = jnp.concatenate(
            [
                fixed(fixed_keys),
                heads(matmul(one.retrieved_full, key_w)),
                heads(matmul(one.input_low, key_w)),
            ],
            axis=1,
        )
        one.values = jnp.concatenate(
            [
                fixed(fixed_values),
                heads(matmul(one.retrieved_full, value_w)),
                heads(matmul(one.input_low, value_w)),
            ],
            axis=1,
        )
        label_rows = one.labels.reshape(blocks, SPAN)
        read_rows = one.reading.reshape(blocks, SPAN)
        visible_own = causal[None] & (label_rows[:, :, None] == label_rows[:, None, :])
        visible_memory = visible_own & (read_rows[:, None, :] > 0.5)
        one.visible = jnp.concatenate(
            [jnp.ones((blocks, SPAN, persist_count), jnp.bool_), visible_memory, visible_own],
            axis=2,
        )
        scores = scores_of(one)
        highest = jnp.max(scores, axis=-1, keepdims=True)
        raised = jnp.exp(scores - highest)
        totals = jnp.sum(raised, axis=-1, keepdims=True)
        one.logsum = highest + jnp.log(totals)
        probs_low = (raised / totals).astype(NARROW)
        one.attended = (
            batched("bhtk,bkhd->bthd", probs_low, one.values)
            .astype(NARROW)
            .reshape(rows, local_width)
        )
        one.residual = own_rows(one.flat).astype(WIDE)
        one.hidden = one.residual + scattered(matmul(one.attended, out_rows))
        normed_mid, one.unit_mid, one.factor_mid = norm_rows(one.hidden, gain_ffn_wide)
        one.mid_low = collected(normed_mid)

    def feed(one):
        gate = matmul(one.mid_low, gate_up_cols[0])
        upper = matmul(one.mid_low, gate_up_cols[1])
        one.activ = (jax.nn.silu(gate) * upper).astype(NARROW)
        grad_act = by_rows(one.upstream_low, down_rows)
        one.grad_gate = (grad_act * upper * silu_slope(gate)).astype(NARROW)
        one.grad_upper = (grad_act * jax.nn.silu(gate)).astype(NARROW)
        grad_mid = scattered(
            by_rows(one.grad_gate, gate_up_cols[0]) + by_rows(one.grad_upper, gate_up_cols[1])
        )
        one.grad_gain_ffn = jnp.sum(grad_mid * one.unit_mid, axis=0)
        upstream = own_rows(one.upstream_low).astype(WIDE)
        one.grad_hidden = upstream + norm_back(
            grad_mid, one.unit_mid, one.factor_mid, gain_ffn_wide
        )
        one.grad_mixed = collected(one.grad_hidden)

    def finish_output(one):
        branch = scattered(matmul(one.activ, down_rows))
        one.output = collected(one.hidden + branch).reshape(count, local_len, width)

    def attend_back(one):
        grad_attended = (
            by_rows(one.grad_mixed, out_rows)
            .astype(NARROW)
            .reshape(blocks, SPAN, local_heads, HD)
        )
        probs = jnp.exp(scores_of(one) - one.logsum)
        grad_probs = batched("bthd,bkhd->bhtk", grad_attended, one.values)
        grad_values = batched("bhtk,bthd->bkhd", probs.astype(NARROW), grad_attended)
        grad_scores = (
            probs * (grad_probs - jnp.sum(grad_probs * probs, axis=-1, keepdims=True))
        ).astype(NARROW)
        one.grad_queries = (
            (batched("bhtk,bkhd->bthd", grad_scores, one.keys) * scale)
            .astype(NARROW)
            .reshape(rows, local_width)
        )
        grad_keys = batched("bhtk,bthd->bkhd", grad_scores, one.queries) * scale

        def split_keys(grads):
            fixed_part = jnp.sum(grads[:, :persist_count], axis=0).reshape(
                persist_count, local_width
            )
            memory_part = (
                grads[:, persist_count : persist_count + SPAN]
                .astype(NARROW)
                .reshape(rows, local_width)
            )
            token_part = (
                grads[:, persist_count + SPAN :].astype(NARROW).reshape(rows, local_width)
            )
            return (fixed_part, memory_part, token_part)

        one.key_fixed, one.key_memory, one.key_token = split_keys(grad_keys)
        one.value_fixed, one.value_memory, one.value_token = split_keys(grad_values)
        grad_retrieved = lax.psum_scatter(
            (by_rows(one.key_memory, key_w) + by_rows(one.value_memory, value_w)).astype(NARROW),
            "tp",
            scatter_dimension=1,
            tiled=True,
        ).astype(WIDE)
        grad_heads = grad_retrieved.reshape(rows, local_heads, HD)
        one.grad_gain_memory = jnp.sum(grad_heads * one.head_unit, axis=0)
        inner = grad_heads * gain_mem
        grad_masked = one.head_factor * (
            inner - one.head_unit * jnp.mean(inner * one.head_unit, axis=-1, keepdims=True)
        )
        one.grad_read = one.reading[..., None] * grad_masked.reshape(
            count, blocks_each, SPAN, local_width
        )

    def remember_back(one):
        later = [0.0] * blocks_each
        pending = {}
        for turn in range(parts):
            for hop in range(1, reach + 1):
                if (turn - hop, hop) in pending:
                    arrived = pending[(turn - hop, hop)].astype(WIDE)
                    for own in range(blocks_each):
                        later[own] = later[own] + arrived[:, own * SPAN : (own + 1) * SPAN]
            known = [0.0] * (reach * blocks_each) + later
            grad_errors = [None] * blocks_each
            grad_recalls = [None] * blocks_each
            raws = [None] * blocks_each
            for own in range(blocks_each - 1, -1, -1):
                grad_scaled = -step * known[reach * blocks_each + own]
                grad_error = one.scales[:, own] * grad_scaled
                grad_recall = (
                    one.grad_read[:, own] + one.writing[:, own] * one.keeping[:, own] * grad_error
                )
                grad_errors[own] = jnp.broadcast_to(grad_error, grad_recall.shape)
                grad_recalls[own] = grad_recall
                raws[own] = (one.scales[:, own] * grad_recall).astype(NARROW)
                carried = batched("stu,std->sud", one.mixing[:, own], raws[own])
                for index in range(LAGS):
                    place = reach * blocks_each - LAGS + own + index
                    known[place] = (
                        known[place] + carried[:, index * SPAN : (index + 1) * SPAN]
                    )
            for hop in range(1, reach + 1):
                place = parts - 1 - turn
                if place - hop >= 0:
                    start = (reach - hop) * blocks_each
                    sent = jnp.concatenate(known[start : start + blocks_each], axis=1)
                    pending[(turn, hop)] = passed_along(
                        sent.astype(NARROW), "ctx", [(place, place - hop)]
                    )
        grad_errors = jnp.stack(grad_errors, 1)
        grad_recalls = jnp.stack(grad_recalls, 1)
        one.grad_targets = (-one.writing * grad_errors).astype(NARROW).reshape(rows, local_width)
        scale_part = jnp.sum(grad_recalls * one.recall + one.errors * grad_errors, axis=3)
        one.scale_sum = jnp.sum(lax.all_gather(scale_part.reshape(rows), "tp", axis=0), axis=0)
        grad_mixing = []
        for own in range(blocks_each):
            grad_mixing.append(
                -step * batched("std,sud->stu", raws[own], one.known[:, span_of(own)])
            )
        grad_mixing = jnp.where(one.linked, jnp.stack(grad_mixing, 1), 0.0)
        one.grad_mixing = lax.psum(grad_mixing.astype(NARROW), "tp")

    def features_back(one):
        def column(own, lag):
            start = (LAGS - 1 - lag) * SPAN
            return one.grad_mixing[:, own, :, start : start + SPAN]

        needed = {}
        for hop in range(1, reach + 1):
            pairs = [
                (own, lag)
                for own in range(blocks_each)
                for lag in range(LAGS)
                if place_of(own, lag)[0] == -hop
            ]
            moved = passed_along(
                jnp.stack([column(own, lag) for own, lag in pairs], axis=1),
                "ctx",
                [(source, source - hop) for source in range(hop, parts)],
            )
            for place, (own, lag) in enumerate(pairs):
                needed[(hop * blocks_each + own, lag)] = moved[:, place]
        for own in range(blocks_each):
            for lag in range(LAGS):
                needed[(own, lag)] = column(own, lag)
        grad_features = []
        one.grad_decays = [0.0] * LAGS
        for own in range(blocks_each):
            total = 0.0
            own_features = one.around[0][:, own].astype(WIDE)
            for lag in range(LAGS):
                delta, place = place_of(own, lag)
                from_reads = batched(
                    "stu,suh->sth", needed[(own, lag)], one.around[delta][:, place]
                )
                one.grad_decays[lag] = one.grad_decays[lag] + jnp.sum(
                    own_features * from_reads, axis=(0, 1)
                )
                later = own + 1 + lag
                delta, place = divmod(later, blocks_each)
                from_writes = batched(
                    "stu,sth->suh", needed[(later, lag)], one.around[delta][:, place]
                )
                total = total + decays[lag] * (from_reads + from_writes)
            grad_features.append(total)
        grad_features = jnp.stack(grad_features, 1).reshape(rows, local_units)
        grad_features = grad_features - (one.key_scale * one.key_scale * one.scale_sum)[
            :, None
        ] * one.features.astype(WIDE)
        one.grad_pre = (grad_features * silu_slope(one.preact)).astype(NARROW)

    def inputs_back(one):
        grad_input = (
            by_rows(one.grad_queries, query_w)
            + by_rows(one.key_token, key_w)
            + by_rows(one.value_token, value_w)
            + by_rows(one.grad_targets, value_cols)
            + by_rows(one.grad_pre, feature_cols)
        )
        grad_input = scattered(grad_input)
        _, unit_in, factor_in = norm_rows(one.residual, gain_in_wide)
        one.grad_gain_in = jnp.sum(grad_input * unit_in, axis=0)
        one.grad_tokens = (
            collected(one.grad_hidden + norm_back(grad_input, unit_in, factor_in, gain_in_wide))
            .astype(WIDE)
            .reshape(count, local_len, width)
        )

    streams = [Stream() for _ in range(STREAMS)]
    for index, one in enumerate(streams):
        begin(one, index)
    for stage in (remember, attend, feed):
        for one in streams:
            stage(one)

    def over(function):
        total = function(streams[0])
        for one in streams[1:]:
            total = total + function(one)
        return total

    core, outer = (part % 2, part // 2)
    fours = (2, 2)

    def shared(array, by_row):
        array = array.astype(NARROW)
        *lead, high, wide = array.shape
        if by_row:
            array = array.reshape(*lead, 2, *fours, high // 8, wide)
            core_axis = len(lead) + 1
            half_axis = len(lead)
        else:
            array = array.reshape(*fours, high // 4, wide)
            core_axis = 0
        sent = flipped(pick(array, 1 - core, core_axis), "ctx", 1)
        array = (pick(array, core, core_axis).astype(WIDE) + sent.astype(WIDE)).astype(NARROW)
        if by_row:
            own, other = (pick(array, place, half_axis) for place in (half_index, 1 - half_index))
            outer_axis = half_axis
        else:
            half = wide // 2
            own, other = (
                lax.dynamic_slice_in_dim(array, place * half, half, 2)
                for place in (half_index, 1 - half_index)
            )
            outer_axis = 0
        array = (own.astype(WIDE) + flipped(other, "shard", 1).astype(WIDE)).astype(NARROW)
        sent = flipped(pick(array, 1 - outer, outer_axis), "ctx", 2)
        array = (pick(array, outer, outer_axis).astype(WIDE) + sent.astype(WIDE)).astype(NARROW)
        array = jnp.stack(either(outer == 0, array, flipped(array, "ctx", 2)), axis=outer_axis)
        array = jnp.stack(either(core == 0, array, flipped(array, "ctx", 1)), axis=outer_axis)
        if by_row:
            return array.reshape(*lead, high // 2, wide).astype(WIDE)
        return array.reshape(high, wide // 2).astype(WIDE)

    grad_down = shared(over(lambda one: over_rows(one.activ, one.upstream_low)), False)
    grad_gate_up = shared(
        jnp.stack(
            [
                over(lambda one: over_rows(one.mid_low, one.grad_gate)).astype(NARROW),
                over(lambda one: over_rows(one.mid_low, one.grad_upper)).astype(NARROW),
            ]
        ),
        True,
    )
    for one in streams:
        attend_back(one)
    for one in streams:
        finish_output(one)
    grad_out_rows = shared(over(lambda one: over_rows(one.attended, one.grad_mixed)), False)
    persist_wide = persist.astype(WIDE)
    key_fixed = over(lambda one: one.key_fixed)
    value_fixed = over(lambda one: one.value_fixed)
    grad_query_w = over(lambda one: over_rows(one.input_low, one.grad_queries))
    grad_key_w = over(
        lambda one: over_rows(one.input_low, one.key_token)
        + over_rows(one.retrieved_full, one.key_memory)
    ) + exact_product(persist_wide.T, key_fixed)
    grad_value_proj = over(
        lambda one: over_rows(one.input_low, one.value_token)
        + over_rows(one.retrieved_full, one.value_memory)
    ) + exact_product(persist_wide.T, value_fixed)
    grad_qkv = shared(
        jnp.stack([item.astype(NARROW) for item in (grad_query_w, grad_key_w, grad_value_proj)]),
        True,
    )
    grad_persist = exact_product(key_fixed, key_w.astype(WIDE).T) + exact_product(
        value_fixed, value_w.astype(WIDE).T
    )
    grad_persist = lax.psum_scatter(grad_persist, "tp", scatter_dimension=0, tiled=True)

    for one in streams:
        remember_back(one)
    grad_target_w = shared(over(lambda one: over_rows(one.input_low, one.grad_targets)), True)
    for one in streams:
        features_back(one)
    grad_feature_w = shared(over(lambda one: over_rows(one.input_low, one.grad_pre)), True)
    for one in streams:
        inputs_back(one)

    grad_decays = [over(lambda one: one.grad_decays[lag]) for lag in range(LAGS)]
    grad_retain = 0.0
    grad_moment = 0.0
    retain_slope = jnp.zeros_like(retain)
    for lag in range(1, LAGS):
        retain_slope = retain * retain_slope + decays[lag - 1]
        moment_slope = 0.0
        for power in range(1, lag + 1):
            moment_slope = moment_slope + power * retain ** (lag - power) * moment ** (power - 1)
        grad_retain = grad_retain + retain_slope * grad_decays[lag]
        grad_moment = grad_moment + moment_slope * grad_decays[lag]
    grad_rates = jnp.stack([grad_retain, grad_moment])

    pieces = [
        grad_persist,
        over(lambda one: one.grad_gain_in),
        over(lambda one: one.grad_gain_ffn),
        over(lambda one: one.grad_gain_memory),
        grad_rates,
    ]
    small = jnp.concatenate([piece.reshape(-1) for piece in pieces])
    small = small + flipped(small, "ctx", 1)
    small = small + flipped(small, "shard", 1)
    small = small + flipped(small, "ctx", 2)
    cut = grad_persist.size + 2 * width
    spread = lax.all_gather(small[:cut], "tp", axis=0)
    grad_persist = spread[:, : grad_persist.size].reshape(persist_count, width)
    gains = jnp.sum(spread[:, grad_persist.size // ranks :], axis=0).reshape(2, width)
    middle = cut + local_heads * HD
    grad_gain_memory = small[cut:middle].reshape(local_heads, HD)
    grad_rates = small[middle:].reshape(2, local_units)

    def own_half(array, axis):
        size = array.shape[axis] // 2
        return lax.dynamic_slice_in_dim(array, half_index * size, size, axis)

    return (
        jnp.concatenate([one.output for one in streams], axis=0),
        jnp.concatenate([one.grad_tokens for one in streams], axis=0),
        own_half(gains[0], 0),
        own_half(gains[1], 0),
        own_half(grad_gain_memory, 1),
        own_half(grad_rates, 0),
        own_half(grad_persist, 1),
        grad_qkv,
        grad_out_rows,
        grad_target_w,
        grad_feature_w,
        grad_gate_up,
        grad_down,
    )


def solution(mesh):
    placed = (
        P("shard", "ctx", None),
        P("shard", "ctx"),
        P("shard"),
        P("shard"),
        P("tp", "shard"),
        P("shard", None),
        P(None, "shard"),
        P(None, "shard", "tp"),
        P("tp", "shard"),
        P("shard", "tp"),
        P("shard", "tp"),
        P(None, "shard", "tp"),
        P("tp", "shard"),
        P("shard", "ctx", None),
    )
    return jax.shard_map(
        on_device,
        mesh=mesh,
        in_specs=placed,
        out_specs=(
            P("shard", "ctx", None),
            P("shard", "ctx", None),
            P("shard"),
            P("shard"),
            P("tp", "shard"),
            P("shard", "tp"),
            P(None, "shard"),
            P(None, "shard", "tp"),
            P("tp", "shard"),
            P("shard", "tp"),
            P("shard", "tp"),
            P(None, "shard", "tp"),
            P("tp", "shard"),
        ),
        check_vma=False,
    )
```

time: 2220 us -> 1330 us (0.60)
  waiting for transfers between devices: 1490 us -> 613 us
  matrix products: 312 us -> 247 us
  other arithmetic: 123 us -> 151 us
    psum x4 -> x2, waiting for transfers between devices: 436 us -> 109 us  [the longest x1 67.1 us: begin(): mixing = lax.psum(products, 'tp')]
    reduce_scatter x6 -> x1, waiting for transfers between devices: 283 us -> 0.01 us  [on_device(): lax.psum_scatter(grad_persist, 'tp', scatter_dimension=0, tiled=True)]
    all_gather x8 -> x1, waiting for transfers between devices: 256 us -> 0.01 us  [remember(): one.retrieved_full = lax.all_gather(retrieved, 'tp', axis=1, tiled=True)]
    ppermute x14 -> x55, waiting for transfers between devices: 112 us -> 255 us  [the longest x43 210 us: flipped(): lax.ppermute(value, axis, [(i, i ^ bit) for i in range(lax.axis_size(axis...]
    all_gather x4, waiting for transfers between devices: 187 us -> 95.8 us  [collected(): return lax.all_gather(array.astype(NARROW), 'tp', axis=0, tiled=True)]
    psum x4 -> x0, blocking collectives: 85.3 us -> none  [the longest x2 66 us: small(): summed = lax.psum(array, axes)]
    all_gather x6 -> x4, blocking collectives: 27.1 us -> 101 us  [the longest x1 61.3 us: on_device(): block_lasts = lax.all_gather(lasts_all, 'ctx', axis=1, tiled=True)]
    reduce_scatter x4, waiting for transfers between devices: 152 us -> 118 us  [scattered(): lax.psum_scatter(array.astype(NARROW), 'tp', scatter_dimension=0, tiled=T...]
  transfers between devices with their start and end apart: 41 -> 68, of which waited for: 36 -> 34; matrix products, arithmetic and copies ran while one was open for 15% -> 26% of each run, Pallas kernels for 0% -> 0%
where the time goes in v2:
time: 1330 us; the launch traced here: 1320 us
  waiting for transfers between devices  613 us (46%)
  matrix products  247 us (19%)
  other arithmetic  151 us (11%)
  local copies, waits for them, and re-layouts  127 us (10%)
  blocking collectives  101 us (8%)
  starting transfers between devices  64.2 us (5%)
  between operations  17.8 us (1%)
    ppermute x43, waiting for transfers between devices, flipped(): lax.ppermute(value, axis, [(i, i ^ bit) for i in range(lax.axis_size(axis...  210 us
    reduce_scatter x4, waiting for transfers between devices, scattered(): lax.psum_scatter(array.astype(NARROW), 'tp', scatter_dimension=0, tiled=T...  118 us
    all_gather x4, waiting for transfers between devices, collected(): return lax.all_gather(array.astype(NARROW), 'tp', axis=0, tiled=True)  95.8 us
    dot_general x16, matrix products, matmul(): return jnp.dot(left, right, preferred_element_type=WIDE)  78 us
    dot_general x47, matrix products, batched(): return jnp.einsum(spec, left, right, preferred_element_type=WIDE)  70.6 us
    psum x1, waiting for transfers between devices, begin(): mixing = lax.psum(products, 'tp')  67.1 us
    dot_general x11, matrix products, by_rows(): lax.dot_general(left, right, (((1,), (1,)), ((), ())), preferred_element_...  62.7 us
    all_gather x1, blocking collectives, on_device(): block_lasts = lax.all_gather(lasts_all, 'ctx', axis=1, tiled=True)  61.3 us
  transfers between devices with their start and end apart: 68, of which 34 were waited for; matrix products, arithmetic and copies ran while one was open for 26% of the time, Pallas kernels for 0%

profile of v2, /device:TPU:1, one launch (start us, length us, event | category | flops | bytes accessed | tf_op | source)
XLA Modules:
  0.0 1321.7 jit_solution(85045902495187591)
XLA Ops:
  18.1 61.3 %all-gather = f32[2,8,1]{0,2,1:T(1,128)S(1)} all-gather(f32[2,2,1]{0,2,1:T(1,128)S(1)} %copy.464), channel_id=2, replica_groups=mesh['shard'=2,'ctx'=4,'tp'=4] {'ctx'}, dimensions={1}, use_global_device_ids=true | all-gather | bytes 80 | tf_op jit(solution)/shard_map/all_gather | solution.py:160
  132.5 10.8 all-gather.1
  148.8 67.1 %all-reduce.5.cloned.1.call-done = bf16[2,2,256,1024]{2,3,0,1:T(8,128)(2,1)} async-done(((bf16[2,2,256,1024]{2,3,0,1:T(8,128)(2,1)}), bf16[2,2,256,1024]{2,3,0,1:T(8,128)(2,1)}) %all-reduce.5.cloned.1.call-update) | async-done | bytes 2097168 | tf_op jit(solution)/shard_map/psum | solution.py:253
  230.8 13.7 %collective-permute-done.10 = bf16[2,512,384]{2,1,0:T(8,128)(2,1)S(1)} collective-permute-done((bf16[2,512,384]{2,1,0:T(8,128)(2,1)}, bf16[2,512,384]{2,1,0:T(8,128)(2,1)S(1)}, u32[]{:S(2)}, u32[]{:S(2)}) %collective-permute-start.10) | collective-permute-done | bytes 786464 | tf_op jit(solution)/shard_map/ppermute | solution.py:20
  275.0 36.4 %collective-permute-done.2 = bf16[3,768,384]{2,1,0:T(8,128)(2,1)S(1)} collective-permute-done((bf16[3,768,384]{2,1,0:T(8,128)(2,1)}, bf16[3,768,384]{2,1,0:T(8,128)(2,1)S(1)}, u32[]{:S(2)}, u32[]{:S(2)}) %collective-permute-start.2) | collective-permute-done | bytes 1769504 | tf_op jit(solution)/shard_map/ppermute | solution.py:24
  383.2 59.4 %reduce-scatter.9.cloned.1.call-done = bf16[256,1536]{1,0:T(8,128)(2,1)} async-done(((bf16[1024,1536]{1,0:T(8,128)(2,1)}), bf16[256,1536]{1,0:T(8,128)(2,1)}) %reduce-scatter.9.cloned.1.call-update) | async-done | bytes 786448 | tf_op jit(solution)/shard_map/reduce_scatter | solution.py:145
  459.0 27.9 %collective-permute-done.14 = bf16[1024,768]{1,0:T(8,128)(2,1)S(1)} collective-permute-done((bf16[1024,768]{1,0:T(8,128)(2,1)}, bf16[1024,768]{1,0:T(8,128)(2,1)S(1)}, u32[]{:S(2)}, u32[]{:S(2)}) %collective-permute-start.14) | collective-permute-done | bytes 1572896 | tf_op jit(solution)/shard_map/ppermute | solution.py:24
  493.8 16.3 %all-gather.12.cloned.1.call-done = bf16[1024,1536]{1,0:T(8,128)(2,1)} async-done(((bf16[256,1536]{1,0:T(8,128)(2,1)}), bf16[1024,1536]{1,0:T(8,128)(2,1)}) %all-gather.12.cloned.1.call-update) | async-done | bytes 3145744 | tf_op jit(solution)/shard_map/all_gather | solution.py:150
  535.0 58.9 %reduce-scatter.13.cloned.1.call-done = bf16[256,1536]{1,0:T(8,128)(2,1)} async-done(((bf16[1024,1536]{1,0:T(8,128)(2,1)}), bf16[256,1536]{1,0:T(8,128)(2,1)}) %reduce-scatter.13.cloned.1.call-update) | async-done | bytes 786448 | tf_op jit(solution)/shard_map/reduce_scatter | solution.py:145
  601.0 62.9 %all-gather.16.cloned.1.call-done = bf16[1024,1536]{1,0:T(8,128)(2,1)} async-done(((bf16[256,1536]{1,0:T(8,128)(2,1)}), bf16[1024,1536]{1,0:T(8,128)(2,1)}) %all-gather.16.cloned.1.call-update) | async-done | bytes 3145744 | tf_op jit(solution)/shard_map/all_gather | solution.py:150
  689.7 10.6 multiply_convert_fusion
  741.1 35.7 %reduce-scatter.19.cloned.1.call-done = bf16[384,1024]{1,0:T(8,128)(2,1)} async-done(((bf16[1536,1024]{1,0:T(8,128)(2,1)}), bf16[384,1024]{1,0:T(8,128)(2,1)}) %reduce-scatter.19.cloned.1.call-update) | async-done | bytes 786448
  876.0 11.0 all-gather.3
  892.8 41.5 %all-reduce.7.cloned.1.call-done = bf16[2,2,256,1024]{2,3,0,1:T(8,128)(2,1)} async-done(((bf16[2,2,256,1024]{2,3,0,1:T(8,128)(2,1)}), bf16[2,2,256,1024]{2,3,0,1:T(8,128)(2,1)}) %all-reduce.7.cloned.1.call-update) | async-done | bytes 2097168 | tf_op jit(solution)/shard_map/psum | solution.py:470
  957.4 13.4 %collective-permute-done.20 = bf16[2,4,256,256]{2,3,0,1:T(8,128)(2,1)} collective-permute-done((bf16[2,4,256,256]{2,3,0,1:T(8,128)(2,1)}, bf16[2,4,256,256]{2,3,0,1:T(8,128)(2,1)}, u32[]{:S(2)}, u32[]{:S(2)}) %collective-permute-start.20) | collective-permute-done | bytes 1048608 | tf_op jit(solution)/shard_map/ppermute | solution.py:20
  991.3 14.6 %add_convert_fusion = bf16[1024,1536]{1,0:T(8,128)(2,1)} fusion(f32[1024,1536]{1,0:T(8,128)} %fusion.227, f32[1024,1536]{1,0:T(8,128)} %fusion.332, f32[1024,1536]{1,0:T(8,128)} %fusion.306, f32[1024,1536]{1,0:T(8,128)} %fusion.331, bf16[1024,1536]{1,0:T(8,128)(2,1)S(1)} %fusion.8, bf16[768,1536]{1,0:T(8,128)(2,1)} %copy-done.98, ...), kind=kOutput, calls=%fused_computation.50 | convolution fusion | flops 4849139712 | bytes 36175872 | tf_op jit(solution)/shard_map/dot_general | solution.py:64
  1017.7 13.6 %collective-permute-done.51 = bf16[2,256,768]{2,1,0:T(8,128)(2,1)} collective-permute-done((bf16[2,256,768]{2,1,0:T(8,128)(2,1)}, bf16[2,256,768]{2,1,0:T(8,128)(2,1)}, u32[]{:S(2)}, u32[]{:S(2)}) %collective-permute-start.51) | collective-permute-done | bytes 786464 | tf_op jit(solution)/shard_map/ppermute | solution.py:24
  1033.9 10.7 collective-permute-done.52
  1126.1 12.6 collective-permute-done.26
  1183.7 27.2 %collective-permute-done.36 = bf16[2,192,384]{2,1,0:T(8,128)(2,1)S(1)} collective-permute-done((bf16[2,192,384]{2,1,0:T(8,128)(2,1)S(1)}, bf16[2,192,384]{2,1,0:T(8,128)(2,1)S(1)}, u32[]{:S(2)}, u32[]{:S(2)}) %collective-permute-start.36) | collective-permute-done | bytes 294944 | tf_op jit(solution)/shard_map/ppermute | solution.py:24
  1220.0 11.9 collective-permute-done.38
  1236.5 12.2 collective-permute-done.43
  1269.0 18.2 %all-gather.2 = f32[110592]{0:T(1024)S(1)} all-gather(f32[27648]{0:T(1024)S(1)} %slice.662), channel_id=4, replica_groups=mesh['shard'=2,'ctx'=4,'tp'=4] {'tp'}, dimensions={0}, use_global_device_ids=true | all-gather | bytes 552960 | tf_op jit(solution)/shard_map/all_gather | solution.py:655
  1291.1 16.6 %all-gather.18.cloned.1.call-done = bf16[1024,1536]{1,0:T(8,128)(2,1)} async-done(((bf16[256,1536]{1,0:T(8,128)(2,1)}), bf16[1024,1536]{1,0:T(8,128)(2,1)}) %all-gather.18.cloned.1.call-update) | async-done | bytes 3145744 | tf_op jit(solution)/shard_map/all_gather | solution.py:150
  (959 shorter events, 639.3 us)
Async XLA Ops:
  7.2 208.7 %all-reduce.5.cloned.1.call-start = ((), (), s32[]{:S(2)}) async-start(), calls=%async_computation.6 | async-start | bytes 4194304 | tf_op jit(solution)/shard_map/psum | solution.py:253
  7.3 76.4 %collective-permute-start.3 = (bf16[2,512,1536]{2,1,0:T(8,128)(2,1)}, bf16[2,512,1536]{2,1,0:T(8,128)(2,1)S(1)}, u32[]{:S(2)}, u32[]{:S(2)}) collective-permute-start(bf16[2,512,1536]{2,1,0:T(8,128)(2,1)} %param.14), channel_id=1, source_target_pairs={{0,8},{4,12},{8,0},{12,4},{1,9},{5,13},{9,1},{13,5},{2,10},{6,14},... | collective-permute-start | bytes 9437192 | tf_op jit(solution)/shard_map/ppermute | solution.py:24
  9.4 79.7 %collective-permute-start.4 = (bf16[2,512,1536]{2,1,0:T(8,128)(2,1)}, bf16[2,512,1536]{2,1,0:T(8,128)(2,1)}, u32[]{:S(2)}, u32[]{:S(2)}) collective-permute-start(bf16[2,512,1536]{2,1,0:T(8,128)(2,1)} %param.14), channel_id=1, source_target_pairs={{0,4},{4,0},{8,12},{12,8},{1,5},{5,1},{9,13},{13,9},{2,6},{6,2},{1... | collective-permute-start | bytes 9437192 | tf_op jit(solution)/shard_map/ppermute | solution.py:24
  15.6 67.3 %collective-permute-start = (bf16[57024]{0:T(1024)(128)(2,1)S(1)}, bf16[57024]{0:T(1024)(128)(2,1)S(1)}, u32[]{:S(2)}, u32[]{:S(2)}) collective-permute-start(bf16[57024]{0:T(1024)(128)(2,1)S(1)} %concatenate.155), channel_id=1, source_target_pairs={{0,16},{16,0},{1,17},{17,1},{2,18},{18,2},{3,19},{19,3},{4,20},{20... | collective-permute-start | bytes 342152 | tf_op jit(solution)/shard_map/ppermute | solution.py:24
  17.8 66.3 %collective-permute-start.1 = (bf16[768,1536]{1,0:T(8,128)(2,1)}, bf16[768,1536]{1,0:T(8,128)(2,1)}, u32[]{:S(2)}, u32[]{:S(2)}) collective-permute-start(bf16[768,1536]{1,0:T(8,128)(2,1)} %param.24), channel_id=1, source_target_pairs={{0,16},{16,0},{1,17},{17,1},{2,18},{18,2},{3,19},{19,3},{4,20},{20... | collective-permute-start | bytes 7077896 | tf_op jit(solution)/shard_map/ppermute | solution.py:24
  84.1 45.8 %collective-permute-start.6 = (bf16[768,384]{1,0:T(8,128)(2,1)}, bf16[768,384]{1,0:T(8,128)(2,1)}, u32[]{:S(2)}, u32[]{:S(2)}) collective-permute-start(bf16[768,384]{1,0:T(8,128)(2,1)} %param.23), channel_id=1, source_target_pairs={{0,16},{16,0},{1,17},{17,1},{2,18},{18,2},{3,19},{19,3},{4,20},{20... | collective-permute-start | bytes 1769480 | tf_op jit(solution)/shard_map/ppermute | solution.py:24
  129.5 224.8 %all-gather.10.cloned.1.call-start = ((), (), s32[]{:S(2)}) async-start(), calls=%async_computation.7 | async-start | bytes 3932160 | tf_op jit(solution)/shard_map/all_gather | solution.py:297
  271.7 170.9 %reduce-scatter.9.cloned.1.call-start = ((), (), s32[]{:S(2)}) async-start(), calls=%async_computation.8 | async-start | bytes 3932160 | tf_op jit(solution)/shard_map/reduce_scatter | solution.py:145
  271.7 39.7 %collective-permute-start.2 = (bf16[3,768,384]{2,1,0:T(8,128)(2,1)}, bf16[3,768,384]{2,1,0:T(8,128)(2,1)S(1)}, u32[]{:S(2)}, u32[]{:S(2)}) collective-permute-start(bf16[3,768,384]{2,1,0:T(8,128)(2,1)} %param.21), channel_id=1, source_target_pairs={{0,16},{16,0},{1,17},{17,1},{2,18},{18,2},{3,19},{19,3},{4,20},{20... | collective-permute-start | bytes 5308424 | tf_op jit(solution)/shard_map/ppermute | solution.py:24
  381.2 128.9 %all-gather.12.cloned.1.call-start = ((), (), s32[]{:S(2)}) async-start(), calls=%async_computation.9 | async-start | bytes 3932160 | tf_op jit(solution)/shard_map/all_gather | solution.py:150
  381.2 70.2 %collective-permute-start.13 = (bf16[2,768,1024]{2,1,0:T(8,128)(2,1)}, bf16[2,768,1024]{2,1,0:T(8,128)(2,1)}, u32[]{:S(2)}, u32[]{:S(2)}) collective-permute-start(bf16[2,768,1024]{2,1,0:T(8,128)(2,1)} %param.25), channel_id=1, source_target_pairs={{0,16},{16,0},{1,17},{17,1},{2,18},{18,2},{3,19},{19,3},{4,20},{20... | collective-permute-start | bytes 9437192 | tf_op jit(solution)/shard_map/ppermute | solution.py:24
  446.4 147.6 %reduce-scatter.13.cloned.1.call-start = ((), (), s32[]{:S(2)}) async-start(), calls=%async_computation.12 | async-start | bytes 3932160 | tf_op jit(solution)/shard_map/reduce_scatter | solution.py:145
  451.4 35.6 %collective-permute-start.14 = (bf16[1024,768]{1,0:T(8,128)(2,1)}, bf16[1024,768]{1,0:T(8,128)(2,1)S(1)}, u32[]{:S(2)}, u32[]{:S(2)}) collective-permute-start(bf16[1024,768]{1,0:T(8,128)(2,1)} %param.26), channel_id=1, source_target_pairs={{0,16},{16,0},{1,17},{17,1},{2,18},{18,2},{3,19},{19,3},{4,20},{20... | collective-permute-start | bytes 4718600 | tf_op jit(solution)/shard_map/ppermute | solution.py:24
  535.0 128.9 %all-gather.16.cloned.1.call-start = ((), (), s32[]{:S(2)}) async-start(), calls=%async_computation.13 | async-start | bytes 3932160 | tf_op jit(solution)/shard_map/all_gather | solution.py:150
  600.2 176.6 %reduce-scatter.19.cloned.1.call-start = ((), (), s32[]{:S(2)}) async-start(), calls=%async_computation.18 | async-start | bytes 3932160
  717.8 216.5 %all-reduce.7.cloned.1.call-start = ((), (), s32[]{:S(2)}) async-start(), calls=%async_computation.14 | async-start | bytes 4194304 | tf_op jit(solution)/shard_map/psum | solution.py:470
  801.5 204.8 %collective-permute-start.50 = (bf16[2,256,1536]{2,1,0:T(8,128)(2,1)}, bf16[2,256,1536]{2,1,0:T(8,128)(2,1)}, u32[]{:S(2)}, u32[]{:S(2)}) collective-permute-start(bf16[2,256,1536]{2,1,0:T(8,128)(2,1)} %dynamic-slice_bitcast_fusion.2), channel_id=1, source_target_pairs={{0,4},{4,0},{8,12},{12,8},{1,5},{5,1},{9,13},{13,9},{2,6},{6,2},{1... | collective-permute-start | bytes 4718600 | tf_op jit(solution)/shard_map/ppermute | solution.py:24
  835.1 177.5 %collective-permute-start.45 = (bf16[2,2,2,192,1024]{4,3,2,1,0:T(8,128)(2,1)}, bf16[2,2,2,192,1024]{4,3,2,1,0:T(8,128)(2,1)}, u32[]{:S(2)}, u32[]{:S(2)}) collective-permute-start(bf16[2,2,2,192,1024]{4,3,2,1,0:T(8,128)(2,1)} %fusion.56), channel_id=1, source_target_pairs={{0,4},{4,0},{8,12},{12,8},{1,5},{5,1},{9,13},{13,9},{2,6},{6,2},{1... | collective-permute-start | bytes 9437192 | tf_op jit(solution)/shard_map/ppermute | solution.py:24
  849.6 274.0 %reduce-scatter.17.cloned.1.call-start = ((), (), s32[]{:S(2)}) async-start(), calls=%async_computation.17 | async-start | bytes 491520 | tf_op jit(solution)/shard_map/reduce_scatter | solution.py:619
  871.1 296.2 %reduce-scatter.15.cloned.1.call-start = ((), (), s32[]{:S(2)}) async-start(), calls=%async_computation.15 | async-start | bytes 3932160 | tf_op jit(solution)/shard_map/reduce_scatter | solution.py:145
  937.9 40.4 %collective-permute-start.21 = (bf16[2,3,256,256]{2,3,0,1:T(8,128)(2,1)}, bf16[2,3,256,256]{2,3,0,1:T(8,128)(2,1)}, u32[]{:S(2)}, u32[]{:S(2)}) collective-permute-start(bf16[2,3,256,256]{2,3,0,1:T(8,128)(2,1)} %pad_maximum_fusion.70), channel_id=1, source_target_pairs={{8,0},{12,4},{9,1},{13,5},{10,2},{14,6},{11,3},{15,7},{24,16},{28,... | collective-permute-start | bytes 2359304 | tf_op jit(solution)/shard_map/ppermute | solution.py:20
  1005.9 163.8 %reduce-scatter.11.cloned.1.call-start = ((), (), s32[]{:S(2)}) async-start(), calls=%async_computation.10 | async-start | bytes 3932160 | tf_op jit(solution)/shard_map/reduce_scatter | solution.py:145
  1079.1 212.0 %all-gather.14.cloned.1.call-start = ((), (), s32[]{:S(2)}) async-start(), calls=%async_computation.11 | async-start | bytes 3932160 | tf_op jit(solution)/shard_map/all_gather | solution.py:150
  1174.2 133.4 %all-gather.18.cloned.1.call-start = ((), (), s32[]{:S(2)}) async-start(), calls=%async_computation.16 | async-start | bytes 3932160 | tf_op jit(solution)/shard_map/all_gather | solution.py:150
  (261 other events, 3610.0 us)
Sparse Core Ops, SparseCore 0:
  129.6 86.2 all-reduce.4
  271.8 62.6 all-gather.9
  381.3 61.2 reduce-scatter.8
  446.5 63.5 all-gather.11
  535.1 58.8 reduce-scatter.12
  600.3 63.5 all-gather.15
  717.9 58.8 reduce-scatter.18
  849.8 84.5 all-reduce.6
  936.6 18.2 reduce-scatter.16
  1006.1 58.0 reduce-scatter.14
  1079.2 62.7 reduce-scatter.10
  1174.4 62.1 all-gather.13
  1238.7 68.9 all-gather.17

commit v3 on v2

--- a/solution.py
+++ b/solution.py
@@ -114,13 +114,7 @@
     for item in smalls:
         small_others.append(small_other[start : start + item.size].reshape(item.shape))
         start += item.size
-    value_other, qkv_other = [
-        flipped(after(item, feature_other), "shard", 1) for item in (w_value, w_qkv)
-    ]
-    out_other, gate_up_other = [
-        flipped(after(item, value_other, qkv_other), "shard", 1) for item in (w_out, w_gate_up)
-    ]
-    down_other = flipped(after(w_down, out_other, gate_up_other), "shard", 1)
+    value_other = flipped(w_value, "shard", 1)
 
     gain_in_wide = joined(norm_gain, small_others[0], 0).astype(WIDE)
     gain_ffn_wide = joined(ffn_gain, small_others[1], 0).astype(WIDE)
@@ -129,17 +123,16 @@
     persist = joined(persistent, small_others[4], 1)
     feature_cols = joined(w_feature, feature_other, 0)
     value_cols = joined(w_value, value_other, 0)
-    qkv_cols = joined(w_qkv, qkv_other, 1)
-    out_rows = joined(w_out, out_other, 1)
-    gate_up_cols = joined(w_gate_up, gate_up_other, 1)
-    down_rows = joined(w_down, down_other, 1)
-    local_width = qkv_cols.shape[2]
+    weights = {}
+
+    def fetch(name, array, start):
+        weights[name] = flipped(after(array, start), "shard", 1)
+        return weights[name]
+
+    local_width = w_qkv.shape[2]
     local_units = feature_cols.shape[1]
     local_heads = local_width // HD
     persist_count = persist.shape[0]
-    query_w = qkv_cols[0]
-    key_w = qkv_cols[1]
-    value_w = qkv_cols[2]
 
     def scattered(array):
         return lax.psum_scatter(
@@ -181,10 +174,6 @@
     def place_of(own, lag):
         return divmod(own - 1 - lag, blocks_each)
 
-    fixed_keys = matmul(persist, key_w).astype(NARROW).reshape(1, persist_count, local_heads, HD)
-    fixed_values = (
-        matmul(persist, value_w).astype(NARROW).reshape(1, persist_count, local_heads, HD)
-    )
     position = jnp.arange(SPAN)
     causal = position[:, None] >= position[None, :]
 
@@ -223,19 +212,21 @@
         low, one.preact = features_of(mine(tokens))
         one.input_low = low.reshape(rows, width)
         one.features = jax.nn.silu(one.preact).astype(NARROW)
-        close = [mine(pair_tokens), mine(diagonal_tokens)]
+        far, pair, diagonal, one.features = lax.optimization_barrier(
+            (mine(far_tokens), mine(pair_tokens), mine(diagonal_tokens), one.features)
+        )
+        close = [pair, diagonal]
         one.around = {0: shaped(one.features)}
         for delta, piece in (
             (-1, jnp.where(odd_part, close[0], close[1])),
             (1, jnp.where(odd_part, close[1], close[0])),
-            (2, mine(far_tokens)),
+            (2, far),
         ):
             one.around[delta] = shaped(jax.nn.silu(features_of(piece)[1]).astype(NARROW))
         one.around[-2] = one.around[2]
         squares = jnp.sum(jnp.square(one.features.astype(WIDE)), axis=1)
         squares = jnp.sum(lax.all_gather(squares, "tp", axis=0), axis=0)
         one.key_scale = lax.rsqrt(squares + EPSILON)
-        one.scales = one.key_scale.reshape(count, blocks_each, SPAN, 1)
         one.targets = matmul(one.input_low, value_cols).reshape(
             count, blocks_each, SPAN, local_width
         )
@@ -250,14 +241,17 @@
                 )
             products.append(jnp.concatenate(row, axis=2))
         products = jnp.stack(products, axis=1).astype(NARROW)
-        mixing = lax.psum(products, "tp")
-        one.mixing = jnp.where(one.linked, mixing, jnp.zeros_like(mixing))
+        products, one.key_scale = lax.optimization_barrier((products, one.key_scale))
+        one.products = products
+        one.mixing = lax.psum(products, "tp")
 
     def span_of(own):
         start = (reach * blocks_each - LAGS + own) * SPAN
         return slice(start, start + LAGS * SPAN)
 
     def remember(one):
+        one.mixing = jnp.where(one.linked, one.mixing, jnp.zeros_like(one.mixing))
+        one.scales = one.key_scale.reshape(count, blocks_each, SPAN, 1)
         halos = [
             jnp.zeros((count, blocks_each * SPAN, local_width), NARROW) for _ in range(reach)
         ]
@@ -344,20 +338,26 @@
             .reshape(rows, local_width)
         )
         one.residual = own_rows(one.flat).astype(WIDE)
-        one.hidden = one.residual + scattered(matmul(one.attended, out_rows))
+        one.branch = scattered(matmul(one.attended, weights["out"]))
+
+    def middle(one):
+        one.hidden = one.residual + one.branch
         normed_mid, one.unit_mid, one.factor_mid = norm_rows(one.hidden, gain_ffn_wide)
         one.mid_low = collected(normed_mid)
 
     def feed(one):
-        gate = matmul(one.mid_low, gate_up_cols[0])
-        upper = matmul(one.mid_low, gate_up_cols[1])
+        gate = matmul(one.mid_low, weights["gate"])
+        upper = matmul(one.mid_low, weights["up"])
         one.activ = (jax.nn.silu(gate) * upper).astype(NARROW)
-        grad_act = by_rows(one.upstream_low, down_rows)
+        grad_act = by_rows(one.upstream_low, weights["down"])
         one.grad_gate = (grad_act * upper * silu_slope(gate)).astype(NARROW)
         one.grad_upper = (grad_act * jax.nn.silu(gate)).astype(NARROW)
-        grad_mid = scattered(
-            by_rows(one.grad_gate, gate_up_cols[0]) + by_rows(one.grad_upper, gate_up_cols[1])
-        )
+        one.grad_mid = scattered(
+            by_rows(one.grad_gate, weights["gate"]) + by_rows(one.grad_upper, weights["up"])
+        )
+
+    def middle_back(one):
+        grad_mid = one.grad_mid
         one.grad_gain_ffn = jnp.sum(grad_mid * one.unit_mid, axis=0)
         upstream = own_rows(one.upstream_low).astype(WIDE)
         one.grad_hidden = upstream + norm_back(
@@ -365,13 +365,19 @@
         )
         one.grad_mixed = collected(one.grad_hidden)
 
+    def branch_out(one):
+        activ, one.grad_mixed = lax.optimization_barrier((one.activ, one.grad_mixed))
+        one.branch = scattered(matmul(activ, weights["down"]))
+
     def finish_output(one):
-        branch = scattered(matmul(one.activ, down_rows))
-        one.output = collected(one.hidden + branch).reshape(count, local_len, width)
+        hidden, one.grad_retrieved = lax.optimization_barrier(
+            (one.hidden + one.branch, one.grad_retrieved)
+        )
+        one.output = collected(hidden)
 
     def attend_back(one):
         grad_attended = (
-            by_rows(one.grad_mixed, out_rows)
+            by_rows(one.grad_mixed, weights["out"])
             .astype(NARROW)
             .reshape(blocks, SPAN, local_heads, HD)
         )
@@ -404,13 +410,12 @@
 
         one.key_fixed, one.key_memory, one.key_token = split_keys(grad_keys)
         one.value_fixed, one.value_memory, one.value_token = split_keys(grad_values)
-        grad_retrieved = lax.psum_scatter(
-            (by_rows(one.key_memory, key_w) + by_rows(one.value_memory, value_w)).astype(NARROW),
-            "tp",
-            scatter_dimension=1,
-            tiled=True,
-        ).astype(WIDE)
-        grad_heads = grad_retrieved.reshape(rows, local_heads, HD)
+        partial = by_rows(one.key_memory, key_w) + by_rows(one.value_memory, value_w)
+        partial, one.branch = lax.optimization_barrier((partial.astype(NARROW), one.branch))
+        one.grad_retrieved = lax.psum_scatter(partial, "tp", scatter_dimension=1, tiled=True)
+
+    def heads_back(one):
+        grad_heads = one.grad_retrieved.astype(WIDE).reshape(rows, local_heads, HD)
         one.grad_gain_memory = jnp.sum(grad_heads * one.head_unit, axis=0)
         inner = grad_heads * gain_mem
         grad_masked = one.head_factor * (
@@ -466,8 +471,11 @@
             grad_mixing.append(
                 -step * batched("std,sud->stu", raws[own], one.known[:, span_of(own)])
             )
-        grad_mixing = jnp.where(one.linked, jnp.stack(grad_mixing, 1), 0.0)
-        one.grad_mixing = lax.psum(grad_mixing.astype(NARROW), "tp")
+        grad_mixing = jnp.where(one.linked, jnp.stack(grad_mixing, 1), 0.0).astype(NARROW)
+        grad_mixing, one.scale_sum, one.output = lax.optimization_barrier(
+            (grad_mixing, one.scale_sum, one.output)
+        )
+        one.grad_mixing = lax.psum(grad_mixing, "tp")
 
     def features_back(one):
         def column(own, lag):
@@ -526,7 +534,10 @@
             + by_rows(one.grad_targets, value_cols)
             + by_rows(one.grad_pre, feature_cols)
         )
-        grad_input = scattered(grad_input)
+        one.grad_input = scattered(grad_input)
+
+    def tokens_back(one):
+        grad_input = one.grad_input
         _, unit_in, factor_in = norm_rows(one.residual, gain_in_wide)
         one.grad_gain_in = jnp.sum(grad_input * unit_in, axis=0)
         one.grad_tokens = (
@@ -536,11 +547,6 @@
         )
 
     streams = [Stream() for _ in range(STREAMS)]
-    for index, one in enumerate(streams):
-        begin(one, index)
-    for stage in (remember, attend, feed):
-        for one in streams:
-            stage(one)
 
     def over(function):
         total = function(streams[0])
@@ -548,55 +554,119 @@
             total = total + function(one)
         return total
 
+    def every(stage):
+        for one in streams:
+            stage(one)
+
     core, outer = (part % 2, part // 2)
-    fours = (2, 2)
-
-    def shared(array, by_row):
-        array = array.astype(NARROW)
-        *lead, high, wide = array.shape
-        if by_row:
-            array = array.reshape(*lead, 2, *fours, high // 8, wide)
-            core_axis = len(lead) + 1
-            half_axis = len(lead)
-        else:
-            array = array.reshape(*fours, high // 4, wide)
-            core_axis = 0
-        sent = flipped(pick(array, 1 - core, core_axis), "ctx", 1)
-        array = (pick(array, core, core_axis).astype(WIDE) + sent.astype(WIDE)).astype(NARROW)
-        if by_row:
-            own, other = (pick(array, place, half_axis) for place in (half_index, 1 - half_index))
-            outer_axis = half_axis
-        else:
-            half = wide // 2
+
+    class Reduction:
+        def __init__(self, array, by_row):
+            array = array.astype(NARROW)
+            *self.lead, self.high, self.wide = array.shape
+            self.by_row = by_row
+            self.axis = len(self.lead)
+            if by_row:
+                array = array.reshape(*self.lead, 2, 2, 2, self.high // 8, self.wide)
+            else:
+                array = array.reshape(2, 2, self.high // 4, self.wide)
+            self.array = array
+            self.exchange(core, self.axis + 1 if by_row else 0, "ctx", 1)
+
+        def exchange(self, index, axis, over_axis, bit):
+            own, other = (pick(self.array, place, axis) for place in (index, 1 - index))
+            self.add(own, flipped(other, over_axis, bit))
+
+        def add(self, own, arrived):
+            self.array = (own.astype(WIDE) + arrived.astype(WIDE)).astype(NARROW)
+
+        def across(self):
+            if self.by_row:
+                self.exchange(half_index, self.axis, "shard", 1)
+                return
+            half = self.wide // 2
             own, other = (
-                lax.dynamic_slice_in_dim(array, place * half, half, 2)
+                lax.dynamic_slice_in_dim(self.array, place * half, half, 2)
                 for place in (half_index, 1 - half_index)
             )
-            outer_axis = 0
-        array = (own.astype(WIDE) + flipped(other, "shard", 1).astype(WIDE)).astype(NARROW)
-        sent = flipped(pick(array, 1 - outer, outer_axis), "ctx", 2)
-        array = (pick(array, outer, outer_axis).astype(WIDE) + sent.astype(WIDE)).astype(NARROW)
-        array = jnp.stack(either(outer == 0, array, flipped(array, "ctx", 2)), axis=outer_axis)
-        array = jnp.stack(either(core == 0, array, flipped(array, "ctx", 1)), axis=outer_axis)
-        if by_row:
-            return array.reshape(*lead, high // 2, wide).astype(WIDE)
-        return array.reshape(high, wide // 2).astype(WIDE)
-
-    grad_down = shared(over(lambda one: over_rows(one.activ, one.upstream_low)), False)
-    grad_gate_up = shared(
-        jnp.stack(
-            [
-                over(lambda one: over_rows(one.mid_low, one.grad_gate)).astype(NARROW),
-                over(lambda one: over_rows(one.mid_low, one.grad_upper)).astype(NARROW),
-            ]
+            self.add(own, flipped(other, "shard", 1))
+
+        def apart(self):
+            self.exchange(outer, self.axis if self.by_row else 0, "ctx", 2)
+
+        def together(self):
+            pair = either(outer == 0, self.array, flipped(self.array, "ctx", 2))
+            self.array = jnp.stack(pair, axis=self.axis if self.by_row else 0)
+
+        def result(self):
+            pair = either(core == 0, self.array, flipped(self.array, "ctx", 1))
+            array = jnp.stack(pair, axis=self.axis if self.by_row else 0).astype(WIDE)
+            if self.by_row:
+                return array.reshape(*self.lead, self.high // 2, self.wide)
+            return array.reshape(self.high, self.wide // 2)
+
+    def tied(names, *reductions):
+        held = [[getattr(one, name) for name in names] for one in streams]
+        held, arrays = lax.optimization_barrier((held, [item.array for item in reductions]))
+        for one, values in zip(streams, held):
+            for name, value in zip(names, values):
+                setattr(one, name, value)
+        for item, array in zip(reductions, arrays):
+            item.array = array
+
+    class Holder:
+        def __init__(self, array):
+            self.array = array
+
+    def fetched(names, *arrays):
+        holders = [Holder(fetch(str(index), item, start)) for index, (item, start) in enumerate(arrays)]
+        tied(names, *holders)
+        return [holder.array for holder in holders]
+
+    for index, one in enumerate(streams):
+        begin(one, index)
+    last = streams[-1]
+    (qkv_other,) = fetched(["mixing"], (w_qkv, last.products))
+    qkv_cols = joined(w_qkv, qkv_other, 1)
+    query_w = qkv_cols[0]
+    key_w = qkv_cols[1]
+    value_w = qkv_cols[2]
+    fixed_keys = matmul(persist, key_w).astype(NARROW).reshape(1, persist_count, local_heads, HD)
+    fixed_values = (
+        matmul(persist, value_w).astype(NARROW).reshape(1, persist_count, local_heads, HD)
+    )
+    every(remember)
+    out_other, down_other = fetched(
+        ["retrieved_full"], (w_out, last.recall), (w_down, last.recall)
+    )
+    weights["out"] = joined(w_out, out_other, 1)
+    weights["down"] = joined(w_down, down_other, 1)
+    every(attend)
+    (gate_other,) = fetched(["branch"], (w_gate_up[0], last.attended))
+    weights["gate"] = joined(w_gate_up[0], gate_other, 0)
+    every(middle)
+    (up_other,) = fetched(["mid_low"], (w_gate_up[1], last.hidden))
+    weights["up"] = joined(w_gate_up[1], up_other, 0)
+    every(feed)
+    feed_reductions = [
+        Reduction(over(lambda one: over_rows(one.activ, one.upstream_low)), False),
+        Reduction(
+            jnp.stack(
+                [
+                    over(lambda one: over_rows(one.mid_low, one.grad_gate)).astype(NARROW),
+                    over(lambda one: over_rows(one.mid_low, one.grad_upper)).astype(NARROW),
+                ]
+            ),
+            True,
         ),
-        True,
-    )
-    for one in streams:
-        attend_back(one)
-    for one in streams:
-        finish_output(one)
-    grad_out_rows = shared(over(lambda one: over_rows(one.attended, one.grad_mixed)), False)
+    ]
+    tied(["grad_mid"], *feed_reductions)
+    every(middle_back)
+    for item in feed_reductions:
+        item.across()
+    tied(["grad_mixed"], *feed_reductions)
+    every(branch_out)
+    every(attend_back)
     persist_wide = persist.astype(WIDE)
     key_fixed = over(lambda one: one.key_fixed)
     value_fixed = over(lambda one: one.value_fixed)
@@ -609,23 +679,34 @@
         lambda one: over_rows(one.input_low, one.value_token)
         + over_rows(one.retrieved_full, one.value_memory)
     ) + exact_product(persist_wide.T, value_fixed)
-    grad_qkv = shared(
-        jnp.stack([item.astype(NARROW) for item in (grad_query_w, grad_key_w, grad_value_proj)]),
-        True,
-    )
+    mix_reductions = [
+        Reduction(over(lambda one: over_rows(one.attended, one.grad_mixed)), False),
+        Reduction(
+            jnp.stack(
+                [item.astype(NARROW) for item in (grad_query_w, grad_key_w, grad_value_proj)]
+            ),
+            True,
+        ),
+    ]
     grad_persist = exact_product(key_fixed, key_w.astype(WIDE).T) + exact_product(
         value_fixed, value_w.astype(WIDE).T
     )
+    for item in feed_reductions:
+        item.apart()
+    tied(["grad_retrieved"], *feed_reductions, *mix_reductions)
+    every(finish_output)
+    every(heads_back)
+    every(remember_back)
+    grad_persist = after(grad_persist, last.grad_mixing)
     grad_persist = lax.psum_scatter(grad_persist, "tp", scatter_dimension=0, tiled=True)
-
-    for one in streams:
-        remember_back(one)
-    grad_target_w = shared(over(lambda one: over_rows(one.input_low, one.grad_targets)), True)
-    for one in streams:
-        features_back(one)
-    grad_feature_w = shared(over(lambda one: over_rows(one.input_low, one.grad_pre)), True)
-    for one in streams:
-        inputs_back(one)
+    target_reduction = Reduction(over(lambda one: over_rows(one.input_low, one.grad_targets)), True)
+    for item in feed_reductions:
+        item.together()
+    for item in mix_reductions:
+        item.across()
+    tied(["grad_mixing"], *feed_reductions, *mix_reductions, target_reduction)
+    every(features_back)
+    every(inputs_back)
 
     grad_decays = [over(lambda one: one.grad_decays[lag]) for lag in range(LAGS)]
     grad_retain = 0.0
@@ -640,34 +721,55 @@
         grad_moment = grad_moment + moment_slope * grad_decays[lag]
     grad_rates = jnp.stack([grad_retain, grad_moment])
 
-    pieces = [
-        grad_persist,
-        over(lambda one: one.grad_gain_in),
-        over(lambda one: one.grad_gain_ffn),
-        over(lambda one: one.grad_gain_memory),
-        grad_rates,
-    ]
-    small = jnp.concatenate([piece.reshape(-1) for piece in pieces])
-    small = small + flipped(small, "ctx", 1)
-    small = small + flipped(small, "shard", 1)
-    small = small + flipped(small, "ctx", 2)
-    cut = grad_persist.size + 2 * width
-    spread = lax.all_gather(small[:cut], "tp", axis=0)
-    grad_persist = spread[:, : grad_persist.size].reshape(persist_count, width)
-    gains = jnp.sum(spread[:, grad_persist.size // ranks :], axis=0).reshape(2, width)
-    middle = cut + local_heads * HD
-    grad_gain_memory = small[cut:middle].reshape(local_heads, HD)
-    grad_rates = small[middle:].reshape(2, local_units)
+    def summed(pieces):
+        small = jnp.concatenate([piece.reshape(-1) for piece in pieces])
+        for axis, bit in (("ctx", 1), ("shard", 1), ("ctx", 2)):
+            small = small + flipped(small, axis, bit)
+        return small
+
+    small = summed(
+        [
+            grad_persist,
+            over(lambda one: one.grad_gain_ffn),
+            over(lambda one: one.grad_gain_memory),
+            grad_rates,
+        ]
+    )
+    cut = grad_persist.size + width
+    spread = Holder(lax.all_gather(small[:cut], "tp", axis=0))
+    feature_reduction = Reduction(over(lambda one: over_rows(one.input_low, one.grad_pre)), True)
+    late_reductions = [feature_reduction, target_reduction]
+    for item in mix_reductions:
+        item.apart()
+    for item in late_reductions:
+        item.across()
+    tied(["grad_input"], spread, *mix_reductions, *late_reductions)
+    every(tokens_back)
+    for item in mix_reductions:
+        item.together()
+    for item in late_reductions:
+        item.apart()
+        item.together()
+    small_in = lax.all_gather(summed([over(lambda one: one.grad_gain_in)]), "tp", axis=0)
+    grad_persist = spread.array[:, : grad_persist.size].reshape(persist_count, width)
+    gain_ffn_sum = jnp.sum(spread.array[:, cut - width :], axis=0)
+    gain_in_sum = jnp.sum(small_in, axis=0)
+    middle_cut = cut + local_heads * HD
+    grad_gain_memory = small[cut:middle_cut].reshape(local_heads, HD)
+    grad_rates = small[middle_cut:].reshape(2, local_units)
+    grad_down, grad_gate_up = [item.result() for item in feed_reductions]
+    grad_out_rows, grad_qkv = [item.result() for item in mix_reductions]
+    grad_feature_w, grad_target_w = [item.result() for item in late_reductions]
 
     def own_half(array, axis):
         size = array.shape[axis] // 2
         return lax.dynamic_slice_in_dim(array, half_index * size, size, axis)
 
     return (
-        jnp.concatenate([one.output for one in streams], axis=0),
+        jnp.concatenate([one.output for one in streams], axis=0).reshape(tokens.shape),
         jnp.concatenate([one.grad_tokens for one in streams], axis=0),
-        own_half(gains[0], 0),
-        own_half(gains[1], 0),
+        own_half(gain_in_sum, 0),
+        own_half(gain_ffn_sum, 0),
         own_half(grad_gain_memory, 1),
         own_half(grad_rates, 0),
         own_half(grad_persist, 1),

time: 1330 us -> 1240 us (0.932)
  waiting for transfers between devices: 613 us -> 465 us
  other arithmetic: 151 us -> 173 us
  starting transfers between devices: 64.2 us -> 81.3 us
  matrix products: 247 us -> 261 us
    all_gather x4, waiting for transfers between devices: 95.8 us -> 41.4 us  [collected(): return lax.all_gather(array.astype(NARROW), 'tp', axis=0, tiled=True)]
    ppermute x43 -> x47, waiting for transfers between devices: 210 us -> 174 us  [flipped(): lax.ppermute(value, axis, [(i, i ^ bit) for i in range(lax.axis_size(axis...]
    reduce_scatter x4, waiting for transfers between devices: 118 us -> 87.9 us  [scattered(): lax.psum_scatter(array.astype(NARROW), 'tp', scatter_dimension=0, tiled=T...]
    unnamed x14, waiting for transfers between devices: 35.9 us -> 6.35 us
    ppermute x12, waiting for transfers between devices: 44.2 us -> 23.9 us  [passed_along(): return lax.ppermute(value, axis, pairs)]
    convert_element_type x27 -> x30, other arithmetic: 30.4 us -> 48.6 us  [the longest x18 30.7 us: add(): self.array = (own.astype(WIDE) + arrived.astype(WIDE)).astype(NARROW)]
    dot_general x47, matrix products: 70.6 us -> 86 us  [batched(): return jnp.einsum(spec, left, right, preferred_element_type=WIDE)]
    ppermute x43 -> x47, starting transfers between devices: 44.5 us -> 59.5 us  [flipped(): lax.ppermute(value, axis, [(i, i ^ bit) for i in range(lax.axis_size(axis...]
  transfers between devices with their start and end apart: 68 -> 72, of which waited for: 34 -> 27; matrix products, arithmetic and copies ran while one was open for 26% -> 32% of each run, Pallas kernels for 0% -> 0%
where the time goes in v3:
time: 1240 us; the launch traced here: 1230 us
  waiting for transfers between devices  465 us (38%)
  matrix products  261 us (21%)
  other arithmetic  173 us (14%)
  local copies, waits for them, and re-layouts  127 us (10%)
  blocking collectives  109 us (9%)
  starting transfers between devices  81.3 us (7%)
  between operations  17.9 us (1%)
    ppermute x47, waiting for transfers between devices, flipped(): lax.ppermute(value, axis, [(i, i ^ bit) for i in range(lax.axis_size(axis...  174 us
    reduce_scatter x4, waiting for transfers between devices, scattered(): lax.psum_scatter(array.astype(NARROW), 'tp', scatter_dimension=0, tiled=T...  87.9 us
    dot_general x47, matrix products, batched(): return jnp.einsum(spec, left, right, preferred_element_type=WIDE)  86 us
    dot_general x16, matrix products, matmul(): return jnp.dot(left, right, preferred_element_type=WIDE)  74.2 us
    psum x1, waiting for transfers between devices, remember_back(): one.grad_mixing = lax.psum(grad_mixing, 'tp')  71.6 us
    ppermute x47, starting transfers between devices, flipped(): lax.ppermute(value, axis, [(i, i ^ bit) for i in range(lax.axis_size(axis...  59.5 us
    dot_general x11, matrix products, by_rows(): lax.dot_general(left, right, (((1,), (1,)), ((), ())), preferred_element_...  59.1 us
    all_gather x1, blocking collectives, on_device(): block_lasts = lax.all_gather(lasts_all, 'ctx', axis=1, tiled=True)  58.2 us
  transfers between devices with their start and end apart: 72, of which 27 were waited for; matrix products, arithmetic and copies ran while one was open for 32% of the time, Pallas kernels for 0%

profile of v3, /device:TPU:1, one launch (start us, length us, event | category | flops | bytes accessed | tf_op | source)
XLA Modules:
  0.0 1234.4 jit_solution(18401537004956823381)
XLA Ops:
  21.3 58.2 %all-gather = f32[2,8,1]{0,2,1:T(1,128)S(1)} all-gather(f32[2,2,1]{0,2,1:T(1,128)S(1)} %copy.463), channel_id=2, replica_groups=mesh['shard'=2,'ctx'=4,'tp'=4] {'ctx'}, dimensions={1}, use_global_device_ids=true | all-gather | bytes 80 | tf_op jit(solution)/shard_map/all_gather | solution.py:153
  126.4 10.8 all-gather.1
  147.3 29.9 %collective-permute-done.5 = bf16[3,768,384]{2,1,0:T(8,128)(2,1)} collective-permute-done((bf16[3,768,384]{2,1,0:T(8,128)(2,1)}, bf16[3,768,384]{2,1,0:T(8,128)(2,1)}, u32[]{:S(2)}, u32[]{:S(2)}) %collective-permute-start.5) | collective-permute-done | bytes 1769504 | tf_op jit(solution)/shard_map/ppermute | solution.py:24
  177.2 51.1 %all-reduce.5.cloned.1.call-done = bf16[2,2,256,1024]{2,3,0,1:T(8,128)(2,1)} async-done(((bf16[2,2,256,1024]{2,3,0,1:T(8,128)(2,1)}), bf16[2,2,256,1024]{2,3,0,1:T(8,128)(2,1)}) %all-reduce.5.cloned.1.call-update) | async-done | bytes 2097168 | tf_op jit(solution)/shard_map/psum | solution.py:246
  243.2 13.7 %collective-permute-done.10 = bf16[2,512,384]{2,1,0:T(8,128)(2,1)S(1)} collective-permute-done((bf16[2,512,384]{2,1,0:T(8,128)(2,1)}, bf16[2,512,384]{2,1,0:T(8,128)(2,1)S(1)}, u32[]{:S(2)}, u32[]{:S(2)}) %collective-permute-start.10) | collective-permute-done | bytes 786464 | tf_op jit(solution)/shard_map/ppermute | solution.py:20
  322.7 16.2 %collective-permute-done.12 = bf16[384,768]{1,0:T(8,128)(2,1)} collective-permute-done((bf16[384,768]{1,0:T(8,128)(2,1)}, bf16[384,768]{1,0:T(8,128)(2,1)}, u32[]{:S(2)}, u32[]{:S(2)}) %collective-permute-start.12) | collective-permute-done | bytes 589856 | tf_op jit(solution)/shard_map/ppermute | solution.py:24
  382.4 53.9 %reduce-scatter.9.cloned.1.call-done = bf16[256,1536]{1,0:T(8,128)(2,1)} async-done(((bf16[1024,1536]{1,0:T(8,128)(2,1)}), bf16[256,1536]{1,0:T(8,128)(2,1)}) %reduce-scatter.9.cloned.1.call-update) | async-done | bytes 786448 | tf_op jit(solution)/shard_map/reduce_scatter | solution.py:138
  449.7 26.7 %collective-permute-done.15 = bf16[768,1024]{1,0:T(8,128)(2,1)} collective-permute-done((bf16[768,1024]{1,0:T(8,128)(2,1)}, bf16[768,1024]{1,0:T(8,128)(2,1)}, u32[]{:S(2)}, u32[]{:S(2)}) %collective-permute-start.15) | collective-permute-done | bytes 1572896 | tf_op jit(solution)/shard_map/ppermute | solution.py:24
  476.3 28.4 %all-gather.15.cloned.1.call-done = bf16[1024,1536]{1,0:T(8,128)(2,1)} async-done(((bf16[256,1536]{1,0:T(8,128)(2,1)}), bf16[1024,1536]{1,0:T(8,128)(2,1)}) %all-gather.15.cloned.1.call-update) | async-done | bytes 3145744 | tf_op jit(solution)/shard_map/all_gather | solution.py:143
  560.0 26.2 %reduce-scatter.11.cloned.1.call-done = bf16[256,1536]{1,0:T(8,128)(2,1)} async-done(((bf16[1024,1536]{1,0:T(8,128)(2,1)}), bf16[256,1536]{1,0:T(8,128)(2,1)}) %reduce-scatter.11.cloned.1.call-update) | async-done | bytes 786448 | tf_op jit(solution)/shard_map/reduce_scatter | solution.py:138
  597.5 10.0 multiply_convert_fusion.1
  607.5 40.2 %collective-permute-done.18 = bf16[2,256,768]{2,1,0:T(8,128)(2,1)S(1)} collective-permute-done((bf16[2,256,768]{2,1,0:T(8,128)(2,1)S(1)}, bf16[2,256,768]{2,1,0:T(8,128)(2,1)S(1)}, u32[]{:S(2)}, u32[]{:S(2)}) %collective-permute-start.18) | collective-permute-done | bytes 786464 | tf_op jit(solution)/shard_map/ppermute | solution.py:24
  678.8 10.8 multiply_reduce_fusion
  689.6 10.7 multiply_convert_fusion
  759.7 17.0 %collective-permute-done.20 = bf16[256,768]{1,0:T(8,128)(2,1)S(1)} collective-permute-done((bf16[256,768]{1,0:T(8,128)(2,1)S(1)}, bf16[256,768]{1,0:T(8,128)(2,1)S(1)}, u32[]{:S(2)}, u32[]{:S(2)}) %collective-permute-start.20) | collective-permute-done | bytes 393248 | tf_op jit(solution)/shard_map/ppermute | solution.py:24
  870.1 11.1 all-gather.4
  886.9 8.6 all-gather.19.cloned.1.call-done
  911.3 71.6 %all-reduce.7.cloned.1.call-done = bf16[2,2,256,1024]{2,3,0,1:T(8,128)(2,1)} async-done(((bf16[2,2,256,1024]{2,3,0,1:T(8,128)(2,1)}), bf16[2,2,256,1024]{2,3,0,1:T(8,128)(2,1)}) %all-reduce.7.cloned.1.call-update) | async-done | bytes 2097168 | tf_op jit(solution)/shard_map/psum | solution.py:478
  1008.4 9.7 fusion.50
  1048.5 17.5 %add_convert_fusion = bf16[1024,1536]{1,0:T(8,128)(2,1)} fusion(f32[1024,1536]{1,0:T(8,128)} %fusion.220, f32[1024,1536]{1,0:T(8,128)} %fusion.331, f32[1024,1536]{1,0:T(8,128)} %fusion.309, f32[1024,1536]{1,0:T(8,128)} %fusion.330, bf16[1024,1536]{1,0:T(8,128)(2,1)} %fusion.14, bf16[768,1536]{1,0:T(8,128)(2,1)} %copy-done.103, ...), kind=kOutput, calls=%fused_computation.48 | convolution fusion | flops 4849139712 | bytes 36175872 | tf_op jit(solution)/shard_map/dot_general | solution.py:64
  1102.5 17.7 %all-gather.5 = f32[4,1,26112]{2,1,0:T(1,128)S(1)} all-gather(f32[1,1,26112]{2,1,0:T(1,128)S(1)} %reshape.1036), channel_id=4, replica_groups=mesh['shard'=2,'ctx'=4,'tp'=4] {'tp'}, dimensions={0}, use_global_device_ids=true | all-gather | bytes 522240 | tf_op jit(solution)/shard_map/all_gather | solution.py:739
  1157.4 13.8 %collective-permute-done.46 = f32[1536]{0:T(1024)S(1)} collective-permute-done((f32[1536]{0:T(1024)S(1)}, f32[1536]{0:T(1024)S(1)}, u32[]{:S(2)}, u32[]{:S(2)}) %collective-permute-start.46) | collective-permute-done | bytes 6176 | tf_op jit(solution)/shard_map/ppermute | solution.py:24
  1171.2 11.5 all-gather.6
  1198.9 12.0 collective-permute-done.55
  (984 shorter events, 639.1 us)
Async XLA Ops:
  7.2 221.1 %all-reduce.5.cloned.1.call-start = ((), (), s32[]{:S(2)}) async-start(), calls=%async_computation.6 | async-start | bytes 4194304 | tf_op jit(solution)/shard_map/psum | solution.py:246
  7.3 74.9 %collective-permute-start = (bf16[2,512,1536]{2,1,0:T(8,128)(2,1)}, bf16[2,512,1536]{2,1,0:T(8,128)(2,1)}, u32[]{:S(2)}, u32[]{:S(2)}) collective-permute-start(bf16[2,512,1536]{2,1,0:T(8,128)(2,1)} %param.14), channel_id=1, source_target_pairs={{0,8},{4,12},{8,0},{12,4},{1,9},{5,13},{9,1},{13,5},{2,10},{6,14},... | collective-permute-start | bytes 9437192 | tf_op jit(solution)/shard_map/ppermute | solution.py:24
  9.4 83.7 %collective-permute-start.1 = (bf16[2,512,1536]{2,1,0:T(8,128)(2,1)}, bf16[2,512,1536]{2,1,0:T(8,128)(2,1)}, u32[]{:S(2)}, u32[]{:S(2)}) collective-permute-start(bf16[2,512,1536]{2,1,0:T(8,128)(2,1)} %param.14), channel_id=1, source_target_pairs={{0,4},{4,0},{8,12},{12,8},{1,5},{5,1},{9,13},{13,9},{2,6},{6,2},{1... | collective-permute-start | bytes 9437192 | tf_op jit(solution)/shard_map/ppermute | solution.py:24
  15.6 64.7 %collective-permute-start.3 = (bf16[57024]{0:T(1024)(128)(2,1)S(1)}, bf16[57024]{0:T(1024)(128)(2,1)S(1)}, u32[]{:S(2)}, u32[]{:S(2)}) collective-permute-start(bf16[57024]{0:T(1024)(128)(2,1)S(1)} %concatenate.160), channel_id=1, source_target_pairs={{0,16},{16,0},{1,17},{17,1},{2,18},{18,2},{3,19},{19,3},{4,20},{20... | collective-permute-start | bytes 342152 | tf_op jit(solution)/shard_map/ppermute | solution.py:24
  16.9 65.5 %collective-permute-start.4 = (bf16[768,1536]{1,0:T(8,128)(2,1)}, bf16[768,1536]{1,0:T(8,128)(2,1)}, u32[]{:S(2)}, u32[]{:S(2)}) collective-permute-start(bf16[768,1536]{1,0:T(8,128)(2,1)} %param.24), channel_id=1, source_target_pairs={{0,16},{16,0},{1,17},{17,1},{2,18},{18,2},{3,19},{19,3},{4,20},{20... | collective-permute-start | bytes 7077896 | tf_op jit(solution)/shard_map/ppermute | solution.py:24
  17.2 124.1 %collective-permute-start.6 = (bf16[768,384]{1,0:T(8,128)(2,1)}, bf16[768,384]{1,0:T(8,128)(2,1)}, u32[]{:S(2)}, u32[]{:S(2)}) collective-permute-start(bf16[768,384]{1,0:T(8,128)(2,1)} %param.23), channel_id=1, source_target_pairs={{0,16},{16,0},{1,17},{17,1},{2,18},{18,2},{3,19},{19,3},{4,20},{20... | collective-permute-start | bytes 1769480 | tf_op jit(solution)/shard_map/ppermute | solution.py:24
  139.0 208.4 %all-gather.13.cloned.1.call-start = ((), (), s32[]{:S(2)}) async-start(), calls=%async_computation.7 | async-start | bytes 3932160 | tf_op jit(solution)/shard_map/all_gather | solution.py:291
  284.5 151.7 %reduce-scatter.9.cloned.1.call-start = ((), (), s32[]{:S(2)}) async-start(), calls=%async_computation.8 | async-start | bytes 3932160 | tf_op jit(solution)/shard_map/reduce_scatter | solution.py:138
  377.3 127.4 %all-gather.15.cloned.1.call-start = ((), (), s32[]{:S(2)}) async-start(), calls=%async_computation.9 | async-start | bytes 3932160 | tf_op jit(solution)/shard_map/all_gather | solution.py:143
  381.2 56.4 %collective-permute-start.14 = (bf16[768,1024]{1,0:T(8,128)(2,1)}, bf16[768,1024]{1,0:T(8,128)(2,1)S(1)}, u32[]{:S(2)}, u32[]{:S(2)}) collective-permute-start(bf16[768,1024]{1,0:T(8,128)(2,1)} %get-tuple-element.79), channel_id=1, source_target_pairs={{0,16},{16,0},{1,17},{17,1},{2,18},{18,2},{3,19},{19,3},{4,20},{20... | collective-permute-start | bytes 4718600 | tf_op jit(solution)/shard_map/ppermute | solution.py:24
  441.0 145.2 %reduce-scatter.11.cloned.1.call-start = ((), (), s32[]{:S(2)}) async-start(), calls=%async_computation.10 | async-start | bytes 3932160 | tf_op jit(solution)/shard_map/reduce_scatter | solution.py:138
  527.3 127.8 %all-gather.17.cloned.1.call-start = ((), (), s32[]{:S(2)}) async-start(), calls=%async_computation.11 | async-start | bytes 3932160 | tf_op jit(solution)/shard_map/all_gather | solution.py:143
  591.3 131.0 %reduce-scatter.13.cloned.1.call-start = ((), (), s32[]{:S(2)}) async-start(), calls=%async_computation.12 | async-start | bytes 3932160 | tf_op jit(solution)/shard_map/reduce_scatter | solution.py:138
  662.2 126.6 %reduce-scatter.19.cloned.1.call-start = ((), (), s32[]{:S(2)}) async-start(), calls=%async_computation.18 | async-start | bytes 3932160
  729.5 166.1 %all-gather.19.cloned.1.call-start = ((), (), s32[]{:S(2)}) async-start(), calls=%async_computation.13 | async-start | bytes 3932160 | tf_op jit(solution)/shard_map/all_gather | solution.py:143
  825.5 72.9 %collective-permute-start.32 = (bf16[3,2,192,384]{3,2,1,0:T(8,128)(2,1)}, bf16[3,2,192,384]{3,2,1,0:T(8,128)(2,1)}, u32[]{:S(2)}, u32[]{:S(2)}) collective-permute-start(bf16[3,2,192,384]{3,2,1,0:T(8,128)(2,1)} %dynamic-slice_bitcast_fusion.5), channel_id=1, source_target_pairs={{0,16},{16,0},{1,17},{17,1},{2,18},{18,2},{3,19},{19,3},{4,20},{20... | collective-permute-start | bytes 2654216 | tf_op jit(solution)/shard_map/ppermute | solution.py:24
  833.4 149.5 %all-reduce.7.cloned.1.call-start = ((), (), s32[]{:S(2)}) async-start(), calls=%async_computation.14 | async-start | bytes 4194304 | tf_op jit(solution)/shard_map/psum | solution.py:478
  895.5 194.8 %reduce-scatter.17.cloned.1.call-start = ((), (), s32[]{:S(2)}) async-start(), calls=%async_computation.16 | async-start | bytes 491520 | tf_op jit(solution)/shard_map/reduce_scatter | solution.py:701
  997.3 94.0 %collective-permute-start.58 = (bf16[2,256,768]{2,1,0:T(8,128)(2,1)}, bf16[2,256,768]{2,1,0:T(8,128)(2,1)}, u32[]{:S(2)}, u32[]{:S(2)}) collective-permute-start(bf16[2,256,768]{2,1,0:T(8,128)(2,1)} %pad_maximum_fusion.75), channel_id=1, source_target_pairs={{0,4},{4,0},{8,12},{12,8},{1,5},{5,1},{9,13},{13,9},{2,6},{6,2},{1... | collective-permute-start | bytes 2359304 | tf_op jit(solution)/shard_map/ppermute | solution.py:24
  998.3 124.1 %collective-permute-start.57 = (bf16[2,2,192,1024]{3,2,0,1:T(8,128)(2,1)}, bf16[2,2,192,1024]{3,2,0,1:T(8,128)(2,1)}, u32[]{:S(2)}, u32[]{:S(2)}) collective-permute-start(bf16[2,2,192,1024]{3,2,0,1:T(8,128)(2,1)} %pad_maximum_fusion.29), channel_id=1, source_target_pairs={{0,4},{4,0},{8,12},{12,8},{1,5},{5,1},{9,13},{13,9},{2,6},{6,2},{1... | collective-permute-start | bytes 4718600 | tf_op jit(solution)/shard_map/ppermute | solution.py:24
  999.1 88.2 %collective-permute-start.43 = (bf16[2,192,384]{2,1,0:T(8,128)(2,1)}, bf16[2,192,384]{2,1,0:T(8,128)(2,1)}, u32[]{:S(2)}, u32[]{:S(2)}) collective-permute-start(bf16[2,192,384]{2,1,0:T(8,128)(2,1)} %dynamic-slice_bitcast_fusion.12), channel_id=1, source_target_pairs={{0,16},{16,0},{1,17},{17,1},{2,18},{18,2},{3,19},{19,3},{4,20},{20... | collective-permute-start | bytes 884744 | tf_op jit(solution)/shard_map/ppermute | solution.py:24
  1008.0 130.7 %reduce-scatter.15.cloned.1.call-start = ((), (), s32[]{:S(2)}) async-start(), calls=%async_computation.15 | async-start | bytes 3932160 | tf_op jit(solution)/shard_map/reduce_scatter | solution.py:138
  1026.5 61.8 %collective-permute-start.40 = (bf16[3,192,384]{2,1,0:T(8,128)(2,1)}, bf16[3,192,384]{2,1,0:T(8,128)(2,1)}, u32[]{:S(2)}, u32[]{:S(2)}) collective-permute-start(bf16[3,192,384]{2,1,0:T(8,128)(2,1)} %dynamic-slice_bitcast_fusion.10), channel_id=1, source_target_pairs={{0,8},{4,12},{8,0},{12,4},{1,9},{5,13},{9,1},{13,5},{2,10},{6,14},... | collective-permute-start | bytes 1327112 | tf_op jit(solution)/shard_map/ppermute | solution.py:24
  1066.0 154.4 %all-gather.21.cloned.1.call-start = ((), (), s32[]{:S(2)}) async-start(), calls=%async_computation.17 | async-start | bytes 3932160 | tf_op jit(solution)/shard_map/all_gather | solution.py:143
  (269 other events, 4231.1 us)
Sparse Core Ops, SparseCore 0:
  139.1 89.2 all-reduce.4
  284.6 62.6 all-gather.12
  377.4 58.7 reduce-scatter.8
  441.1 63.5 all-gather.14
  527.4 58.8 reduce-scatter.10
  591.4 63.5 all-gather.16
  662.3 58.8 reduce-scatter.12
  729.6 59.1 reduce-scatter.18
  833.5 61.9 all-gather.18
  898.3 84.5 all-reduce.6
  1008.1 18.1 reduce-scatter.16
  1066.1 72.5 reduce-scatter.14
  1150.5 63.0 all-gather.20

commit v4 on v3

--- a/solution.py
+++ b/solution.py
@@ -7,6 +7,7 @@
 SPAN = 256
 LIMIT = 800
 LAGS = (LIMIT + SPAN - 2) // SPAN
+CORNER = LIMIT - (LAGS - 1) * SPAN
 STREAMS = 1
 
 
@@ -104,7 +105,6 @@
 
     pair_tokens = flipped(tokens, "ctx", 1)
     far_tokens = flipped(tokens, "ctx", 2)
-    diagonal_tokens = flipped(far_tokens, "ctx", 1)
     feature_other = flipped(w_feature, "shard", 1)
     smalls = [norm_gain, ffn_gain, memory_gain, memory_rates, persistent]
     small_flat = jnp.concatenate([item.reshape(-1) for item in smalls])
@@ -150,26 +150,26 @@
 
     labels_all = segments.astype(WIDE).reshape(groups, blocks_each, SPAN) + 1.0
     lasts_all = labels_all[:, :, -1]
-    block_lasts = lax.all_gather(lasts_all, "ctx", axis=1, tiled=True)
-    total_blocks = parts * blocks_each
-    first = part * blocks_each
+    late_lasts = after(lasts_all, far_tokens)
+    far_lasts = flipped(late_lasts, "ctx", 2)
+    lasts_around = jnp.stack(
+        [lasts_all, flipped(late_lasts, "ctx", 1), far_lasts, flipped(far_lasts, "ctx", 1)]
+    )
 
     def last_of(index):
-        found = lax.dynamic_index_in_dim(
-            block_lasts, jnp.clip(index, 0, total_blocks - 1), 1, False
-        )
-        return jnp.where(index >= 0, found, 0.0)
-
-    before_all = jnp.stack([last_of(first + own - 1) for own in range(blocks_each)], axis=1)
+        delta, place = divmod(index, blocks_each)
+        source = part + delta
+        found = pick(lasts_around, jnp.clip(source, 0, parts - 1) ^ part, 0)[:, place]
+        return jnp.where(source >= 0, found, 0.0)
+
+    before_all = jnp.stack([last_of(own - 1) for own in range(blocks_each)], axis=1)
     linked_all = []
     for own in range(blocks_each):
-        links = []
-        for lag in range(LAGS - 1, -1, -1):
-            source = first + own - 1 - lag
-            link = (source >= 0) & (last_of(source) == last_of(first + own - 1))
-            links.append(jnp.broadcast_to(link[:, None, None], (groups, 1, SPAN)))
-        linked_all.append(jnp.concatenate(links, axis=2))
-    linked_all = jnp.stack(linked_all, axis=1)
+        for lag in range(LAGS):
+            source = own - 1 - lag
+            present = part + source // blocks_each >= 0
+            linked_all.append(present & (last_of(source) == last_of(own - 1)))
+    linked_all = jnp.stack(linked_all, axis=1).reshape(groups, blocks_each, LAGS)
 
     def place_of(own, lag):
         return divmod(own - 1 - lag, blocks_each)
@@ -187,6 +187,26 @@
 
     class Stream:
         pass
+
+    def linked(one, square, corner):
+        spread = jnp.repeat(one.linked[:, :, LAGS - 2 :: -1], SPAN, axis=2)[:, :, None]
+        square = jnp.where(spread, square, jnp.zeros_like(square))
+        corner = jnp.where(
+            one.linked[:, :, LAGS - 1, None, None], corner, jnp.zeros_like(corner)
+        )
+        return square, corner
+
+    def packed(square, corner):
+        wide = square.shape[-1]
+        lanes = corner.transpose(2, 0, 1, 3).reshape(CORNER, -1)
+        lanes = jnp.pad(lanes, ((0, 0), (0, wide - lanes.shape[1])))
+        return jnp.concatenate([square.reshape(-1, wide), lanes], axis=0)
+
+    def unpacked(array):
+        square = array[:-CORNER].reshape(count, blocks_each, SPAN, -1)
+        corner = array[-CORNER:, : blocks * CORNER]
+        corner = corner.reshape(CORNER, count, blocks_each, CORNER).transpose(1, 2, 0, 3)
+        return square, corner
 
     def begin(one, index):
         def mine(array):
@@ -212,10 +232,13 @@
         low, one.preact = features_of(mine(tokens))
         one.input_low = low.reshape(rows, width)
         one.features = jax.nn.silu(one.preact).astype(NARROW)
-        far, pair, diagonal, one.features = lax.optimization_barrier(
-            (mine(far_tokens), mine(pair_tokens), mine(diagonal_tokens), one.features)
-        )
-        close = [pair, diagonal]
+        squares = jnp.sum(jnp.square(one.features.astype(WIDE)), axis=1)
+        squares = jnp.sum(lax.all_gather(squares, "tp", axis=0), axis=0)
+        one.key_scale = lax.rsqrt(squares + EPSILON)
+        far, pair, one.features, one.key_scale = lax.optimization_barrier(
+            (mine(far_tokens), mine(pair_tokens), one.features, one.key_scale)
+        )
+        close = [pair, flipped(far, "ctx", 1)]
         one.around = {0: shaped(one.features)}
         for delta, piece in (
             (-1, jnp.where(odd_part, close[0], close[1])),
@@ -224,33 +247,38 @@
         ):
             one.around[delta] = shaped(jax.nn.silu(features_of(piece)[1]).astype(NARROW))
         one.around[-2] = one.around[2]
-        squares = jnp.sum(jnp.square(one.features.astype(WIDE)), axis=1)
-        squares = jnp.sum(lax.all_gather(squares, "tp", axis=0), axis=0)
-        one.key_scale = lax.rsqrt(squares + EPSILON)
         one.targets = matmul(one.input_low, value_cols).reshape(
             count, blocks_each, SPAN, local_width
         )
         weighted = [(one.around[0].astype(WIDE) * decay).astype(NARROW) for decay in decays]
         products = []
+        corners = []
         for own in range(blocks_each):
             row = []
             for lag in range(LAGS - 1, -1, -1):
                 delta, place = place_of(own, lag)
-                row.append(
-                    batched("sth,suh->stu", weighted[lag][:, own], one.around[delta][:, place])
-                )
+                near, past = weighted[lag][:, own], one.around[delta][:, place]
+                if lag == LAGS - 1:
+                    near, past = near[:, :CORNER], past[:, SPAN - CORNER :]
+                    corners.append(batched("sth,suh->stu", near, past))
+                else:
+                    row.append(batched("sth,suh->stu", near, past))
             products.append(jnp.concatenate(row, axis=2))
-        products = jnp.stack(products, axis=1).astype(NARROW)
-        products, one.key_scale = lax.optimization_barrier((products, one.key_scale))
-        one.products = products
-        one.mixing = lax.psum(products, "tp")
+        one.products = packed(
+            jnp.stack(products, axis=1).astype(NARROW), jnp.stack(corners, axis=1).astype(NARROW)
+        )
+        one.mixing = lax.psum(one.products, "tp")
 
     def span_of(own):
         start = (reach * blocks_each - LAGS + own) * SPAN
         return slice(start, start + LAGS * SPAN)
 
     def remember(one):
-        one.mixing = jnp.where(one.linked, one.mixing, jnp.zeros_like(one.mixing))
+        square, corner = linked(one, *unpacked(one.mixing))
+        corner = jnp.pad(
+            corner, ((0, 0), (0, 0), (0, SPAN - CORNER), (SPAN - CORNER, 0))
+        )
+        one.mixing = jnp.concatenate([corner, square], axis=3)
         one.scales = one.key_scale.reshape(count, blocks_each, SPAN, 1)
         halos = [
             jnp.zeros((count, blocks_each * SPAN, local_width), NARROW) for _ in range(reach)
@@ -471,53 +499,70 @@
             grad_mixing.append(
                 -step * batched("std,sud->stu", raws[own], one.known[:, span_of(own)])
             )
-        grad_mixing = jnp.where(one.linked, jnp.stack(grad_mixing, 1), 0.0).astype(NARROW)
-        grad_mixing, one.scale_sum, one.output = lax.optimization_barrier(
-            (grad_mixing, one.scale_sum, one.output)
+        grad_mixing = jnp.stack(grad_mixing, 1)
+        square, corner = linked(
+            one, grad_mixing[..., SPAN:], grad_mixing[:, :, :CORNER, SPAN - CORNER : SPAN]
+        )
+        grad_mixing, one.output = lax.optimization_barrier(
+            (packed(square.astype(NARROW), corner.astype(NARROW)), one.output)
         )
         one.grad_mixing = lax.psum(grad_mixing, "tp")
 
     def features_back(one):
+        square, corner = unpacked(one.grad_mixing)
+
         def column(own, lag):
-            start = (LAGS - 1 - lag) * SPAN
-            return one.grad_mixing[:, own, :, start : start + SPAN]
+            if lag == LAGS - 1:
+                return corner[:, own]
+            start = (LAGS - 2 - lag) * SPAN
+            return square[:, own, :, start : start + SPAN]
 
         needed = {}
         for hop in range(1, reach + 1):
-            pairs = [
-                (own, lag)
-                for own in range(blocks_each)
-                for lag in range(LAGS)
-                if place_of(own, lag)[0] == -hop
-            ]
-            moved = passed_along(
-                jnp.stack([column(own, lag) for own, lag in pairs], axis=1),
-                "ctx",
-                [(source, source - hop) for source in range(hop, parts)],
-            )
-            for place, (own, lag) in enumerate(pairs):
-                needed[(hop * blocks_each + own, lag)] = moved[:, place]
+            sends = [(source, source - hop) for source in range(hop, parts)]
+            for last_lag in (False, True):
+                pairs = [
+                    (own, lag)
+                    for own in range(blocks_each)
+                    for lag in range(LAGS)
+                    if place_of(own, lag)[0] == -hop and (lag == LAGS - 1) == last_lag
+                ]
+                if not pairs:
+                    continue
+                moved = passed_along(
+                    jnp.stack([column(own, lag) for own, lag in pairs], axis=1), "ctx", sends
+                )
+                for place, (own, lag) in enumerate(pairs):
+                    needed[(hop * blocks_each + own, lag)] = moved[:, place]
         for own in range(blocks_each):
             for lag in range(LAGS):
                 needed[(own, lag)] = column(own, lag)
         grad_features = []
         one.grad_decays = [0.0] * LAGS
+        rest = SPAN - CORNER
         for own in range(blocks_each):
             total = 0.0
-            own_features = one.around[0][:, own].astype(WIDE)
             for lag in range(LAGS):
+                own_features = one.around[0][:, own].astype(WIDE)
                 delta, place = place_of(own, lag)
-                from_reads = batched(
-                    "stu,suh->sth", needed[(own, lag)], one.around[delta][:, place]
-                )
+                past = one.around[delta][:, place]
+                later = own + 1 + lag
+                delta, place = divmod(later, blocks_each)
+                future = one.around[delta][:, place]
+                if lag == LAGS - 1:
+                    own_features, past, future = (
+                        own_features[:, :CORNER],
+                        past[:, rest:],
+                        future[:, :CORNER],
+                    )
+                from_reads = batched("stu,suh->sth", needed[(own, lag)], past)
                 one.grad_decays[lag] = one.grad_decays[lag] + jnp.sum(
                     own_features * from_reads, axis=(0, 1)
                 )
-                later = own + 1 + lag
-                delta, place = divmod(later, blocks_each)
-                from_writes = batched(
-                    "stu,sth->suh", needed[(later, lag)], one.around[delta][:, place]
-                )
+                from_writes = batched("stu,sth->suh", needed[(later, lag)], future)
+                if lag == LAGS - 1:
+                    from_reads = jnp.pad(from_reads, ((0, 0), (0, rest), (0, 0)))
+                    from_writes = jnp.pad(from_writes, ((0, 0), (rest, 0), (0, 0)))
                 total = total + decays[lag] * (from_reads + from_writes)
             grad_features.append(total)
         grad_features = jnp.stack(grad_features, 1).reshape(rows, local_units)
@@ -704,7 +749,7 @@
         item.together()
     for item in mix_reductions:
         item.across()
-    tied(["grad_mixing"], *feed_reductions, *mix_reductions, target_reduction)
+    tied(["grad_mixing", "scale_sum"], *feed_reductions, *mix_reductions, target_reduction)
     every(features_back)
     every(inputs_back)
 

time: 1240 us -> 1220 us (0.984)
  blocking collectives: 109 us -> 50.7 us
  local copies, waits for them, and re-layouts: 127 us -> 149 us
  other arithmetic: 173 us -> 187 us
    all_gather x1 -> x0, blocking collectives: 58.2 us -> none  [on_device(): block_lasts = lax.all_gather(lasts_all, 'ctx', axis=1, tiled=True)]
    psum x1, waiting for transfers between devices: 71.6 us -> 44.7 us  [remember_back(): one.grad_mixing = lax.psum(grad_mixing, 'tp')]
    ppermute x47 -> x50, waiting for transfers between devices: 174 us -> 195 us  [flipped(): lax.ppermute(value, axis, [(i, i ^ bit) for i in range(lax.axis_size(axis...]
    psum x1, waiting for transfers between devices: 51.1 us -> 66.3 us  [begin(): one.mixing = lax.psum(one.products, 'tp')]
    unnamed x460 -> x491, local copies, waits for them, and re-layouts: 41.4 us -> 48.9 us
    ppermute x47 -> x50, starting transfers between devices: 59.5 us -> 59.9 us  [flipped(): lax.ppermute(value, axis, [(i, i ^ bit) for i in range(lax.axis_size(axis...]
  transfers between devices with their start and end apart: 72 -> 76, of which waited for: 27 -> 26; matrix products, arithmetic and copies ran while one was open for 32% -> 36% of each run, Pallas kernels for 0% -> 0%
where the time goes in v4:
time: 1220 us; the launch traced here: 1210 us
  waiting for transfers between devices  455 us (37%)
  matrix products  269 us (22%)
  other arithmetic  187 us (15%)
  local copies, waits for them, and re-layouts  149 us (12%)
  starting transfers between devices  82.8 us (7%)
  blocking collectives  50.7 us (4%)
  between operations  17.8 us (1%)
    ppermute x50, waiting for transfers between devices, flipped(): lax.ppermute(value, axis, [(i, i ^ bit) for i in range(lax.axis_size(axis...  195 us
    dot_general x47, matrix products, batched(): return jnp.einsum(spec, left, right, preferred_element_type=WIDE)  95.5 us
    reduce_scatter x4, waiting for transfers between devices, scattered(): lax.psum_scatter(array.astype(NARROW), 'tp', scatter_dimension=0, tiled=T...  89.1 us
    dot_general x16, matrix products, matmul(): return jnp.dot(left, right, preferred_element_type=WIDE)  73.6 us
    psum x1, waiting for transfers between devices, begin(): one.mixing = lax.psum(one.products, 'tp')  66.3 us
    ppermute x50, starting transfers between devices, flipped(): lax.ppermute(value, axis, [(i, i ^ bit) for i in range(lax.axis_size(axis...  59.9 us
    dot_general x11, matrix products, by_rows(): lax.dot_general(left, right, (((1,), (1,)), ((), ())), preferred_element_...  59.2 us
    unnamed x491, local copies, waits for them, and re-layouts  48.9 us
  transfers between devices with their start and end apart: 76, of which 26 were waited for; matrix products, arithmetic and copies ran while one was open for 36% of the time, Pallas kernels for 0%

profile of v4, /device:TPU:1, one launch (start us, length us, event | category | flops | bytes accessed | tf_op | source)
XLA Modules:
  0.0 1212.6 jit_solution(13623795219073797338)
XLA Ops:
  23.7 47.4 %collective-permute-done.6 = bf16[768,1536]{1,0:T(8,128)(2,1)} collective-permute-done((bf16[768,1536]{1,0:T(8,128)(2,1)}, bf16[768,1536]{1,0:T(8,128)(2,1)}, u32[]{:S(2)}, u32[]{:S(2)}) %collective-permute-start.6) | collective-permute-done | bytes 2359328 | tf_op jit(solution)/shard_map/ppermute | solution.py:25
  73.1 7.6 multiply_reduce_fusion.1
  80.7 10.5 all-gather
  148.1 66.3 %all-reduce.12.cloned.1.call-done = bf16[1056,768]{1,0:T(8,128)(2,1)} async-done(((bf16[1056,768]{1,0:T(8,128)(2,1)}), bf16[1056,768]{1,0:T(8,128)(2,1)}) %all-reduce.12.cloned.1.call-update) | async-done | bytes 1622032 | tf_op jit(solution)/shard_map/psum | solution.py:270
  234.1 11.0 collective-permute-done.13
  311.5 17.3 %collective-permute-done.15 = bf16[384,768]{1,0:T(8,128)(2,1)} collective-permute-done((bf16[384,768]{1,0:T(8,128)(2,1)}, bf16[384,768]{1,0:T(8,128)(2,1)}, u32[]{:S(2)}, u32[]{:S(2)}) %collective-permute-start.15) | collective-permute-done | bytes 589856 | tf_op jit(solution)/shard_map/ppermute | solution.py:25
  328.8 9.1 all-gather.12.cloned.1.call-done
  372.9 53.9 %reduce-scatter.9.cloned.1.call-done = bf16[256,1536]{1,0:T(8,128)(2,1)} async-done(((bf16[1024,1536]{1,0:T(8,128)(2,1)}), bf16[256,1536]{1,0:T(8,128)(2,1)}) %reduce-scatter.9.cloned.1.call-update) | async-done | bytes 786448 | tf_op jit(solution)/shard_map/reduce_scatter | solution.py:138
  440.4 26.5 %collective-permute-done.18 = bf16[768,1024]{1,0:T(8,128)(2,1)} collective-permute-done((bf16[768,1024]{1,0:T(8,128)(2,1)}, bf16[768,1024]{1,0:T(8,128)(2,1)}, u32[]{:S(2)}, u32[]{:S(2)}) %collective-permute-start.18) | collective-permute-done | bytes 1572896 | tf_op jit(solution)/shard_map/ppermute | solution.py:25
  466.9 28.4 %all-gather.14.cloned.1.call-done = bf16[1024,1536]{1,0:T(8,128)(2,1)} async-done(((bf16[256,1536]{1,0:T(8,128)(2,1)}), bf16[1024,1536]{1,0:T(8,128)(2,1)}) %all-gather.14.cloned.1.call-update) | async-done | bytes 3145744 | tf_op jit(solution)/shard_map/all_gather | solution.py:143
  552.3 24.5 %reduce-scatter.11.cloned.1.call-done = bf16[256,1536]{1,0:T(8,128)(2,1)} async-done(((bf16[1024,1536]{1,0:T(8,128)(2,1)}), bf16[256,1536]{1,0:T(8,128)(2,1)}) %reduce-scatter.11.cloned.1.call-update) | async-done | bytes 786448 | tf_op jit(solution)/shard_map/reduce_scatter | solution.py:138
  608.8 34.0 %collective-permute-done.21 = bf16[2,256,768]{2,1,0:T(8,128)(2,1)} collective-permute-done((bf16[2,256,768]{2,1,0:T(8,128)(2,1)}, bf16[2,256,768]{2,1,0:T(8,128)(2,1)}, u32[]{:S(2)}, u32[]{:S(2)}) %collective-permute-start.21) | collective-permute-done | bytes 786464 | tf_op jit(solution)/shard_map/ppermute | solution.py:25
  648.4 7.6 convolution_convert_fusion.2
  665.8 9.7 multiply_reduce_fusion
  675.6 10.7 multiply_convert_fusion
  767.6 13.4 %collective-permute-done.24 = bf16[2,192,1024]{2,1,0:T(8,128)(2,1)S(1)} collective-permute-done((bf16[2,192,1024]{2,1,0:T(8,128)(2,1)}, bf16[2,192,1024]{2,1,0:T(8,128)(2,1)S(1)}, u32[]{:S(2)}, u32[]{:S(2)}) %collective-permute-start.24) | collective-permute-done | bytes 786464 | tf_op jit(solution)/shard_map/ppermute | solution.py:25
  828.7 13.5 %collective-permute-done.34 = bf16[2,96,768]{2,1,0:T(8,128)(2,1)} collective-permute-done((bf16[2,96,768]{2,1,0:T(8,128)(2,1)}, bf16[2,96,768]{2,1,0:T(8,128)(2,1)}, u32[]{:S(2)}, u32[]{:S(2)}) %collective-permute-start.34) | collective-permute-done | bytes 294944 | tf_op jit(solution)/shard_map/ppermute | solution.py:25
  891.7 10.8 all-gather.3
  910.5 44.7 %all-reduce.14.cloned.1.call-done = bf16[1056,768]{1,0:T(8,128)(2,1)} async-done(((bf16[1056,768]{1,0:T(8,128)(2,1)}), bf16[1056,768]{1,0:T(8,128)(2,1)}) %all-reduce.14.cloned.1.call-update) | async-done | bytes 1622032 | tf_op jit(solution)/shard_map/psum | solution.py:509
  1035.7 17.5 %add_convert_fusion = bf16[1024,1536]{1,0:T(8,128)(2,1)} fusion(f32[1024,1536]{1,0:T(8,128)} %fusion.214, f32[1024,1536]{1,0:T(8,128)} %fusion.332, f32[1024,1536]{1,0:T(8,128)} %fusion.312, f32[1024,1536]{1,0:T(8,128)} %fusion.331, bf16[1024,1536]{1,0:T(8,128)(2,1)} %fusion.19, bf16[768,1536]{1,0:T(8,128)(2,1)} %copy-done.113, ...), kind=kOutput, calls=%fused_computation.45 | convolution fusion | flops 4849139712 | bytes 36175872 | tf_op jit(solution)/shard_map/dot_general | solution.py:65
  1082.7 17.5 %all-gather.4 = f32[4,1,26112]{2,1,0:T(1,128)S(1)} all-gather(f32[1,1,26112]{2,1,0:T(1,128)S(1)} %reshape.921), channel_id=3, replica_groups=mesh['shard'=2,'ctx'=4,'tp'=4] {'tp'}, dimensions={0}, use_global_device_ids=true | all-gather | bytes 522240 | tf_op jit(solution)/shard_map/all_gather | solution.py:784
  1135.5 13.8 %collective-permute-done.50 = f32[1536]{0:T(1024)S(1)} collective-permute-done((f32[1536]{0:T(1024)S(1)}, f32[1536]{0:T(1024)S(1)}, u32[]{:S(2)}, u32[]{:S(2)}) %collective-permute-start.50) | collective-permute-done | bytes 6176 | tf_op jit(solution)/shard_map/ppermute | solution.py:25
  1149.3 11.9 all-gather.5
  1177.1 12.0 collective-permute-done.59
  (1040 shorter events, 675.2 us)
Async XLA Ops:
  7.2 207.2 %all-reduce.12.cloned.1.call-start = ((), (), s32[]{:S(2)}) async-start(), calls=%async_computation.6 | async-start | bytes 3244032 | tf_op jit(solution)/shard_map/psum | solution.py:270
  7.3 84.0 %collective-permute-start = (bf16[2,512,1536]{2,1,0:T(8,128)(2,1)}, bf16[2,512,1536]{2,1,0:T(8,128)(2,1)}, u32[]{:S(2)}, u32[]{:S(2)}) collective-permute-start(bf16[2,512,1536]{2,1,0:T(8,128)(2,1)} %param.14), channel_id=1, source_target_pairs={{0,8},{4,12},{8,0},{12,4},{1,9},{5,13},{9,1},{13,5},{2,10},{6,14},... | collective-permute-start | bytes 9437192 | tf_op jit(solution)/shard_map/ppermute | solution.py:25
  9.4 81.9 %collective-permute-start.4 = (bf16[2,512,1536]{2,1,0:T(8,128)(2,1)}, bf16[2,512,1536]{2,1,0:T(8,128)(2,1)}, u32[]{:S(2)}, u32[]{:S(2)}) collective-permute-start(bf16[2,512,1536]{2,1,0:T(8,128)(2,1)} %param.14), channel_id=1, source_target_pairs={{0,4},{4,0},{8,12},{12,8},{1,5},{5,1},{9,13},{13,9},{2,6},{6,2},{1... | collective-permute-start | bytes 9437192 | tf_op jit(solution)/shard_map/ppermute | solution.py:25
  16.9 54.2 %collective-permute-start.6 = (bf16[768,1536]{1,0:T(8,128)(2,1)}, bf16[768,1536]{1,0:T(8,128)(2,1)}, u32[]{:S(2)}, u32[]{:S(2)}) collective-permute-start(bf16[768,1536]{1,0:T(8,128)(2,1)} %param.24), channel_id=1, source_target_pairs={{0,16},{16,0},{1,17},{17,1},{2,18},{18,2},{3,19},{19,3},{4,20},{20... | collective-permute-start | bytes 7077896 | tf_op jit(solution)/shard_map/ppermute | solution.py:25
  17.2 78.4 %collective-permute-start.9 = (bf16[768,384]{1,0:T(8,128)(2,1)}, bf16[768,384]{1,0:T(8,128)(2,1)}, u32[]{:S(2)}, u32[]{:S(2)}) collective-permute-start(bf16[768,384]{1,0:T(8,128)(2,1)} %param.23), channel_id=1, source_target_pairs={{0,16},{16,0},{1,17},{17,1},{2,18},{18,2},{3,19},{19,3},{4,20},{20... | collective-permute-start | bytes 1769480 | tf_op jit(solution)/shard_map/ppermute | solution.py:25
  143.2 71.3 %collective-permute-start.8 = (bf16[3,768,384]{2,1,0:T(8,128)(2,1)}, bf16[3,768,384]{2,1,0:T(8,128)(2,1)}, u32[]{:S(2)}, u32[]{:S(2)}) collective-permute-start(bf16[3,768,384]{2,1,0:T(8,128)(2,1)} %param.21), channel_id=1, source_target_pairs={{0,16},{16,0},{1,17},{17,1},{2,18},{18,2},{3,19},{19,3},{4,20},{20... | collective-permute-start | bytes 5308424 | tf_op jit(solution)/shard_map/ppermute | solution.py:25
  144.5 193.5 %all-gather.12.cloned.1.call-start = ((), (), s32[]{:S(2)}) async-start(), calls=%async_computation.7 | async-start | bytes 3932160 | tf_op jit(solution)/shard_map/all_gather | solution.py:319
  273.7 153.1 %reduce-scatter.9.cloned.1.call-start = ((), (), s32[]{:S(2)}) async-start(), calls=%async_computation.8 | async-start | bytes 3932160 | tf_op jit(solution)/shard_map/reduce_scatter | solution.py:138
  367.8 127.5 %all-gather.14.cloned.1.call-start = ((), (), s32[]{:S(2)}) async-start(), calls=%async_computation.9 | async-start | bytes 3932160 | tf_op jit(solution)/shard_map/all_gather | solution.py:143
  371.7 56.4 %collective-permute-start.17 = (bf16[768,1024]{1,0:T(8,128)(2,1)}, bf16[768,1024]{1,0:T(8,128)(2,1)S(1)}, u32[]{:S(2)}, u32[]{:S(2)}) collective-permute-start(bf16[768,1024]{1,0:T(8,128)(2,1)} %get-tuple-element.77), channel_id=1, source_target_pairs={{0,16},{16,0},{1,17},{17,1},{2,18},{18,2},{3,19},{19,3},{4,20},{20... | collective-permute-start | bytes 4718600 | tf_op jit(solution)/shard_map/ppermute | solution.py:25
  431.6 145.2 %reduce-scatter.11.cloned.1.call-start = ((), (), s32[]{:S(2)}) async-start(), calls=%async_computation.10 | async-start | bytes 3932160 | tf_op jit(solution)/shard_map/reduce_scatter | solution.py:138
  517.8 130.6 %all-gather.16.cloned.1.call-start = ((), (), s32[]{:S(2)}) async-start(), calls=%async_computation.11 | async-start | bytes 3932160 | tf_op jit(solution)/shard_map/all_gather | solution.py:143
  582.6 135.2 %reduce-scatter.13.cloned.1.call-start = ((), (), s32[]{:S(2)}) async-start(), calls=%async_computation.12 | async-start | bytes 3932160 | tf_op jit(solution)/shard_map/reduce_scatter | solution.py:138
  590.7 54.4 %collective-permute-start.22 = (bf16[2,2,192,1024]{3,2,1,0:T(8,128)(2,1)}, bf16[2,2,192,1024]{3,2,1,0:T(8,128)(2,1)}, u32[]{:S(2)}, u32[]{:S(2)}) collective-permute-start(bf16[2,2,192,1024]{3,2,1,0:T(8,128)(2,1)} %dynamic-slice_bitcast_fusion.2), channel_id=1, source_target_pairs={{0,16},{16,0},{1,17},{17,1},{2,18},{18,2},{3,19},{19,3},{4,20},{20... | collective-permute-start | bytes 4718600 | tf_op jit(solution)/shard_map/ppermute | solution.py:25
  656.1 131.7 %reduce-scatter.19.cloned.1.call-start = ((), (), s32[]{:S(2)}) async-start(), calls=%async_computation.18 | async-start | bytes 3932160
  724.9 158.4 %all-gather.18.cloned.1.call-start = ((), (), s32[]{:S(2)}) async-start(), calls=%async_computation.13 | async-start | bytes 3932160 | tf_op jit(solution)/shard_map/all_gather | solution.py:143
  821.2 134.0 %all-reduce.14.cloned.1.call-start = ((), (), s32[]{:S(2)}) async-start(), calls=%async_computation.14 | async-start | bytes 3244032 | tf_op jit(solution)/shard_map/psum | solution.py:509
  883.3 186.9 %reduce-scatter.17.cloned.1.call-start = ((), (), s32[]{:S(2)}) async-start(), calls=%async_computation.16 | async-start | bytes 491520 | tf_op jit(solution)/shard_map/reduce_scatter | solution.py:746
  968.7 103.0 %collective-permute-start.62 = (bf16[2,256,768]{2,1,0:T(8,128)(2,1)}, bf16[2,256,768]{2,1,0:T(8,128)(2,1)}, u32[]{:S(2)}, u32[]{:S(2)}) collective-permute-start(bf16[2,256,768]{2,1,0:T(8,128)(2,1)} %pad_maximum_fusion.75), channel_id=1, source_target_pairs={{0,4},{4,0},{8,12},{12,8},{1,5},{5,1},{9,13},{13,9},{2,6},{6,2},{1... | collective-permute-start | bytes 2359304 | tf_op jit(solution)/shard_map/ppermute | solution.py:25
  970.2 132.1 %collective-permute-start.61 = (bf16[2,2,192,1024]{3,2,0,1:T(8,128)(2,1)}, bf16[2,2,192,1024]{3,2,0,1:T(8,128)(2,1)}, u32[]{:S(2)}, u32[]{:S(2)}) collective-permute-start(bf16[2,2,192,1024]{3,2,0,1:T(8,128)(2,1)} %pad_maximum_fusion.29), channel_id=1, source_target_pairs={{0,4},{4,0},{8,12},{12,8},{1,5},{5,1},{9,13},{13,9},{2,6},{6,2},{1... | collective-permute-start | bytes 4718600 | tf_op jit(solution)/shard_map/ppermute | solution.py:25
  971.0 96.2 %collective-permute-start.47 = (bf16[2,192,384]{2,1,0:T(8,128)(2,1)}, bf16[2,192,384]{2,1,0:T(8,128)(2,1)}, u32[]{:S(2)}, u32[]{:S(2)}) collective-permute-start(bf16[2,192,384]{2,1,0:T(8,128)(2,1)} %dynamic-slice_bitcast_fusion.12), channel_id=1, source_target_pairs={{0,16},{16,0},{1,17},{17,1},{2,18},{18,2},{3,19},{19,3},{4,20},{20... | collective-permute-start | bytes 884744 | tf_op jit(solution)/shard_map/ppermute | solution.py:25
  994.7 122.1 %reduce-scatter.15.cloned.1.call-start = ((), (), s32[]{:S(2)}) async-start(), calls=%async_computation.15 | async-start | bytes 3932160 | tf_op jit(solution)/shard_map/reduce_scatter | solution.py:138
  1010.8 57.5 %collective-permute-start.44 = (bf16[3,192,384]{2,1,0:T(8,128)(2,1)}, bf16[3,192,384]{2,1,0:T(8,128)(2,1)}, u32[]{:S(2)}, u32[]{:S(2)}) collective-permute-start(bf16[3,192,384]{2,1,0:T(8,128)(2,1)} %dynamic-slice_bitcast_fusion.10), channel_id=1, source_target_pairs={{0,8},{4,12},{8,0},{12,4},{1,9},{5,13},{9,1},{13,5},{2,10},{6,14},... | collective-permute-start | bytes 1327112 | tf_op jit(solution)/shard_map/ppermute | solution.py:25
  1053.1 145.4 %all-gather.20.cloned.1.call-start = ((), (), s32[]{:S(2)}) async-start(), calls=%async_computation.17 | async-start | bytes 3932160 | tf_op jit(solution)/shard_map/all_gather | solution.py:143
  (288 other events, 4225.7 us)
Sparse Core Ops, SparseCore 0:
  144.6 69.8 all-reduce.11
  273.8 64.1 all-gather.11
  368.0 58.7 reduce-scatter.8
  431.7 63.5 all-gather.13
  517.9 58.7 reduce-scatter.10
  582.7 63.6 all-gather.15
  656.2 61.5 reduce-scatter.12
  725.0 60.3 reduce-scatter.18
  821.3 61.9 all-gather.17
  886.1 69.1 all-reduce.13
  994.8 19.0 reduce-scatter.16
  1053.3 63.5 reduce-scatter.14
  1128.6 62.9 all-gather.19

commit v5 on v4

--- a/solution.py
+++ b/solution.py
@@ -8,7 +8,7 @@
 LIMIT = 800
 LAGS = (LIMIT + SPAN - 2) // SPAN
 CORNER = LIMIT - (LAGS - 1) * SPAN
-STREAMS = 1
+STREAMS = 2
 
 
 EPSILON = 1e-06
@@ -105,7 +105,12 @@
 
     pair_tokens = flipped(tokens, "ctx", 1)
     far_tokens = flipped(tokens, "ctx", 2)
-    feature_other = flipped(w_feature, "shard", 1)
+    core, outer = (part % 2, part // 2)
+    feature_half = pick(w_feature.reshape(2, -1, w_feature.shape[1]), core, 0)
+    feature_half = flipped(feature_half, "shard", 1)
+    feature_other = jnp.concatenate(
+        either(core == 0, feature_half, flipped(feature_half, "ctx", 1)), axis=0
+    )
     smalls = [norm_gain, ffn_gain, memory_gain, memory_rates, persistent]
     small_flat = jnp.concatenate([item.reshape(-1) for item in smalls])
     small_other = flipped(small_flat, "shard", 1)
@@ -114,7 +119,7 @@
     for item in smalls:
         small_others.append(small_other[start : start + item.size].reshape(item.shape))
         start += item.size
-    value_other = flipped(w_value, "shard", 1)
+    value_other = flipped(after(w_value, feature_half), "shard", 1)
 
     gain_in_wide = joined(norm_gain, small_others[0], 0).astype(WIDE)
     gain_ffn_wide = joined(ffn_gain, small_others[1], 0).astype(WIDE)
@@ -124,11 +129,6 @@
     feature_cols = joined(w_feature, feature_other, 0)
     value_cols = joined(w_value, value_other, 0)
     weights = {}
-
-    def fetch(name, array, start):
-        weights[name] = flipped(after(array, start), "shard", 1)
-        return weights[name]
-
     local_width = w_qkv.shape[2]
     local_units = feature_cols.shape[1]
     local_heads = local_width // HD
@@ -141,6 +141,13 @@
 
     def collected(array):
         return lax.all_gather(array.astype(NARROW), "tp", axis=0, tiled=True)
+
+    def summed_over_ranks(array):
+        bit = 1
+        while bit < ranks:
+            array = array + flipped(array, "tp", bit)
+            bit *= 2
+        return array
 
     own_units = lax.dynamic_slice_in_dim(rates.astype(WIDE), rank * local_units, local_units, 1)
     retain, moment = (own_units[0], own_units[1])
@@ -177,12 +184,14 @@
     position = jnp.arange(SPAN)
     causal = position[:, None] >= position[None, :]
 
-    count = groups // STREAMS
+    count = groups
     rows = count * local_len
     blocks = count * blocks_each
-    sub = rows // ranks
+    part_rows = rows // STREAMS
+    part_blocks = blocks // STREAMS
 
     def own_rows(array):
+        sub = array.shape[0] // ranks
         return lax.dynamic_slice_in_dim(array, rank * sub, sub, 0)
 
     class Stream:
@@ -233,8 +242,7 @@
         one.input_low = low.reshape(rows, width)
         one.features = jax.nn.silu(one.preact).astype(NARROW)
         squares = jnp.sum(jnp.square(one.features.astype(WIDE)), axis=1)
-        squares = jnp.sum(lax.all_gather(squares, "tp", axis=0), axis=0)
-        one.key_scale = lax.rsqrt(squares + EPSILON)
+        one.key_scale = lax.rsqrt(summed_over_ranks(squares) + EPSILON)
         far, pair, one.features, one.key_scale = lax.optimization_barrier(
             (mine(far_tokens), mine(pair_tokens), one.features, one.key_scale)
         )
@@ -319,10 +327,10 @@
         one.retrieved_full = lax.all_gather(retrieved, "tp", axis=1, tiled=True)
 
     def heads(values):
-        return values.astype(NARROW).reshape(blocks, SPAN, local_heads, HD)
+        return values.astype(NARROW).reshape(-1, SPAN, local_heads, HD)
 
     def fixed(values):
-        return jnp.broadcast_to(values, (blocks, persist_count, local_heads, HD))
+        return jnp.broadcast_to(values, (part_blocks, persist_count, local_heads, HD))
 
     def scores_of(one):
         raw = batched("bthd,bkhd->bhtk", one.queries, one.keys) * scale
@@ -346,12 +354,12 @@
             ],
             axis=1,
         )
-        label_rows = one.labels.reshape(blocks, SPAN)
-        read_rows = one.reading.reshape(blocks, SPAN)
+        label_rows = one.labels.reshape(part_blocks, SPAN)
+        read_rows = one.reading.reshape(part_blocks, SPAN)
         visible_own = causal[None] & (label_rows[:, :, None] == label_rows[:, None, :])
         visible_memory = visible_own & (read_rows[:, None, :] > 0.5)
         one.visible = jnp.concatenate(
-            [jnp.ones((blocks, SPAN, persist_count), jnp.bool_), visible_memory, visible_own],
+            [jnp.ones((part_blocks, SPAN, persist_count), jnp.bool_), visible_memory, visible_own],
             axis=2,
         )
         scores = scores_of(one)
@@ -363,15 +371,18 @@
         one.attended = (
             batched("bhtk,bkhd->bthd", probs_low, one.values)
             .astype(NARROW)
-            .reshape(rows, local_width)
+            .reshape(part_rows, local_width)
         )
         one.residual = own_rows(one.flat).astype(WIDE)
         one.branch = scattered(matmul(one.attended, weights["out"]))
 
     def middle(one):
+        if one is not streams[0]:
+            one.branch = after(one.branch, streams[0].mid_own)
         one.hidden = one.residual + one.branch
         normed_mid, one.unit_mid, one.factor_mid = norm_rows(one.hidden, gain_ffn_wide)
-        one.mid_low = collected(normed_mid)
+        one.mid_own = normed_mid.astype(NARROW)
+        one.mid_low = collected(one.mid_own)
 
     def feed(one):
         gate = matmul(one.mid_low, weights["gate"])
@@ -385,6 +396,8 @@
         )
 
     def middle_back(one):
+        if one is not streams[0]:
+            one.grad_mid = after(one.grad_mid, streams[0].grad_hidden)
         grad_mid = one.grad_mid
         one.grad_gain_ffn = jnp.sum(grad_mid * one.unit_mid, axis=0)
         upstream = own_rows(one.upstream_low).astype(WIDE)
@@ -394,20 +407,17 @@
         one.grad_mixed = collected(one.grad_hidden)
 
     def branch_out(one):
-        activ, one.grad_mixed = lax.optimization_barrier((one.activ, one.grad_mixed))
+        activ = after(one.activ, whole.grad_retrieved)
         one.branch = scattered(matmul(activ, weights["down"]))
 
     def finish_output(one):
-        hidden, one.grad_retrieved = lax.optimization_barrier(
-            (one.hidden + one.branch, one.grad_retrieved)
-        )
-        one.output = collected(hidden)
+        one.output = collected(after(one.hidden + one.branch, whole.grad_mixing))
 
     def attend_back(one):
         grad_attended = (
             by_rows(one.grad_mixed, weights["out"])
             .astype(NARROW)
-            .reshape(blocks, SPAN, local_heads, HD)
+            .reshape(part_blocks, SPAN, local_heads, HD)
         )
         probs = jnp.exp(scores_of(one) - one.logsum)
         grad_probs = batched("bthd,bkhd->bhtk", grad_attended, one.values)
@@ -418,7 +428,7 @@
         one.grad_queries = (
             (batched("bhtk,bkhd->bthd", grad_scores, one.keys) * scale)
             .astype(NARROW)
-            .reshape(rows, local_width)
+            .reshape(part_rows, local_width)
         )
         grad_keys = batched("bhtk,bthd->bkhd", grad_scores, one.queries) * scale
 
@@ -429,18 +439,18 @@
             memory_part = (
                 grads[:, persist_count : persist_count + SPAN]
                 .astype(NARROW)
-                .reshape(rows, local_width)
+                .reshape(part_rows, local_width)
             )
             token_part = (
-                grads[:, persist_count + SPAN :].astype(NARROW).reshape(rows, local_width)
+                grads[:, persist_count + SPAN :].astype(NARROW).reshape(part_rows, local_width)
             )
             return (fixed_part, memory_part, token_part)
 
         one.key_fixed, one.key_memory, one.key_token = split_keys(grad_keys)
         one.value_fixed, one.value_memory, one.value_token = split_keys(grad_values)
         partial = by_rows(one.key_memory, key_w) + by_rows(one.value_memory, value_w)
-        partial, one.branch = lax.optimization_barrier((partial.astype(NARROW), one.branch))
-        one.grad_retrieved = lax.psum_scatter(partial, "tp", scatter_dimension=1, tiled=True)
+        one.partial = partial.astype(NARROW)
+        one.grad_retrieved = lax.psum_scatter(one.partial, "tp", scatter_dimension=1, tiled=True)
 
     def heads_back(one):
         grad_heads = one.grad_retrieved.astype(WIDE).reshape(rows, local_heads, HD)
@@ -493,7 +503,7 @@
         grad_recalls = jnp.stack(grad_recalls, 1)
         one.grad_targets = (-one.writing * grad_errors).astype(NARROW).reshape(rows, local_width)
         scale_part = jnp.sum(grad_recalls * one.recall + one.errors * grad_errors, axis=3)
-        one.scale_sum = jnp.sum(lax.all_gather(scale_part.reshape(rows), "tp", axis=0), axis=0)
+        one.scale_sum = summed_over_ranks(scale_part.reshape(rows))
         grad_mixing = []
         for own in range(blocks_each):
             grad_mixing.append(
@@ -503,9 +513,11 @@
         square, corner = linked(
             one, grad_mixing[..., SPAN:], grad_mixing[:, :, :CORNER, SPAN - CORNER : SPAN]
         )
-        grad_mixing, one.output = lax.optimization_barrier(
-            (packed(square.astype(NARROW), corner.astype(NARROW)), one.output)
-        )
+        grad_mixing = packed(square.astype(NARROW), corner.astype(NARROW))
+        branches = [item.branch for item in streams]
+        grad_mixing, branches = lax.optimization_barrier((grad_mixing, branches))
+        for item, branch in zip(streams, branches):
+            item.branch = branch
         one.grad_mixing = lax.psum(grad_mixing, "tp")
 
     def features_back(one):
@@ -572,25 +584,27 @@
         one.grad_pre = (grad_features * silu_slope(one.preact)).astype(NARROW)
 
     def inputs_back(one):
-        grad_input = (
+        one.grad_input = (one.early + by_rows(one.grad_pre, feature_cols)).astype(NARROW)
+
+    def input_early(one):
+        one.early = (
             by_rows(one.grad_queries, query_w)
             + by_rows(one.key_token, key_w)
             + by_rows(one.value_token, value_w)
             + by_rows(one.grad_targets, value_cols)
-            + by_rows(one.grad_pre, feature_cols)
-        )
-        one.grad_input = scattered(grad_input)
+        )
 
     def tokens_back(one):
+        if one is not streams[0]:
+            one.grad_input = after(one.grad_input, streams[0].grad_own)
         grad_input = one.grad_input
         _, unit_in, factor_in = norm_rows(one.residual, gain_in_wide)
         one.grad_gain_in = jnp.sum(grad_input * unit_in, axis=0)
-        one.grad_tokens = (
-            collected(one.grad_hidden + norm_back(grad_input, unit_in, factor_in, gain_in_wide))
-            .astype(WIDE)
-            .reshape(count, local_len, width)
-        )
-
+        grad_own = one.grad_hidden + norm_back(grad_input, unit_in, factor_in, gain_in_wide)
+        one.grad_own = grad_own.astype(NARROW)
+        one.grad_tokens = collected(one.grad_own).astype(WIDE).reshape(-1, local_len, width)
+
+    whole = Stream()
     streams = [Stream() for _ in range(STREAMS)]
 
     def over(function):
@@ -602,8 +616,6 @@
     def every(stage):
         for one in streams:
             stage(one)
-
-    core, outer = (part % 2, part // 2)
 
     class Reduction:
         def __init__(self, array, by_row):
@@ -650,12 +662,11 @@
                 return array.reshape(*self.lead, self.high // 2, self.wide)
             return array.reshape(self.high, self.wide // 2)
 
-    def tied(names, *reductions):
-        held = [[getattr(one, name) for name in names] for one in streams]
+    def tied(one, names, *reductions):
+        held = [getattr(one, name) for name in names]
         held, arrays = lax.optimization_barrier((held, [item.array for item in reductions]))
-        for one, values in zip(streams, held):
-            for name, value in zip(names, values):
-                setattr(one, name, value)
+        for name, value in zip(names, held):
+            setattr(one, name, value)
         for item, array in zip(reductions, arrays):
             item.array = array
 
@@ -663,15 +674,18 @@
         def __init__(self, array):
             self.array = array
 
-    def fetched(names, *arrays):
-        holders = [Holder(fetch(str(index), item, start)) for index, (item, start) in enumerate(arrays)]
-        tied(names, *holders)
+    def fetched(one, names, start, *arrays):
+        holders = [Holder(flipped(after(item, start), "shard", 1)) for item in arrays]
+        tied(one, names, *holders)
         return [holder.array for holder in holders]
 
-    for index, one in enumerate(streams):
-        begin(one, index)
-    last = streams[-1]
-    (qkv_other,) = fetched(["mixing"], (w_qkv, last.products))
+    def merged(name):
+        setattr(
+            whole, name, jnp.concatenate([getattr(one, name) for one in streams], axis=0)
+        )
+
+    begin(whole, 0)
+    (qkv_other,) = fetched(whole, ["mixing"], whole.products, w_qkv)
     qkv_cols = joined(w_qkv, qkv_other, 1)
     query_w = qkv_cols[0]
     key_w = qkv_cols[1]
@@ -680,19 +694,25 @@
     fixed_values = (
         matmul(persist, value_w).astype(NARROW).reshape(1, persist_count, local_heads, HD)
     )
-    every(remember)
-    out_other, down_other = fetched(
-        ["retrieved_full"], (w_out, last.recall), (w_down, last.recall)
-    )
+    remember(whole)
+    out_other, down_other = fetched(whole, ["retrieved_full"], whole.recall, w_out, w_down)
     weights["out"] = joined(w_out, out_other, 1)
     weights["down"] = joined(w_down, down_other, 1)
-    every(attend)
-    (gate_other,) = fetched(["branch"], (w_gate_up[0], last.attended))
+    for index, one in enumerate(streams):
+        for name in ("flat", "upstream_low", "input_low", "retrieved_full", "labels", "reading"):
+            array = getattr(whole, name)
+            size = array.shape[0] // STREAMS
+            setattr(one, name, array[index * size : (index + 1) * size])
+        attend(one)
+    first_stream, last_stream = streams[0], streams[-1]
+    (gate_other,) = fetched(last_stream, ["branch"], first_stream.attended, w_gate_up[0])
     weights["gate"] = joined(w_gate_up[0], gate_other, 0)
     every(middle)
-    (up_other,) = fetched(["mid_low"], (w_gate_up[1], last.hidden))
+    (up_other,) = fetched(first_stream, ["mid_low"], first_stream.hidden, w_gate_up[1])
     weights["up"] = joined(w_gate_up[1], up_other, 0)
+    first_stream.mid_low = after(first_stream.mid_low, last_stream.hidden)
     every(feed)
+    first_stream.grad_mid = after(first_stream.grad_mid, last_stream.mid_low)
     feed_reductions = [
         Reduction(over(lambda one: over_rows(one.activ, one.upstream_low)), False),
         Reduction(
@@ -705,25 +725,36 @@
             True,
         ),
     ]
-    tied(["grad_mid"], *feed_reductions)
     every(middle_back)
+    first_stream.grad_mixed = after(first_stream.grad_mixed, last_stream.grad_mid)
     for item in feed_reductions:
         item.across()
-    tied(["grad_mixed"], *feed_reductions)
-    every(branch_out)
-    every(attend_back)
+    attend_back(first_stream)
+    tied(last_stream, ["grad_mixed"], *feed_reductions, Holder(first_stream.partial))
+    attend_back(last_stream)
+    for name in (
+        "grad_retrieved",
+        "grad_queries",
+        "key_token",
+        "value_token",
+        "key_memory",
+        "value_memory",
+    ):
+        merged(name)
     persist_wide = persist.astype(WIDE)
     key_fixed = over(lambda one: one.key_fixed)
     value_fixed = over(lambda one: one.value_fixed)
-    grad_query_w = over(lambda one: over_rows(one.input_low, one.grad_queries))
-    grad_key_w = over(
-        lambda one: over_rows(one.input_low, one.key_token)
-        + over_rows(one.retrieved_full, one.key_memory)
-    ) + exact_product(persist_wide.T, key_fixed)
-    grad_value_proj = over(
-        lambda one: over_rows(one.input_low, one.value_token)
-        + over_rows(one.retrieved_full, one.value_memory)
-    ) + exact_product(persist_wide.T, value_fixed)
+    grad_query_w = over_rows(whole.input_low, whole.grad_queries)
+    grad_key_w = (
+        over_rows(whole.input_low, whole.key_token)
+        + over_rows(whole.retrieved_full, whole.key_memory)
+        + exact_product(persist_wide.T, key_fixed)
+    )
+    grad_value_proj = (
+        over_rows(whole.input_low, whole.value_token)
+        + over_rows(whole.retrieved_full, whole.value_memory)
+        + exact_product(persist_wide.T, value_fixed)
+    )
     mix_reductions = [
         Reduction(over(lambda one: over_rows(one.attended, one.grad_mixed)), False),
         Reduction(
@@ -738,22 +769,34 @@
     )
     for item in feed_reductions:
         item.apart()
-    tied(["grad_retrieved"], *feed_reductions, *mix_reductions)
-    every(finish_output)
-    every(heads_back)
-    every(remember_back)
-    grad_persist = after(grad_persist, last.grad_mixing)
+    tied(whole, ["grad_retrieved"], *feed_reductions, *mix_reductions)
+    every(branch_out)
+    heads_back(whole)
+    remember_back(whole)
+    input_early(whole)
+    grad_persist = after(grad_persist, whole.grad_mixing)
     grad_persist = lax.psum_scatter(grad_persist, "tp", scatter_dimension=0, tiled=True)
-    target_reduction = Reduction(over(lambda one: over_rows(one.input_low, one.grad_targets)), True)
+    target_reduction = Reduction(over_rows(whole.input_low, whole.grad_targets), True)
     for item in feed_reductions:
         item.together()
     for item in mix_reductions:
         item.across()
-    tied(["grad_mixing", "scale_sum"], *feed_reductions, *mix_reductions, target_reduction)
-    every(features_back)
-    every(inputs_back)
-
-    grad_decays = [over(lambda one: one.grad_decays[lag]) for lag in range(LAGS)]
+    tied(
+        whole,
+        ["grad_mixing", "scale_sum", "early"],
+        *feed_reductions,
+        *mix_reductions,
+        target_reduction,
+    )
+    every(finish_output)
+    features_back(whole)
+    inputs_back(whole)
+    outputs = [one.output for one in streams]
+    whole.grad_input, outputs = lax.optimization_barrier((whole.grad_input, outputs))
+    for index, one in enumerate(streams):
+        one.grad_input = scattered(whole.grad_input[index * part_rows : (index + 1) * part_rows])
+
+    grad_decays = whole.grad_decays
     grad_retain = 0.0
     grad_moment = 0.0
     retain_slope = jnp.zeros_like(retain)
@@ -776,29 +819,28 @@
         [
             grad_persist,
             over(lambda one: one.grad_gain_ffn),
-            over(lambda one: one.grad_gain_memory),
+            whole.grad_gain_memory,
             grad_rates,
         ]
     )
     cut = grad_persist.size + width
     spread = Holder(lax.all_gather(small[:cut], "tp", axis=0))
-    feature_reduction = Reduction(over(lambda one: over_rows(one.input_low, one.grad_pre)), True)
+    feature_reduction = Reduction(over_rows(whole.input_low, whole.grad_pre), True)
     late_reductions = [feature_reduction, target_reduction]
     for item in mix_reductions:
         item.apart()
     for item in late_reductions:
         item.across()
-    tied(["grad_input"], spread, *mix_reductions, *late_reductions)
+    tied(last_stream, ["grad_input"], spread, *mix_reductions, *late_reductions)
     every(tokens_back)
     for item in mix_reductions:
         item.together()
     for item in late_reductions:
         item.apart()
         item.together()
-    small_in = lax.all_gather(summed([over(lambda one: one.grad_gain_in)]), "tp", axis=0)
+    gain_in_sum = summed_over_ranks(summed([over(lambda one: one.grad_gain_in)]))
     grad_persist = spread.array[:, : grad_persist.size].reshape(persist_count, width)
     gain_ffn_sum = jnp.sum(spread.array[:, cut - width :], axis=0)
-    gain_in_sum = jnp.sum(small_in, axis=0)
     middle_cut = cut + local_heads * HD
     grad_gain_memory = small[cut:middle_cut].reshape(local_heads, HD)
     grad_rates = small[middle_cut:].reshape(2, local_units)
@@ -811,7 +853,7 @@
         return lax.dynamic_slice_in_dim(array, half_index * size, size, axis)
 
     return (
-        jnp.concatenate([one.output for one in streams], axis=0).reshape(tokens.shape),
+        jnp.concatenate(outputs, axis=0).reshape(tokens.shape),
         jnp.concatenate([one.grad_tokens for one in streams], axis=0),
         own_half(gain_in_sum, 0),
         own_half(gain_ffn_sum, 0),

time: 1220 us -> 1210 us (level)
  blocking collectives: 50.7 us -> 17.7 us
  matrix products: 269 us -> 286 us
  waiting for transfers between devices: 455 us -> 440 us
    reduce_scatter x4 -> x8, waiting for transfers between devices: 89.1 us -> 23.6 us  [scattered(): lax.psum_scatter(array.astype(NARROW), 'tp', scatter_dimension=0, tiled=T...]
    all_gather x3 -> x0, blocking collectives: 33.2 us -> none  [the longest x1 11.9 us: on_device(): lax.all_gather(summed([over(lambda one: one.grad_gain_in)]), 'tp', axis=0)]
    unnamed x14 -> x24, waiting for transfers between devices: 0.22 us -> 19.2 us
    ppermute x50 -> x57, waiting for transfers between devices: 195 us -> 214 us  [flipped(): lax.ppermute(value, axis, [(i, i ^ bit) for i in range(lax.axis_size(axis...]
    dot_general x16 -> x25, matrix products: 73.6 us -> 86.6 us  [matmul(): return jnp.dot(left, right, preferred_element_type=WIDE)]
    ppermute x50 -> x57, starting transfers between devices: 59.9 us -> 66.1 us  [flipped(): lax.ppermute(value, axis, [(i, i ^ bit) for i in range(lax.axis_size(axis...]
    dot_general x47 -> x53, matrix products: 95.5 us -> 89.7 us  [batched(): return jnp.einsum(spec, left, right, preferred_element_type=WIDE)]
    dot_general x11 -> x15, matrix products: 35.2 us -> 40.8 us  [over_rows(): lax.dot_general(left, right, (((0,), (0,)), ((), ())), preferred_element_...]
  transfers between devices with their start and end apart: 76 -> 92, of which waited for: 26 -> 35; matrix products, arithmetic and copies ran while one was open for 36% -> 41% of each run, Pallas kernels for 0% -> 0%
where the time goes in v5:
time: 1210 us; the launch traced here: 1200 us
  waiting for transfers between devices  440 us (36%)
  matrix products  286 us (24%)
  other arithmetic  189 us (16%)
  local copies, waits for them, and re-layouts  158 us (13%)
  starting transfers between devices  90.6 us (7%)
  between operations  19.8 us (2%)
  blocking collectives  17.7 us (1%)
    ppermute x57, waiting for transfers between devices, flipped(): lax.ppermute(value, axis, [(i, i ^ bit) for i in range(lax.axis_size(axis...  214 us
    dot_general x53, matrix products, batched(): return jnp.einsum(spec, left, right, preferred_element_type=WIDE)  89.7 us
    dot_general x25, matrix products, matmul(): return jnp.dot(left, right, preferred_element_type=WIDE)  86.6 us
    ppermute x57, starting transfers between devices, flipped(): lax.ppermute(value, axis, [(i, i ^ bit) for i in range(lax.axis_size(axis...  66.1 us
    psum x1, waiting for transfers between devices, begin(): one.mixing = lax.psum(one.products, 'tp')  64.8 us
    dot_general x17, matrix products, by_rows(): lax.dot_general(left, right, (((1,), (1,)), ((), ())), preferred_element_...  61.3 us
    unnamed x656, local copies, waits for them, and re-layouts  52.4 us
    psum x1, waiting for transfers between devices, remember_back(): one.grad_mixing = lax.psum(grad_mixing, 'tp')  52 us
  transfers between devices with their start and end apart: 92, of which 35 were waited for; matrix products, arithmetic and copies ran while one was open for 41% of the time, Pallas kernels for 0%

profile of v5, /device:TPU:1, one launch (start us, length us, event | category | flops | bytes accessed | tf_op | source)
XLA Modules:
  0.0 1201.5 jit_solution(3481688468096941721)
XLA Ops:
  25.2 21.6 %collective-permute-done.6 = bf16[384,1536]{1,0:T(8,128)(2,1)} collective-permute-done((bf16[384,1536]{1,0:T(8,128)(2,1)}, bf16[384,1536]{1,0:T(8,128)(2,1)}, u32[]{:S(2)}, u32[]{:S(2)}) %collective-permute-start.6) | collective-permute-done | bytes 1179680 | tf_op jit(solution)/shard_map/ppermute | solution.py:25
  53.9 7.6 multiply_reduce_fusion
  67.8 9.6 collective-permute-done
  127.0 64.8 %all-reduce.12.cloned.1.call-done = bf16[1056,768]{1,0:T(8,128)(2,1)} async-done(((bf16[1056,768]{1,0:T(8,128)(2,1)}), bf16[1056,768]{1,0:T(8,128)(2,1)}) %all-reduce.12.cloned.1.call-update) | async-done | bytes 1622032 | tf_op jit(solution)/shard_map/psum | solution.py:278
  212.0 10.9 collective-permute-done.16
  274.6 29.5 %collective-permute-done.18 = bf16[384,768]{1,0:T(8,128)(2,1)} collective-permute-done((bf16[384,768]{1,0:T(8,128)(2,1)}, bf16[384,768]{1,0:T(8,128)(2,1)}, u32[]{:S(2)}, u32[]{:S(2)}) %collective-permute-start.18) | collective-permute-done | bytes 589856 | tf_op jit(solution)/shard_map/ppermute | solution.py:25
  304.1 12.0 all-gather.12.cloned.1.call-done
  391.6 17.1 %reduce-scatter.18.cloned.1.call-done = bf16[128,1536]{1,0:T(8,128)(2,1)} async-done(((bf16[512,1536]{1,0:T(8,128)(2,1)}), bf16[128,1536]{1,0:T(8,128)(2,1)}) %reduce-scatter.18.cloned.1.call-update) | async-done | bytes 393232 | tf_op jit(solution)/shard_map/reduce_scatter | solution.py:138
  415.6 30.1 %collective-permute-done.20 = bf16[768,1024]{1,0:T(8,128)(2,1)} collective-permute-done((bf16[768,1024]{1,0:T(8,128)(2,1)}, bf16[768,1024]{1,0:T(8,128)(2,1)}, u32[]{:S(2)}, u32[]{:S(2)}) %collective-permute-start.20) | collective-permute-done | bytes 1572896 | tf_op jit(solution)/shard_map/ppermute | solution.py:25
  464.9 18.4 %all-gather.16.cloned.1.call-done = bf16[512,1536]{1,0:T(8,128)(2,1)} async-done(((bf16[128,1536]{1,0:T(8,128)(2,1)}), bf16[512,1536]{1,0:T(8,128)(2,1)}) %all-gather.16.cloned.1.call-update) | async-done | bytes 1572880 | tf_op jit(solution)/shard_map/all_gather | solution.py:143
  545.4 9.9 collective-permute-done.23
  560.9 28.1 %collective-permute-done.25 = bf16[2,2,192,1024]{3,2,1,0:T(8,128)(2,1)S(1)} collective-permute-done((bf16[2,2,192,1024]{3,2,1,0:T(8,128)(2,1)}, bf16[2,2,192,1024]{3,2,1,0:T(8,128)(2,1)S(1)}, u32[]{:S(2)}, u32[]{:S(2)}) %collective-permute-start.25) | collective-permute-done | bytes 1572896 | tf_op jit(solution)/shard_map/ppermute | solution.py:25
  613.5 17.4 %all-gather.20.cloned.1.call-done = bf16[512,1536]{1,0:T(8,128)(2,1)} async-done(((bf16[128,1536]{1,0:T(8,128)(2,1)}), bf16[512,1536]{1,0:T(8,128)(2,1)}) %all-gather.20.cloned.1.call-update) | async-done | bytes 1572880 | tf_op jit(solution)/shard_map/all_gather | solution.py:143
  719.0 18.9 %reduce-scatter.34.cloned.1.call-done = bf16[384,512]{1,0:T(8,128)(2,1)} async-done(((bf16[1536,512]{1,0:T(8,128)(2,1)}), bf16[384,512]{1,0:T(8,128)(2,1)}) %reduce-scatter.34.cloned.1.call-update) | async-done | bytes 393232
  846.4 7.8 collective-permute-start.41
  856.0 11.3 add_add_fusion
  869.7 52.0 %all-reduce.14.cloned.1.call-done = bf16[1056,768]{1,0:T(8,128)(2,1)} async-done(((bf16[1056,768]{1,0:T(8,128)(2,1)}), bf16[1056,768]{1,0:T(8,128)(2,1)}) %all-reduce.14.cloned.1.call-update) | async-done | bytes 1622032 | tf_op jit(solution)/shard_map/psum | solution.py:521
  922.0 9.7 multiply_convert_fusion
  995.7 8.1 add_convert_fusion
  1008.1 7.3 convolution_convert_fusion
  1042.0 26.9 %collective-permute-done.46 = f32[29568]{0:T(1024)S(1)} collective-permute-done((f32[29568]{0:T(1024)S(1)}, f32[29568]{0:T(1024)S(1)}, u32[]{:S(2)}, u32[]{:S(2)}) %collective-permute-start.46) | collective-permute-done | bytes 118304 | tf_op jit(solution)/shard_map/ppermute | solution.py:25
  1074.4 17.7 %all-gather.1 = f32[4,1,26112]{2,1,0:T(1,128)S(1)} all-gather(f32[1,1,26112]{2,1,0:T(1,128)S(1)} %reshape.1034), channel_id=2, replica_groups=mesh['shard'=2,'ctx'=4,'tp'=4] {'tp'}, dimensions={0}, use_global_device_ids=true | all-gather | bytes 522240 | tf_op jit(solution)/shard_map/all_gather | solution.py:827
  1150.9 11.7 collective-permute-done.63
  1165.7 13.9 %collective-permute-done.66 = bf16[192,1536]{1,0:T(8,128)(2,1)S(1)} collective-permute-done((bf16[192,1536]{1,0:T(8,128)(2,1)S(1)}, bf16[192,1536]{1,0:T(8,128)(2,1)S(1)}, u32[]{:S(2)}, u32[]{:S(2)}) %collective-permute-start.66) | collective-permute-done | bytes 589856 | tf_op jit(solution)/shard_map/ppermute | solution.py:25
  (1322 shorter events, 719.3 us)
Async XLA Ops:
  7.2 184.6 %all-reduce.12.cloned.1.call-start = ((), (), s32[]{:S(2)}) async-start(), calls=%async_computation.11 | async-start | bytes 3244032 | tf_op jit(solution)/shard_map/psum | solution.py:278
  121.1 70.7 %collective-permute-start.11 = (bf16[3,768,384]{2,1,0:T(8,128)(2,1)}, bf16[3,768,384]{2,1,0:T(8,128)(2,1)S(1)}, u32[]{:S(2)}, u32[]{:S(2)}) collective-permute-start(bf16[3,768,384]{2,1,0:T(8,128)(2,1)} %param.21), channel_id=1, source_target_pairs={{0,16},{16,0},{1,17},{17,1},{2,18},{18,2},{3,19},{19,3},{4,20},{20... | collective-permute-start | bytes 5308424 | tf_op jit(solution)/shard_map/ppermute | solution.py:25
  122.4 193.7 %all-gather.12.cloned.1.call-start = ((), (), s32[]{:S(2)}) async-start(), calls=%async_computation.12 | async-start | bytes 3932160 | tf_op jit(solution)/shard_map/all_gather | solution.py:327
  251.5 126.4 %reduce-scatter.16.cloned.1.call-start = ((), (), s32[]{:S(2)}) async-start(), calls=%async_computation.13 | async-start | bytes 1966080 | tf_op jit(solution)/shard_map/reduce_scatter | solution.py:138
  368.5 77.2 %all-gather.14.cloned.1.call-start = ((), (), s32[]{:S(2)}) async-start(), calls=%async_computation.14 | async-start | bytes 1966080 | tf_op jit(solution)/shard_map/all_gather | solution.py:143
  381.6 101.7 %all-gather.16.cloned.1.call-start = ((), (), s32[]{:S(2)}) async-start(), calls=%async_computation.17 | async-start | bytes 1966080 | tf_op jit(solution)/shard_map/all_gather | solution.py:143
  415.6 115.7 %reduce-scatter.20.cloned.1.call-start = ((), (), s32[]{:S(2)}) async-start(), calls=%async_computation.16 | async-start | bytes 1966080 | tf_op jit(solution)/shard_map/reduce_scatter | solution.py:138
  464.9 91.8 %reduce-scatter.22.cloned.1.call-start = ((), (), s32[]{:S(2)}) async-start(), calls=%async_computation.19 | async-start | bytes 1966080 | tf_op jit(solution)/shard_map/reduce_scatter | solution.py:138
  514.8 78.8 %all-gather.18.cloned.1.call-start = ((), (), s32[]{:S(2)}) async-start(), calls=%async_computation.18 | async-start | bytes 1966080 | tf_op jit(solution)/shard_map/all_gather | solution.py:143
  535.8 95.2 %all-gather.20.cloned.1.call-start = ((), (), s32[]{:S(2)}) async-start(), calls=%async_computation.20 | async-start | bytes 1966080 | tf_op jit(solution)/shard_map/all_gather | solution.py:143
  560.7 157.1 %reduce-scatter.36.cloned.1.call-start = ((), (), s32[]{:S(2)}) async-start(), calls=%async_computation.32 | async-start | bytes 1966080
  666.5 71.4 %reduce-scatter.34.cloned.1.call-start = ((), (), s32[]{:S(2)}) async-start(), calls=%async_computation.31 | async-start | bytes 1966080
  694.7 147.4 %reduce-scatter.24.cloned.1.call-start = ((), (), s32[]{:S(2)}) async-start(), calls=%async_computation.21 | async-start | bytes 1966080 | tf_op jit(solution)/shard_map/reduce_scatter | solution.py:138
  755.0 89.1 %reduce-scatter.26.cloned.1.call-start = ((), (), s32[]{:S(2)}) async-start(), calls=%async_computation.22 | async-start | bytes 1966080 | tf_op jit(solution)/shard_map/reduce_scatter | solution.py:138
  790.0 131.7 %all-reduce.14.cloned.1.call-start = ((), (), s32[]{:S(2)}) async-start(), calls=%async_computation.23 | async-start | bytes 3244032 | tf_op jit(solution)/shard_map/psum | solution.py:521
  845.1 158.7 %all-gather.22.cloned.1.call-start = ((), (), s32[]{:S(2)}) async-start(), calls=%async_computation.24 | async-start | bytes 1966080 | tf_op jit(solution)/shard_map/all_gather | solution.py:143
  921.7 82.1 %all-gather.24.cloned.1.call-start = ((), (), s32[]{:S(2)}) async-start(), calls=%async_computation.25 | async-start | bytes 1966080 | tf_op jit(solution)/shard_map/all_gather | solution.py:143
  938.8 95.1 %reduce-scatter.32.cloned.1.call-start = ((), (), s32[]{:S(2)}) async-start(), calls=%async_computation.29 | async-start | bytes 491520 | tf_op jit(solution)/shard_map/reduce_scatter | solution.py:778
  963.4 129.9 %reduce-scatter.30.cloned.1.call-start = ((), (), s32[]{:S(2)}) async-start(), calls=%async_computation.28 | async-start | bytes 1966080 | tf_op jit(solution)/shard_map/reduce_scatter | solution.py:138
  1007.8 92.0 %reduce-scatter.28.cloned.1.call-start = ((), (), s32[]{:S(2)}) async-start(), calls=%async_computation.26 | async-start | bytes 1966080 | tf_op jit(solution)/shard_map/reduce_scatter | solution.py:138
  1031.2 84.2 %collective-permute-start.68 = (bf16[2,2,192,1024]{3,2,0,1:T(8,128)(2,1)}, bf16[2,2,192,1024]{3,2,0,1:T(8,128)(2,1)}, u32[]{:S(2)}, u32[]{:S(2)}) collective-permute-start(bf16[2,2,192,1024]{3,2,0,1:T(8,128)(2,1)} %pad_maximum_fusion.23), channel_id=1, source_target_pairs={{0,4},{4,0},{8,12},{12,8},{1,5},{5,1},{9,13},{13,9},{2,6},{6,2},{1... | collective-permute-start | bytes 4718600 | tf_op jit(solution)/shard_map/ppermute | solution.py:25
  1032.3 76.7 %collective-permute-start.69 = (bf16[2,256,768]{2,1,0:T(8,128)(2,1)}, bf16[2,256,768]{2,1,0:T(8,128)(2,1)}, u32[]{:S(2)}, u32[]{:S(2)}) collective-permute-start(bf16[2,256,768]{2,1,0:T(8,128)(2,1)} %pad_maximum_fusion.70), channel_id=1, source_target_pairs={{0,4},{4,0},{8,12},{12,8},{1,5},{5,1},{9,13},{13,9},{2,6},{6,2},{1... | collective-permute-start | bytes 2359304 | tf_op jit(solution)/shard_map/ppermute | solution.py:25
  1034.8 154.3 %all-gather.28.cloned.1.call-start = ((), (), s32[]{:S(2)}) async-start(), calls=%async_computation.30 | async-start | bytes 1966080 | tf_op jit(solution)/shard_map/all_gather | solution.py:143
  1108.7 80.5 %all-gather.26.cloned.1.call-start = ((), (), s32[]{:S(2)}) async-start(), calls=%async_computation.27 | async-start | bytes 1966080 | tf_op jit(solution)/shard_map/all_gather | solution.py:143
  (382 other events, 4498.0 us)
Sparse Core Ops, SparseCore 0:
  122.5 69.2 all-reduce.11
  251.6 64.4 all-gather.11
  338.3 33.8 reduce-scatter.15
  374.4 34.2 reduce-scatter.17
  410.1 35.3 all-gather.13
  447.0 36.2 all-gather.15
  485.6 34.3 reduce-scatter.19
  522.3 34.2 reduce-scatter.21
  558.2 35.3 all-gather.17
  595.0 35.8 all-gather.19
  666.6 34.7 reduce-scatter.35
  703.6 34.2 reduce-scatter.33
  755.1 34.2 reduce-scatter.23
  791.6 34.2 reduce-scatter.25
  845.3 76.3 all-reduce.13
  923.1 36.1 all-gather.21
  961.3 35.8 all-gather.23
  999.3 18.2 reduce-scatter.31
  1020.6 35.4 reduce-scatter.29
  1058.8 40.9 reduce-scatter.27
  1108.8 35.7 all-gather.27
  1146.1 35.8 all-gather.25

commit v6 on v5

--- a/solution.py
+++ b/solution.py
@@ -1,10 +1,13 @@
 import jax
 import jax.numpy as jnp
 from jax import lax
+from jax.experimental import pallas as pl
+from jax.experimental.pallas import tpu as pltpu
 from jax.sharding import PartitionSpec as P
 
 HD = 96
 SPAN = 256
+LANES = 128
 LIMIT = 800
 LAGS = (LIMIT + SPAN - 2) // SPAN
 CORNER = LIMIT - (LAGS - 1) * SPAN
@@ -71,6 +74,143 @@
 
 def batched(spec, left, right):
     return jnp.einsum(spec, left, right, preferred_element_type=WIDE)
+
+
+def windows(width):
+    found = []
+    for start in range(0, width, HD):
+        low = start // LANES * LANES
+        high = min(-(-(start + HD) // LANES) * LANES, width)
+        found.append((low, high, start - low))
+    return found
+
+
+def masks_of(label_col, label_row, read_row):
+    rows = lax.broadcasted_iota(jnp.int32, (SPAN, SPAN), 0)
+    columns = lax.broadcasted_iota(jnp.int32, (SPAN, SPAN), 1)
+    own = (rows >= columns) & (label_col == label_row)
+    return own & (read_row > 0.5), own
+
+
+def head_probs(query, keys, visible_memory, visible_own):
+    scale = HD ** (-0.5)
+    scores = [by_rows(query, key) * scale for key in keys]
+    scores[1] = jnp.where(visible_memory, scores[1], MASKED)
+    scores[2] = jnp.where(visible_own, scores[2], MASKED)
+    highest = jnp.max(scores[0], axis=-1, keepdims=True)
+    for item in scores[1:]:
+        highest = jnp.maximum(highest, jnp.max(item, axis=-1, keepdims=True))
+    raised = [jnp.exp(item - highest) for item in scores]
+    totals = sum(jnp.sum(item, axis=-1, keepdims=True) for item in raised)
+    inverse = 1.0 / totals
+    return [item * inverse for item in raised]
+
+
+def attention_kernel(
+    query, key_memory, key_own, value_memory, value_own, key_fixed, value_fixed,
+    label_col, label_row, read_row, out, total,
+):
+    visible_memory, visible_own = masks_of(label_col[0], label_row[0], read_row[0])
+    total[...] = jnp.zeros_like(total)
+    for low, high, offset in windows(query.shape[1]):
+        lanes = lax.broadcasted_iota(jnp.int32, (SPAN, high - low), 1)
+        inside = (lanes >= offset) & (lanes < offset + HD)
+        mine = jnp.where(inside, query[:, low:high], jnp.zeros((), NARROW))
+        keys = [item[:, low:high] for item in (key_fixed, key_memory, key_own)]
+        values = [item[:, low:high] for item in (value_fixed, value_memory, value_own)]
+        probs = head_probs(mine, keys, visible_memory, visible_own)
+        result = sum(matmul(item.astype(NARROW), value) for item, value in zip(probs, values))
+        total[:, low:high] += jnp.where(inside, result, 0.0)
+    out[...] = total[...].astype(NARROW)
+
+
+def attention_back_kernel(
+    query, key_memory, key_own, value_memory, value_own, key_fixed, value_fixed,
+    label_col, label_row, read_row, upstream,
+    grad_query, grad_key_memory, grad_key_own, grad_value_memory, grad_value_own,
+    grad_key_fixed, grad_value_fixed, *totals,
+):
+    scale = HD ** (-0.5)
+    visible_memory, visible_own = masks_of(label_col[0], label_row[0], read_row[0])
+    for total in totals:
+        total[...] = jnp.zeros_like(total)
+
+    @pl.when(pl.program_id(0) == 0)
+    def _():
+        grad_key_fixed[...] = jnp.zeros_like(grad_key_fixed)
+        grad_value_fixed[...] = jnp.zeros_like(grad_value_fixed)
+
+    key_sums = (grad_key_fixed, totals[1], totals[2])
+    value_sums = (grad_value_fixed, totals[3], totals[4])
+    for low, high, offset in windows(query.shape[1]):
+        lanes = lax.broadcasted_iota(jnp.int32, (SPAN, high - low), 1)
+        inside = (lanes >= offset) & (lanes < offset + HD)
+        mine = jnp.where(inside, query[:, low:high], jnp.zeros((), NARROW))
+        above = jnp.where(inside, upstream[:, low:high], jnp.zeros((), NARROW))
+        keys = [item[:, low:high] for item in (key_fixed, key_memory, key_own)]
+        values = [item[:, low:high] for item in (value_fixed, value_memory, value_own)]
+        probs = head_probs(mine, keys, visible_memory, visible_own)
+        grads = [by_rows(above, value) for value in values]
+        inner = sum(
+            jnp.sum(grad * item, axis=-1, keepdims=True) for grad, item in zip(grads, probs)
+        )
+        result = 0.0
+        for index in range(3):
+            slope = (probs[index] * (grads[index] - inner)).astype(NARROW)
+            result = result + matmul(slope, keys[index])
+            key_sums[index][:, low:high] += over_rows(slope, mine) * scale
+            value_sums[index][:, low:high] += over_rows(probs[index].astype(NARROW), above)
+        totals[0][:, low:high] += jnp.where(inside, result, 0.0) * scale
+    places = (grad_query, grad_key_memory, grad_key_own, grad_value_memory, grad_value_own)
+    for place, total in zip(places, totals):
+        place[...] = total[...].astype(NARROW)
+
+
+def attention_specs(blocks, width, fixed_count):
+    rows = pl.BlockSpec((SPAN, width), lambda block: (block, 0))
+    fixed = pl.BlockSpec((fixed_count, width), lambda block: (0, 0))
+    col = pl.BlockSpec((1, SPAN, 1), lambda block: (block, 0, 0))
+    row = pl.BlockSpec((1, 1, SPAN), lambda block: (block, 0, 0))
+    return rows, fixed, [rows] * 5 + [fixed] * 2 + [col, row, row]
+
+
+def attention(*operands):
+    blocks, width, fixed_count = (operands[7].shape[0], operands[0].shape[1], operands[5].shape[0])
+    rows, _, specs = attention_specs(blocks, width, fixed_count)
+    pairs = blocks * SPAN * (2 * SPAN + fixed_count)
+    return pl.pallas_call(
+        attention_kernel,
+        grid=(blocks,),
+        in_specs=specs,
+        out_specs=rows,
+        out_shape=jax.ShapeDtypeStruct((blocks * SPAN, width), NARROW),
+        scratch_shapes=[pltpu.VMEM((SPAN, width), WIDE)],
+        cost_estimate=pl.CostEstimate(
+            flops=16 * pairs * width,
+            bytes_accessed=12 * blocks * SPAN * width,
+            transcendentals=pairs * width // HD,
+        ),
+    )(*operands)
+
+
+def attention_back(*operands):
+    blocks, width, fixed_count = (operands[7].shape[0], operands[0].shape[1], operands[5].shape[0])
+    rows, fixed, specs = attention_specs(blocks, width, fixed_count)
+    pairs = blocks * SPAN * (2 * SPAN + fixed_count)
+    return pl.pallas_call(
+        attention_back_kernel,
+        grid=(blocks,),
+        in_specs=specs + [rows],
+        out_specs=[rows] * 5 + [fixed] * 2,
+        out_shape=[jax.ShapeDtypeStruct((blocks * SPAN, width), NARROW)] * 5
+        + [jax.ShapeDtypeStruct((fixed_count, width), WIDE)] * 2,
+        scratch_shapes=[pltpu.VMEM((SPAN, width), WIDE)] * 5,
+        cost_estimate=pl.CostEstimate(
+            flops=40 * pairs * width,
+            bytes_accessed=24 * blocks * SPAN * width,
+            transcendentals=pairs * width // HD,
+        ),
+    )(*operands)
 
 
 def on_device(
@@ -181,8 +321,14 @@
     def place_of(own, lag):
         return divmod(own - 1 - lag, blocks_each)
 
-    position = jnp.arange(SPAN)
-    causal = position[:, None] >= position[None, :]
+    head_of = (jnp.arange(local_width)[:, None] // HD == jnp.arange(local_heads)).astype(WIDE)
+    gain_flat = gain_mem.reshape(local_width)
+
+    def head_mean(values):
+        return exact_product(values, head_of) / HD
+
+    def head_spread(values):
+        return exact_product(values, head_of.T)
 
     count = groups
     rows = count * local_len
@@ -318,61 +464,31 @@
         one.known = known
         one.recall = jnp.stack(recalls, 1)
         one.errors = jnp.stack(errors, 1)
-        heads_view = (one.reading[..., None] * one.recall).reshape(rows, local_heads, HD)
-        one.head_factor = lax.rsqrt(
-            jnp.mean(heads_view * heads_view, axis=-1, keepdims=True) + EPSILON
-        )
-        one.head_unit = heads_view * one.head_factor
-        retrieved = (one.head_unit * gain_mem).reshape(rows, local_width).astype(NARROW)
+        masked = (one.reading[..., None] * one.recall).reshape(rows, local_width)
+        one.head_factor = head_spread(lax.rsqrt(head_mean(masked * masked) + EPSILON))
+        one.head_unit = masked * one.head_factor
+        retrieved = (one.head_unit * gain_flat).astype(NARROW)
         one.retrieved_full = lax.all_gather(retrieved, "tp", axis=1, tiled=True)
 
-    def heads(values):
-        return values.astype(NARROW).reshape(-1, SPAN, local_heads, HD)
-
-    def fixed(values):
-        return jnp.broadcast_to(values, (part_blocks, persist_count, local_heads, HD))
-
-    def scores_of(one):
-        raw = batched("bthd,bkhd->bhtk", one.queries, one.keys) * scale
-        return jnp.where(one.visible[:, None], raw, MASKED)
-
     def attend(one):
-        one.queries = heads(matmul(one.input_low, query_w))
-        one.keys = jnp.concatenate(
-            [
-                fixed(fixed_keys),
-                heads(matmul(one.retrieved_full, key_w)),
-                heads(matmul(one.input_low, key_w)),
-            ],
-            axis=1,
-        )
-        one.values = jnp.concatenate(
-            [
-                fixed(fixed_values),
-                heads(matmul(one.retrieved_full, value_w)),
-                heads(matmul(one.input_low, value_w)),
-            ],
-            axis=1,
-        )
-        label_rows = one.labels.reshape(part_blocks, SPAN)
-        read_rows = one.reading.reshape(part_blocks, SPAN)
-        visible_own = causal[None] & (label_rows[:, :, None] == label_rows[:, None, :])
-        visible_memory = visible_own & (read_rows[:, None, :] > 0.5)
-        one.visible = jnp.concatenate(
-            [jnp.ones((part_blocks, SPAN, persist_count), jnp.bool_), visible_memory, visible_own],
-            axis=2,
-        )
-        scores = scores_of(one)
-        highest = jnp.max(scores, axis=-1, keepdims=True)
-        raised = jnp.exp(scores - highest)
-        totals = jnp.sum(raised, axis=-1, keepdims=True)
-        one.logsum = highest + jnp.log(totals)
-        probs_low = (raised / totals).astype(NARROW)
-        one.attended = (
-            batched("bhtk,bkhd->bthd", probs_low, one.values)
-            .astype(NARROW)
-            .reshape(part_rows, local_width)
-        )
+        def projected(values, weight):
+            return matmul(values, weight).astype(NARROW)
+
+        labels = one.labels.reshape(part_blocks, SPAN)
+        reading = one.reading.reshape(part_blocks, SPAN)
+        one.operands = (
+            projected(one.input_low, query_w),
+            projected(one.retrieved_full, key_w),
+            projected(one.input_low, key_w),
+            projected(one.retrieved_full, value_w),
+            projected(one.input_low, value_w),
+            fixed_keys,
+            fixed_values,
+            labels[:, :, None],
+            labels[:, None, :],
+            reading[:, None, :],
+        )
+        one.attended = attention(*one.operands)
         one.residual = own_rows(one.flat).astype(WIDE)
         one.branch = scattered(matmul(one.attended, weights["out"]))
 
@@ -414,50 +530,26 @@
         one.output = collected(after(one.hidden + one.branch, whole.grad_mixing))
 
     def attend_back(one):
-        grad_attended = (
-            by_rows(one.grad_mixed, weights["out"])
-            .astype(NARROW)
-            .reshape(part_blocks, SPAN, local_heads, HD)
-        )
-        probs = jnp.exp(scores_of(one) - one.logsum)
-        grad_probs = batched("bthd,bkhd->bhtk", grad_attended, one.values)
-        grad_values = batched("bhtk,bthd->bkhd", probs.astype(NARROW), grad_attended)
-        grad_scores = (
-            probs * (grad_probs - jnp.sum(grad_probs * probs, axis=-1, keepdims=True))
-        ).astype(NARROW)
-        one.grad_queries = (
-            (batched("bhtk,bkhd->bthd", grad_scores, one.keys) * scale)
-            .astype(NARROW)
-            .reshape(part_rows, local_width)
-        )
-        grad_keys = batched("bhtk,bthd->bkhd", grad_scores, one.queries) * scale
-
-        def split_keys(grads):
-            fixed_part = jnp.sum(grads[:, :persist_count], axis=0).reshape(
-                persist_count, local_width
-            )
-            memory_part = (
-                grads[:, persist_count : persist_count + SPAN]
-                .astype(NARROW)
-                .reshape(part_rows, local_width)
-            )
-            token_part = (
-                grads[:, persist_count + SPAN :].astype(NARROW).reshape(part_rows, local_width)
-            )
-            return (fixed_part, memory_part, token_part)
-
-        one.key_fixed, one.key_memory, one.key_token = split_keys(grad_keys)
-        one.value_fixed, one.value_memory, one.value_token = split_keys(grad_values)
+        grad_attended = by_rows(one.grad_mixed, weights["out"]).astype(NARROW)
+        (
+            one.grad_queries,
+            one.key_memory,
+            one.key_token,
+            one.value_memory,
+            one.value_token,
+            one.key_fixed,
+            one.value_fixed,
+        ) = attention_back(*one.operands, grad_attended)
         partial = by_rows(one.key_memory, key_w) + by_rows(one.value_memory, value_w)
         one.partial = partial.astype(NARROW)
         one.grad_retrieved = lax.psum_scatter(one.partial, "tp", scatter_dimension=1, tiled=True)
 
     def heads_back(one):
-        grad_heads = one.grad_retrieved.astype(WIDE).reshape(rows, local_heads, HD)
+        grad_heads = one.grad_retrieved.astype(WIDE)
         one.grad_gain_memory = jnp.sum(grad_heads * one.head_unit, axis=0)
-        inner = grad_heads * gain_mem
+        inner = grad_heads * gain_flat
         grad_masked = one.head_factor * (
-            inner - one.head_unit * jnp.mean(inner * one.head_unit, axis=-1, keepdims=True)
+            inner - one.head_unit * head_spread(head_mean(inner * one.head_unit))
         )
         one.grad_read = one.reading[..., None] * grad_masked.reshape(
             count, blocks_each, SPAN, local_width
@@ -690,10 +782,8 @@
     query_w = qkv_cols[0]
     key_w = qkv_cols[1]
     value_w = qkv_cols[2]
-    fixed_keys = matmul(persist, key_w).astype(NARROW).reshape(1, persist_count, local_heads, HD)
-    fixed_values = (
-        matmul(persist, value_w).astype(NARROW).reshape(1, persist_count, local_heads, HD)
-    )
+    fixed_keys = matmul(persist, key_w).astype(NARROW)
+    fixed_values = matmul(persist, value_w).astype(NARROW)
     remember(whole)
     out_other, down_other = fetched(whole, ["retrieved_full"], whole.recall, w_out, w_down)
     weights["out"] = joined(w_out, out_other, 1)

time: 1210 us -> 1170 us (0.967)
  local copies, waits for them, and re-layouts: 158 us -> 114 us
  Pallas kernels: 0 us -> 32.4 us
  other arithmetic: 189 us -> 164 us
  matrix products: 286 us -> 269 us
  waiting for transfers between devices: 440 us -> 453 us
    pallas_call x0 -> x4, Pallas kernels: none -> 32.4 us  [the longest x2 20.9 us: attention_back(): pl.pallas_call(attention_back_kernel, grid=(blocks,), in_specs=specs + [r...]
    dot_general x53 -> x41, matrix products: 89.7 us -> 59.2 us  [batched(): return jnp.einsum(spec, left, right, preferred_element_type=WIDE)]
    reduce_scatter x8, waiting for transfers between devices: 23.6 us -> 46.5 us  [scattered(): lax.psum_scatter(array.astype(NARROW), 'tp', scatter_dimension=0, tiled=T...]
    reshape x24 -> x0, local copies, waits for them, and re-layouts: 18 us -> none  [the longest x20 16.8 us: heads(): return values.astype(NARROW).reshape(-1, SPAN, local_heads, HD)]
    ppermute x57, waiting for transfers between devices: 214 us -> 199 us  [flipped(): lax.ppermute(value, axis, [(i, i ^ bit) for i in range(lax.axis_size(axis...]
    mul x7 -> x0, local copies, waits for them, and re-layouts: 13.3 us -> none  [the longest x4 6.81 us: heads_back(): one.head_factor * (inner - one.head_unit * jnp.mean(inner * one.head_unit...]
    unnamed x656 -> x567, local copies, waits for them, and re-layouts: 52.4 us -> 51.7 us
  transfers between devices with their start and end apart: 92 -> 92, of which waited for: 35 -> 34; matrix products, arithmetic and copies ran while one was open for 41% -> 40% of each run, Pallas kernels for 0% -> 1%
where the time goes in v6:
time: 1170 us; the launch traced here: 1160 us
  waiting for transfers between devices  453 us (39%)
  matrix products  269 us (23%)
  other arithmetic  164 us (14%)
  local copies, waits for them, and re-layouts  114 us (10%)
  starting transfers between devices  93.7 us (8%)
  Pallas kernels  32.4 us (3%)
  between operations  18.9 us (2%)
  blocking collectives  17.7 us (2%)
    ppermute x57, waiting for transfers between devices, flipped(): lax.ppermute(value, axis, [(i, i ^ bit) for i in range(lax.axis_size(axis...  199 us
    dot_general x25, matrix products, matmul(): return jnp.dot(left, right, preferred_element_type=WIDE)  79.8 us
    ppermute x57, starting transfers between devices, flipped(): lax.ppermute(value, axis, [(i, i ^ bit) for i in range(lax.axis_size(axis...  68.8 us
    psum x1, waiting for transfers between devices, begin(): one.mixing = lax.psum(one.products, 'tp')  66.1 us
    dot_general x17, matrix products, by_rows(): lax.dot_general(left, right, (((1,), (1,)), ((), ())), preferred_element_...  65 us
    dot_general x41, matrix products, batched(): return jnp.einsum(spec, left, right, preferred_element_type=WIDE)  59.2 us
    psum x1, waiting for transfers between devices, remember_back(): one.grad_mixing = lax.psum(grad_mixing, 'tp')  52 us
    unnamed x567, local copies, waits for them, and re-layouts  51.7 us
  transfers between devices with their start and end apart: 92, of which 34 were waited for; matrix products, arithmetic and copies ran while one was open for 40% of the time, Pallas kernels for 1%

profile of v6, /device:TPU:1, one launch (start us, length us, event | category | flops | bytes accessed | tf_op | source)
XLA Modules:
  0.0 1162.9 jit_solution(11135767494141454051)
XLA Ops:
  22.9 24.0 %collective-permute-done.6 = bf16[384,1536]{1,0:T(8,128)(2,1)} collective-permute-done((bf16[384,1536]{1,0:T(8,128)(2,1)}, bf16[384,1536]{1,0:T(8,128)(2,1)}, u32[]{:S(2)}, u32[]{:S(2)}) %collective-permute-start.6) | collective-permute-done | bytes 1179680 | tf_op jit(solution)/shard_map/ppermute | solution.py:28
  67.8 9.7 collective-permute-done
  125.0 66.1 %all-reduce.12.cloned.1.call-done = bf16[1056,768]{1,0:T(8,128)(2,1)} async-done(((bf16[1056,768]{1,0:T(8,128)(2,1)}), bf16[1056,768]{1,0:T(8,128)(2,1)}) %all-reduce.12.cloned.1.call-update) | async-done | bytes 1622032 | tf_op jit(solution)/shard_map/psum | solution.py:424
  211.4 10.9 collective-permute-done.16
  262.4 35.9 %collective-permute-done.18 = bf16[384,768]{1,0:T(8,128)(2,1)S(1)} collective-permute-done((bf16[384,768]{1,0:T(8,128)(2,1)S(1)}, bf16[384,768]{1,0:T(8,128)(2,1)S(1)}, u32[]{:S(2)}, u32[]{:S(2)}) %collective-permute-start.18) | collective-permute-done | bytes 589856 | tf_op jit(solution)/shard_map/ppermute | solution.py:28
  299.1 9.6 all-gather.12.cloned.1.call-done
  372.4 22.4 %reduce-scatter.18.cloned.1.call-done = bf16[128,1536]{1,0:T(8,128)(2,1)} async-done(((bf16[512,1536]{1,0:T(8,128)(2,1)}), bf16[128,1536]{1,0:T(8,128)(2,1)}) %reduce-scatter.18.cloned.1.call-update) | async-done | bytes 393232 | tf_op jit(solution)/shard_map/reduce_scatter | solution.py:278
  398.8 22.3 %collective-permute-done.20 = bf16[768,1024]{1,0:T(8,128)(2,1)} collective-permute-done((bf16[768,1024]{1,0:T(8,128)(2,1)}, bf16[768,1024]{1,0:T(8,128)(2,1)}, u32[]{:S(2)}, u32[]{:S(2)}) %collective-permute-start.20) | collective-permute-done | bytes 1572896 | tf_op jit(solution)/shard_map/ppermute | solution.py:28
  421.1 10.6 all-gather.14.cloned.1.call-done
  452.5 16.5 %all-gather.16.cloned.1.call-done = bf16[512,1536]{1,0:T(8,128)(2,1)} async-done(((bf16[128,1536]{1,0:T(8,128)(2,1)}), bf16[512,1536]{1,0:T(8,128)(2,1)}) %all-gather.16.cloned.1.call-update) | async-done | bytes 1572880 | tf_op jit(solution)/shard_map/all_gather | solution.py:283
  528.7 14.0 %reduce-scatter.22.cloned.1.call-done = bf16[128,1536]{1,0:T(8,128)(2,1)} async-done(((bf16[512,1536]{1,0:T(8,128)(2,1)}), bf16[128,1536]{1,0:T(8,128)(2,1)}) %reduce-scatter.22.cloned.1.call-update) | async-done | bytes 393232 | tf_op jit(solution)/shard_map/reduce_scatter | solution.py:278
  559.5 24.9 %collective-permute-done.25 = bf16[2,2,192,1024]{3,2,1,0:T(8,128)(2,1)} collective-permute-done((bf16[2,2,192,1024]{3,2,1,0:T(8,128)(2,1)}, bf16[2,2,192,1024]{3,2,1,0:T(8,128)(2,1)}, u32[]{:S(2)}, u32[]{:S(2)}) %collective-permute-start.25) | collective-permute-done | bytes 1572896 | tf_op jit(solution)/shard_map/ppermute | solution.py:28
  591.0 10.6 shard_map.239
  605.9 11.2 all-gather.20.cloned.1.call-done
  620.5 10.3 shard_map.240
  684.2 22.7 %reduce-scatter.34.cloned.1.call-done = bf16[384,512]{1,0:T(8,128)(2,1)} async-done(((bf16[1536,512]{1,0:T(8,128)(2,1)}), bf16[384,512]{1,0:T(8,128)(2,1)}) %reduce-scatter.34.cloned.1.call-update) | async-done | bytes 393232
  817.6 11.3 add_add_fusion
  831.3 52.0 %all-reduce.14.cloned.1.call-done = bf16[1056,768]{1,0:T(8,128)(2,1)} async-done(((bf16[1056,768]{1,0:T(8,128)(2,1)}), bf16[1056,768]{1,0:T(8,128)(2,1)}) %all-reduce.14.cloned.1.call-update) | async-done | bytes 1622032 | tf_op jit(solution)/shard_map/psum | solution.py:613
  883.9 9.7 multiply_convert_fusion
  957.5 8.1 add_convert_fusion
  1003.4 26.8 %collective-permute-done.46 = f32[29568]{0:T(1024)S(1)} collective-permute-done((f32[29568]{0:T(1024)S(1)}, f32[29568]{0:T(1024)S(1)}, u32[]{:S(2)}, u32[]{:S(2)}) %collective-permute-start.46) | collective-permute-done | bytes 118304 | tf_op jit(solution)/shard_map/ppermute | solution.py:28
  1035.9 17.7 %all-gather.1 = f32[4,1,26112]{2,1,0:T(1,128)S(1)} all-gather(f32[1,1,26112]{2,1,0:T(1,128)S(1)} %reshape.830), channel_id=2, replica_groups=mesh['shard'=2,'ctx'=4,'tp'=4] {'tp'}, dimensions={0}, use_global_device_ids=true | all-gather | bytes 522240 | tf_op jit(solution)/shard_map/all_gather | solution.py:917
  1112.4 11.7 %collective-permute-done.63 = bf16[192,384]{1,0:T(8,128)(2,1)S(1)} collective-permute-done((bf16[192,384]{1,0:T(8,128)(2,1)S(1)}, bf16[192,384]{1,0:T(8,128)(2,1)S(1)}, u32[]{:S(2)}, u32[]{:S(2)}) %collective-permute-start.63) | collective-permute-done | bytes 147488 | tf_op jit(solution)/shard_map/ppermute | solution.py:28
  1127.3 13.9 %collective-permute-done.66 = bf16[192,1536]{1,0:T(8,128)(2,1)S(1)} collective-permute-done((bf16[192,1536]{1,0:T(8,128)(2,1)S(1)}, bf16[192,1536]{1,0:T(8,128)(2,1)S(1)}, u32[]{:S(2)}, u32[]{:S(2)}) %collective-permute-start.66) | collective-permute-done | bytes 589856 | tf_op jit(solution)/shard_map/ppermute | solution.py:28
  (1149 shorter events, 671.2 us)
Async XLA Ops:
  7.2 184.0 %all-reduce.12.cloned.1.call-start = ((), (), s32[]{:S(2)}) async-start(), calls=%async_computation.11 | async-start | bytes 3244032 | tf_op jit(solution)/shard_map/psum | solution.py:424
  121.8 187.0 %all-gather.12.cloned.1.call-start = ((), (), s32[]{:S(2)}) async-start(), calls=%async_computation.12 | async-start | bytes 3932160 | tf_op jit(solution)/shard_map/all_gather | solution.py:471
  244.6 113.1 %reduce-scatter.16.cloned.1.call-start = ((), (), s32[]{:S(2)}) async-start(), calls=%async_computation.13 | async-start | bytes 1966080 | tf_op jit(solution)/shard_map/reduce_scatter | solution.py:278
  323.8 71.0 %reduce-scatter.18.cloned.1.call-start = ((), (), s32[]{:S(2)}) async-start(), calls=%async_computation.15 | async-start | bytes 1966080 | tf_op jit(solution)/shard_map/reduce_scatter | solution.py:278
  346.0 85.6 %all-gather.14.cloned.1.call-start = ((), (), s32[]{:S(2)}) async-start(), calls=%async_computation.14 | async-start | bytes 1966080 | tf_op jit(solution)/shard_map/all_gather | solution.py:283
  360.8 108.2 %all-gather.16.cloned.1.call-start = ((), (), s32[]{:S(2)}) async-start(), calls=%async_computation.17 | async-start | bytes 1966080 | tf_op jit(solution)/shard_map/all_gather | solution.py:283
  398.5 116.6 %reduce-scatter.20.cloned.1.call-start = ((), (), s32[]{:S(2)}) async-start(), calls=%async_computation.16 | async-start | bytes 1966080 | tf_op jit(solution)/shard_map/reduce_scatter | solution.py:278
  447.0 95.8 %reduce-scatter.22.cloned.1.call-start = ((), (), s32[]{:S(2)}) async-start(), calls=%async_computation.19 | async-start | bytes 1966080 | tf_op jit(solution)/shard_map/reduce_scatter | solution.py:278
  491.4 96.4 %all-gather.18.cloned.1.call-start = ((), (), s32[]{:S(2)}) async-start(), calls=%async_computation.18 | async-start | bytes 1966080 | tf_op jit(solution)/shard_map/all_gather | solution.py:283
  519.7 97.3 %all-gather.20.cloned.1.call-start = ((), (), s32[]{:S(2)}) async-start(), calls=%async_computation.20 | async-start | bytes 1966080 | tf_op jit(solution)/shard_map/all_gather | solution.py:283
  553.4 128.8 %reduce-scatter.36.cloned.1.call-start = ((), (), s32[]{:S(2)}) async-start(), calls=%async_computation.32 | async-start | bytes 1966080
  635.6 71.4 %reduce-scatter.34.cloned.1.call-start = ((), (), s32[]{:S(2)}) async-start(), calls=%async_computation.31 | async-start | bytes 1966080
  659.9 142.9 %reduce-scatter.24.cloned.1.call-start = ((), (), s32[]{:S(2)}) async-start(), calls=%async_computation.21 | async-start | bytes 1966080 | tf_op jit(solution)/shard_map/reduce_scatter | solution.py:278
  717.5 87.3 %reduce-scatter.26.cloned.1.call-start = ((), (), s32[]{:S(2)}) async-start(), calls=%async_computation.22 | async-start | bytes 1966080 | tf_op jit(solution)/shard_map/reduce_scatter | solution.py:278
  749.8 133.5 %all-reduce.14.cloned.1.call-start = ((), (), s32[]{:S(2)}) async-start(), calls=%async_computation.23 | async-start | bytes 3244032 | tf_op jit(solution)/shard_map/psum | solution.py:613
  806.8 158.8 %all-gather.22.cloned.1.call-start = ((), (), s32[]{:S(2)}) async-start(), calls=%async_computation.24 | async-start | bytes 1966080 | tf_op jit(solution)/shard_map/all_gather | solution.py:283
  883.3 82.3 %all-gather.24.cloned.1.call-start = ((), (), s32[]{:S(2)}) async-start(), calls=%async_computation.25 | async-start | bytes 1966080 | tf_op jit(solution)/shard_map/all_gather | solution.py:283
  900.6 94.7 %reduce-scatter.32.cloned.1.call-start = ((), (), s32[]{:S(2)}) async-start(), calls=%async_computation.29 | async-start | bytes 491520 | tf_op jit(solution)/shard_map/reduce_scatter | solution.py:868
  925.2 129.6 %reduce-scatter.30.cloned.1.call-start = ((), (), s32[]{:S(2)}) async-start(), calls=%async_computation.28 | async-start | bytes 1966080 | tf_op jit(solution)/shard_map/reduce_scatter | solution.py:278
  969.6 91.8 %reduce-scatter.28.cloned.1.call-start = ((), (), s32[]{:S(2)}) async-start(), calls=%async_computation.26 | async-start | bytes 1966080 | tf_op jit(solution)/shard_map/reduce_scatter | solution.py:278
  992.7 84.2 %collective-permute-start.68 = (bf16[2,2,192,1024]{3,2,0,1:T(8,128)(2,1)}, bf16[2,2,192,1024]{3,2,0,1:T(8,128)(2,1)}, u32[]{:S(2)}, u32[]{:S(2)}) collective-permute-start(bf16[2,2,192,1024]{3,2,0,1:T(8,128)(2,1)} %pad_maximum_fusion.23), channel_id=1, source_target_pairs={{0,4},{4,0},{8,12},{12,8},{1,5},{5,1},{9,13},{13,9},{2,6},{6,2},{1... | collective-permute-start | bytes 4718600 | tf_op jit(solution)/shard_map/ppermute | solution.py:28
  993.7 76.8 %collective-permute-start.69 = (bf16[2,256,768]{2,1,0:T(8,128)(2,1)}, bf16[2,256,768]{2,1,0:T(8,128)(2,1)}, u32[]{:S(2)}, u32[]{:S(2)}) collective-permute-start(bf16[2,256,768]{2,1,0:T(8,128)(2,1)} %pad_maximum_fusion.66), channel_id=1, source_target_pairs={{0,4},{4,0},{8,12},{12,8},{1,5},{5,1},{9,13},{13,9},{2,6},{6,2},{1... | collective-permute-start | bytes 2359304 | tf_op jit(solution)/shard_map/ppermute | solution.py:28
  996.3 154.4 %all-gather.28.cloned.1.call-start = ((), (), s32[]{:S(2)}) async-start(), calls=%async_computation.30 | async-start | bytes 1966080 | tf_op jit(solution)/shard_map/all_gather | solution.py:283
  1070.2 80.4 %all-gather.26.cloned.1.call-start = ((), (), s32[]{:S(2)}) async-start(), calls=%async_computation.27 | async-start | bytes 1966080 | tf_op jit(solution)/shard_map/all_gather | solution.py:283
  (343 other events, 4690.8 us)
Sparse Core Ops, SparseCore 0:
  121.9 69.2 all-reduce.11
  244.7 63.9 all-gather.11
  323.9 33.7 reduce-scatter.15
  360.5 34.2 reduce-scatter.17
  396.2 35.3 all-gather.13
  433.1 35.8 all-gather.15
  471.3 34.7 reduce-scatter.19
  508.4 34.2 reduce-scatter.21
  544.3 35.3 all-gather.17
  581.1 35.8 all-gather.19
  635.7 34.7 reduce-scatter.35
  672.7 34.2 reduce-scatter.33
  717.6 34.2 reduce-scatter.23
  754.0 34.2 reduce-scatter.25
  806.9 76.3 all-reduce.13
  884.7 36.1 all-gather.21
  922.9 35.8 all-gather.23
  960.9 18.2 reduce-scatter.31
  982.1 35.4 reduce-scatter.29
  1020.4 40.9 reduce-scatter.27
  1070.3 35.7 all-gather.27
  1107.7 35.8 all-gather.25

commit v7 on v6

--- a/solution.py
+++ b/solution.py
@@ -282,10 +282,11 @@
     def collected(array):
         return lax.all_gather(array.astype(NARROW), "tp", axis=0, tiled=True)
 
-    def summed_over_ranks(array):
+    def summed_over_ranks(array, kind=WIDE):
         bit = 1
         while bit < ranks:
-            array = array + flipped(array, "tp", bit)
+            array = array.astype(kind)
+            array = array.astype(WIDE) + flipped(array, "tp", bit).astype(WIDE)
             bit *= 2
         return array
 
@@ -384,7 +385,8 @@
         def shaped(values):
             return values.reshape(count, blocks_each, SPAN, local_units)
 
-        low, one.preact = features_of(mine(tokens))
+        low, preact = features_of(mine(tokens))
+        one.preact = lax.optimization_barrier(preact)
         one.input_low = low.reshape(rows, width)
         one.features = jax.nn.silu(one.preact).astype(NARROW)
         squares = jnp.sum(jnp.square(one.features.astype(WIDE)), axis=1)
@@ -526,8 +528,17 @@
         activ = after(one.activ, whole.grad_retrieved)
         one.branch = scattered(matmul(activ, weights["down"]))
 
+    def rank_major(array):
+        array = array.reshape(STREAMS, ranks, -1, width)
+        return array.transpose(1, 0, 2, 3).reshape(-1, width)
+
+    def stream_major(array):
+        array = array.reshape(ranks, STREAMS, -1, width)
+        return array.transpose(1, 0, 2, 3).reshape(-1, width)
+
     def finish_output(one):
-        one.output = collected(after(one.hidden + one.branch, whole.grad_mixing))
+        own = jnp.concatenate([item.hidden + item.branch for item in streams], axis=0)
+        one.output = collected(after(own, one.grad_mixing))
 
     def attend_back(one):
         grad_attended = by_rows(one.grad_mixed, weights["out"]).astype(NARROW)
@@ -610,6 +621,7 @@
         grad_mixing, branches = lax.optimization_barrier((grad_mixing, branches))
         for item, branch in zip(streams, branches):
             item.branch = branch
+        one.packed_back = grad_mixing
         one.grad_mixing = lax.psum(grad_mixing, "tp")
 
     def features_back(one):
@@ -679,22 +691,22 @@
         one.grad_input = (one.early + by_rows(one.grad_pre, feature_cols)).astype(NARROW)
 
     def input_early(one):
+        queries, keys, values, targets, _ = lax.optimization_barrier(
+            (one.grad_queries, one.key_token, one.value_token, one.grad_targets, one.packed_back)
+        )
         one.early = (
-            by_rows(one.grad_queries, query_w)
-            + by_rows(one.key_token, key_w)
-            + by_rows(one.value_token, value_w)
-            + by_rows(one.grad_targets, value_cols)
+            by_rows(queries, query_w)
+            + by_rows(keys, key_w)
+            + by_rows(values, value_w)
+            + by_rows(targets, value_cols)
         )
 
     def tokens_back(one):
-        if one is not streams[0]:
-            one.grad_input = after(one.grad_input, streams[0].grad_own)
         grad_input = one.grad_input
         _, unit_in, factor_in = norm_rows(one.residual, gain_in_wide)
         one.grad_gain_in = jnp.sum(grad_input * unit_in, axis=0)
         grad_own = one.grad_hidden + norm_back(grad_input, unit_in, factor_in, gain_in_wide)
-        one.grad_own = grad_own.astype(NARROW)
-        one.grad_tokens = collected(one.grad_own).astype(WIDE).reshape(-1, local_len, width)
+        one.grad_tokens = stream_major(collected(grad_own)).astype(WIDE)
 
     whole = Stream()
     streams = [Stream() for _ in range(STREAMS)]
@@ -863,10 +875,12 @@
     every(branch_out)
     heads_back(whole)
     remember_back(whole)
+    persist_sum = Holder(summed_over_ranks(after(grad_persist, whole.packed_back), NARROW))
     input_early(whole)
-    grad_persist = after(grad_persist, whole.grad_mixing)
-    grad_persist = lax.psum_scatter(grad_persist, "tp", scatter_dimension=0, tiled=True)
-    target_reduction = Reduction(over_rows(whole.input_low, whole.grad_targets), True)
+    grad_targets = after(whole.grad_targets, whole.packed_back)
+    target_reduction = Reduction(over_rows(whole.input_low, grad_targets), True)
+    for item in feed_reductions + mix_reductions:
+        item.array = after(item.array, whole.packed_back)
     for item in feed_reductions:
         item.together()
     for item in mix_reductions:
@@ -877,14 +891,17 @@
         *feed_reductions,
         *mix_reductions,
         target_reduction,
+        persist_sum,
     )
-    every(finish_output)
+    finish_output(whole)
     features_back(whole)
     inputs_back(whole)
-    outputs = [one.output for one in streams]
-    whole.grad_input, outputs = lax.optimization_barrier((whole.grad_input, outputs))
-    for index, one in enumerate(streams):
-        one.grad_input = scattered(whole.grad_input[index * part_rows : (index + 1) * part_rows])
+    grad_input, whole.output = lax.optimization_barrier(
+        (rank_major(whole.grad_input), whole.output)
+    )
+    whole.grad_input = scattered(grad_input)
+    merged("residual")
+    merged("grad_hidden")
 
     grad_decays = whole.grad_decays
     grad_retain = 0.0
@@ -905,35 +922,27 @@
             small = small + flipped(small, axis, bit)
         return small
 
-    small = summed(
-        [
-            grad_persist,
-            over(lambda one: one.grad_gain_ffn),
-            whole.grad_gain_memory,
-            grad_rates,
-        ]
-    )
-    cut = grad_persist.size + width
-    spread = Holder(lax.all_gather(small[:cut], "tp", axis=0))
+    small = Holder(summed([persist_sum.array, whole.grad_gain_memory, grad_rates]))
     feature_reduction = Reduction(over_rows(whole.input_low, whole.grad_pre), True)
     late_reductions = [feature_reduction, target_reduction]
     for item in mix_reductions:
         item.apart()
     for item in late_reductions:
         item.across()
-    tied(last_stream, ["grad_input"], spread, *mix_reductions, *late_reductions)
-    every(tokens_back)
+    tied(whole, ["grad_input"], small, *mix_reductions, *late_reductions)
+    tokens_back(whole)
     for item in mix_reductions:
         item.together()
     for item in late_reductions:
         item.apart()
         item.together()
-    gain_in_sum = summed_over_ranks(summed([over(lambda one: one.grad_gain_in)]))
-    grad_persist = spread.array[:, : grad_persist.size].reshape(persist_count, width)
-    gain_ffn_sum = jnp.sum(spread.array[:, cut - width :], axis=0)
-    middle_cut = cut + local_heads * HD
-    grad_gain_memory = small[cut:middle_cut].reshape(local_heads, HD)
-    grad_rates = small[middle_cut:].reshape(2, local_units)
+    gains = summed([whole.grad_gain_in, over(lambda one: one.grad_gain_ffn)])
+    gain_in_sum, gain_ffn_sum = summed_over_ranks(gains).reshape(2, width)
+    cut = persist_sum.array.size
+    middle_cut = cut + local_width
+    grad_persist = small.array[:cut].reshape(persist_count, width)
+    grad_gain_memory = small.array[cut:middle_cut].reshape(local_heads, HD)
+    grad_rates = small.array[middle_cut:].reshape(2, local_units)
     grad_down, grad_gate_up = [item.result() for item in feed_reductions]
     grad_out_rows, grad_qkv = [item.result() for item in mix_reductions]
     grad_feature_w, grad_target_w = [item.result() for item in late_reductions]
@@ -943,8 +952,8 @@
         return lax.dynamic_slice_in_dim(array, half_index * size, size, axis)
 
     return (
-        jnp.concatenate(outputs, axis=0).reshape(tokens.shape),
-        jnp.concatenate([one.grad_tokens for one in streams], axis=0),
+        stream_major(whole.output).reshape(tokens.shape),
+        whole.grad_tokens.reshape(tokens.shape),
         own_half(gain_in_sum, 0),
         own_half(gain_ffn_sum, 0),
         own_half(grad_gain_memory, 1),

time: 1170 us -> 1170 us (level)
  blocking collectives: 17.7 us -> 0 us
  waiting for transfers between devices: 453 us -> 470 us
    reduce_scatter x8 -> x7, waiting for transfers between devices: 46.5 us -> 87.5 us  [scattered(): lax.psum_scatter(array.astype(NARROW), 'tp', scatter_dimension=0, tiled=T...]
    psum x1, waiting for transfers between devices: 52 us -> 25.6 us  [remember_back(): one.grad_mixing = lax.psum(grad_mixing, 'tp')]
    all_gather x1 -> x0, blocking collectives: 17.7 us -> none  [on_device(): spread = Holder(lax.all_gather(small[:cut], 'tp', axis=0))]
    unnamed x24 -> x20, waiting for transfers between devices: 23.1 us -> 27.7 us
    unnamed x567 -> x539, local copies, waits for them, and re-layouts: 51.7 us -> 48.3 us
    all_gather x8 -> x6, waiting for transfers between devices: 38.2 us -> 35.9 us  [collected(): return lax.all_gather(array.astype(NARROW), 'tp', axis=0, tiled=True)]
    ppermute x57 -> x59, waiting for transfers between devices: 199 us -> 198 us  [flipped(): lax.ppermute(value, axis, [(i, i ^ bit) for i in range(lax.axis_size(axis...]
    ppermute x57 -> x59, starting transfers between devices: 68.8 us -> 67.5 us  [flipped(): lax.ppermute(value, axis, [(i, i ^ bit) for i in range(lax.axis_size(axis...]
  transfers between devices with their start and end apart: 92 -> 90, of which waited for: 34 -> 41; matrix products, arithmetic and copies ran while one was open for 40% -> 36% of each run, Pallas kernels for 1% -> 1%
where the time goes in v7:
time: 1170 us; the launch traced here: 1160 us
  waiting for transfers between devices  470 us (40%)
  matrix products  261 us (22%)
  other arithmetic  168 us (14%)
  local copies, waits for them, and re-layouts  114 us (10%)
  starting transfers between devices  94.5 us (8%)
  Pallas kernels  32.2 us (3%)
  between operations  18.5 us (2%)
    ppermute x59, waiting for transfers between devices, flipped(): lax.ppermute(value, axis, [(i, i ^ bit) for i in range(lax.axis_size(axis...  198 us
    reduce_scatter x7, waiting for transfers between devices, scattered(): lax.psum_scatter(array.astype(NARROW), 'tp', scatter_dimension=0, tiled=T...  87.5 us
    dot_general x25, matrix products, matmul(): return jnp.dot(left, right, preferred_element_type=WIDE)  77.3 us
    ppermute x59, starting transfers between devices, flipped(): lax.ppermute(value, axis, [(i, i ^ bit) for i in range(lax.axis_size(axis...  67.5 us
    dot_general x17, matrix products, by_rows(): lax.dot_general(left, right, (((1,), (1,)), ((), ())), preferred_element_...  64.5 us
    psum x1, waiting for transfers between devices, begin(): one.mixing = lax.psum(one.products, 'tp')  64.4 us
    dot_general x41, matrix products, batched(): return jnp.einsum(spec, left, right, preferred_element_type=WIDE)  62.8 us
    unnamed x539, local copies, waits for them, and re-layouts  48.3 us
  transfers between devices with their start and end apart: 90, of which 41 were waited for; matrix products, arithmetic and copies ran while one was open for 36% of the time, Pallas kernels for 1%

profile of v7, /device:TPU:1, one launch (start us, length us, event | category | flops | bytes accessed | tf_op | source)
XLA Modules:
  0.0 1157.9 jit_solution(3703757517637239565)
XLA Ops:
  24.6 22.3 %collective-permute-done.6 = bf16[384,1536]{1,0:T(8,128)(2,1)} collective-permute-done((bf16[384,1536]{1,0:T(8,128)(2,1)}, bf16[384,1536]{1,0:T(8,128)(2,1)}, u32[]{:S(2)}, u32[]{:S(2)}) %collective-permute-start.6) | collective-permute-done | bytes 1179680 | tf_op jit(solution)/shard_map/ppermute | solution.py:28
  67.8 9.6 collective-permute-done
  127.3 64.4 %all-reduce.12.cloned.1.call-done = bf16[1056,768]{1,0:T(8,128)(2,1)} async-done(((bf16[1056,768]{1,0:T(8,128)(2,1)}), bf16[1056,768]{1,0:T(8,128)(2,1)}) %all-reduce.12.cloned.1.call-update) | async-done | bytes 1622032 | tf_op jit(solution)/shard_map/psum | solution.py:426
  211.9 10.9 collective-permute-done.16
  263.1 36.0 %collective-permute-done.18 = bf16[384,768]{1,0:T(8,128)(2,1)S(1)} collective-permute-done((bf16[384,768]{1,0:T(8,128)(2,1)S(1)}, bf16[384,768]{1,0:T(8,128)(2,1)S(1)}, u32[]{:S(2)}, u32[]{:S(2)}) %collective-permute-start.18) | collective-permute-done | bytes 589856 | tf_op jit(solution)/shard_map/ppermute | solution.py:28
  299.9 9.3 all-gather.8.cloned.1.call-done
  371.4 24.0 %reduce-scatter.16.cloned.1.call-done = bf16[128,1536]{1,0:T(8,128)(2,1)} async-done(((bf16[512,1536]{1,0:T(8,128)(2,1)}), bf16[128,1536]{1,0:T(8,128)(2,1)}) %reduce-scatter.16.cloned.1.call-update) | async-done | bytes 393232 | tf_op jit(solution)/shard_map/reduce_scatter | solution.py:278
  399.1 21.8 %collective-permute-done.20 = bf16[768,1024]{1,0:T(8,128)(2,1)} collective-permute-done((bf16[768,1024]{1,0:T(8,128)(2,1)}, bf16[768,1024]{1,0:T(8,128)(2,1)}, u32[]{:S(2)}, u32[]{:S(2)}) %collective-permute-start.20) | collective-permute-done | bytes 1572896 | tf_op jit(solution)/shard_map/ppermute | solution.py:28
  420.9 11.3 all-gather.10.cloned.1.call-done
  457.1 12.5 %all-gather.12.cloned.1.call-done = bf16[512,1536]{1,0:T(8,128)(2,1)} async-done(((bf16[128,1536]{1,0:T(8,128)(2,1)}), bf16[512,1536]{1,0:T(8,128)(2,1)}) %all-gather.12.cloned.1.call-update) | async-done | bytes 1572880 | tf_op jit(solution)/shard_map/all_gather | solution.py:283
  519.9 23.4 %reduce-scatter.20.cloned.1.call-done = bf16[128,1536]{1,0:T(8,128)(2,1)} async-done(((bf16[512,1536]{1,0:T(8,128)(2,1)}), bf16[128,1536]{1,0:T(8,128)(2,1)}) %reduce-scatter.20.cloned.1.call-update) | async-done | bytes 393232 | tf_op jit(solution)/shard_map/reduce_scatter | solution.py:278
  558.4 27.1 %collective-permute-done.25 = bf16[2,2,192,1024]{3,2,1,0:T(8,128)(2,1)} collective-permute-done((bf16[2,2,192,1024]{3,2,1,0:T(8,128)(2,1)}, bf16[2,2,192,1024]{3,2,1,0:T(8,128)(2,1)}, u32[]{:S(2)}, u32[]{:S(2)}) %collective-permute-start.25) | collective-permute-done | bytes 1572896 | tf_op jit(solution)/shard_map/ppermute | solution.py:28
  592.4 10.5 shard_map.239
  607.2 10.5 all-gather.16.cloned.1.call-done
  620.8 10.3 shard_map.240
  682.1 27.4 %reduce-scatter.28.cloned.1.call-done = bf16[384,512]{1,0:T(8,128)(2,1)} async-done(((bf16[1536,512]{1,0:T(8,128)(2,1)}), bf16[384,512]{1,0:T(8,128)(2,1)}) %reduce-scatter.28.cloned.1.call-update) | async-done | bytes 393232
  793.1 15.4 %reduce-scatter.24.cloned.1.call-done = bf16[128,1536]{1,0:T(8,128)(2,1)} async-done(((bf16[512,1536]{1,0:T(8,128)(2,1)}), bf16[128,1536]{1,0:T(8,128)(2,1)}) %reduce-scatter.24.cloned.1.call-update) | async-done | bytes 393232 | tf_op jit(solution)/shard_map/reduce_scatter | solution.py:278
  838.1 11.1 add_add_fusion
  862.3 15.2 %collective-permute-done.43 = bf16[64,1536]{1,0:T(8,128)(2,1)S(1)} collective-permute-done((bf16[64,1536]{1,0:T(8,128)(2,1)S(1)}, bf16[64,1536]{1,0:T(8,128)(2,1)S(1)}, u32[]{:S(2)}, u32[]{:S(2)}) %collective-permute-start.43) | collective-permute-done | bytes 196640 | tf_op jit(solution)/shard_map/ppermute | solution.py:28
  885.2 25.6 %all-reduce.14.cloned.1.call-done = bf16[1056,768]{1,0:T(8,128)(2,1)} async-done(((bf16[1056,768]{1,0:T(8,128)(2,1)}), bf16[1056,768]{1,0:T(8,128)(2,1)}) %all-reduce.14.cloned.1.call-update) | async-done | bytes 1622032 | tf_op jit(solution)/shard_map/psum | solution.py:625
  1045.0 9.2 collective-permute-done.53
  1056.4 18.9 %reduce-scatter.26.cloned.1.call-done = bf16[256,1536]{1,0:T(8,128)(2,1)} async-done(((bf16[1024,1536]{1,0:T(8,128)(2,1)}), bf16[256,1536]{1,0:T(8,128)(2,1)}) %reduce-scatter.26.cloned.1.call-update) | async-done | bytes 786448 | tf_op jit(solution)/shard_map/reduce_scatter | solution.py:278
  1088.0 11.9 %collective-permute-done.57 = f32[3072]{0:T(1024)S(1)} collective-permute-done((f32[3072]{0:T(1024)S(1)}, f32[3072]{0:T(1024)S(1)}, u32[]{:S(2)}, u32[]{:S(2)}) %collective-permute-start.57) | collective-permute-done | bytes 12320 | tf_op jit(solution)/shard_map/ppermute | solution.py:28
  1122.2 13.1 %collective-permute-done.68 = bf16[192,1536]{1,0:T(8,128)(2,1)S(1)} collective-permute-done((bf16[192,1536]{1,0:T(8,128)(2,1)S(1)}, bf16[192,1536]{1,0:T(8,128)(2,1)S(1)}, u32[]{:S(2)}, u32[]{:S(2)}) %collective-permute-start.68) | collective-permute-done | bytes 589856 | tf_op jit(solution)/shard_map/ppermute | solution.py:28
  (1116 shorter events, 687.8 us)
Async XLA Ops:
  7.2 184.5 %all-reduce.12.cloned.1.call-start = ((), (), s32[]{:S(2)}) async-start(), calls=%async_computation.9 | async-start | bytes 3244032 | tf_op jit(solution)/shard_map/psum | solution.py:426
  7.2 70.2 %collective-permute-start = (bf16[2,512,1536]{2,1,0:T(8,128)(2,1)}, bf16[2,512,1536]{2,1,0:T(8,128)(2,1)}, u32[]{:S(2)}, u32[]{:S(2)}) collective-permute-start(bf16[2,512,1536]{2,1,0:T(8,128)(2,1)} %param.14), channel_id=1, source_target_pairs={{0,8},{4,12},{8,0},{12,4},{1,9},{5,13},{9,1},{13,5},{2,10},{6,14},... | collective-permute-start | bytes 9437192 | tf_op jit(solution)/shard_map/ppermute | solution.py:28
  9.3 68.1 %collective-permute-start.4 = (bf16[2,512,1536]{2,1,0:T(8,128)(2,1)}, bf16[2,512,1536]{2,1,0:T(8,128)(2,1)}, u32[]{:S(2)}, u32[]{:S(2)}) collective-permute-start(bf16[2,512,1536]{2,1,0:T(8,128)(2,1)} %param.14), channel_id=1, source_target_pairs={{0,4},{4,0},{8,12},{12,8},{1,5},{5,1},{9,13},{13,9},{2,6},{6,2},{1... | collective-permute-start | bytes 9437192 | tf_op jit(solution)/shard_map/ppermute | solution.py:28
  121.0 70.7 %collective-permute-start.11 = (bf16[3,768,384]{2,1,0:T(8,128)(2,1)}, bf16[3,768,384]{2,1,0:T(8,128)(2,1)S(1)}, u32[]{:S(2)}, u32[]{:S(2)}) collective-permute-start(bf16[3,768,384]{2,1,0:T(8,128)(2,1)} %param.21), channel_id=1, source_target_pairs={{0,16},{16,0},{1,17},{17,1},{2,18},{18,2},{3,19},{19,3},{4,20},{20... | collective-permute-start | bytes 5308424 | tf_op jit(solution)/shard_map/ppermute | solution.py:28
  122.3 187.0 %all-gather.8.cloned.1.call-start = ((), (), s32[]{:S(2)}) async-start(), calls=%async_computation.10 | async-start | bytes 3932160 | tf_op jit(solution)/shard_map/all_gather | solution.py:473
  245.2 113.2 %reduce-scatter.14.cloned.1.call-start = ((), (), s32[]{:S(2)}) async-start(), calls=%async_computation.11 | async-start | bytes 1966080 | tf_op jit(solution)/shard_map/reduce_scatter | solution.py:278
  324.4 71.0 %reduce-scatter.16.cloned.1.call-start = ((), (), s32[]{:S(2)}) async-start(), calls=%async_computation.13 | async-start | bytes 1966080 | tf_op jit(solution)/shard_map/reduce_scatter | solution.py:278
  345.6 86.7 %all-gather.10.cloned.1.call-start = ((), (), s32[]{:S(2)}) async-start(), calls=%async_computation.12 | async-start | bytes 1966080 | tf_op jit(solution)/shard_map/all_gather | solution.py:283
  361.5 108.1 %all-gather.12.cloned.1.call-start = ((), (), s32[]{:S(2)}) async-start(), calls=%async_computation.15 | async-start | bytes 1966080 | tf_op jit(solution)/shard_map/all_gather | solution.py:283
  363.8 57.1 %collective-permute-start.20 = (bf16[768,1024]{1,0:T(8,128)(2,1)}, bf16[768,1024]{1,0:T(8,128)(2,1)}, u32[]{:S(2)}, u32[]{:S(2)}) collective-permute-start(bf16[768,1024]{1,0:T(8,128)(2,1)} %get-tuple-element.107), channel_id=1, source_target_pairs={{0,16},{16,0},{1,17},{17,1},{2,18},{18,2},{3,19},{19,3},{4,20},{20... | collective-permute-start | bytes 4718600 | tf_op jit(solution)/shard_map/ppermute | solution.py:28
  398.8 107.9 %reduce-scatter.18.cloned.1.call-start = ((), (), s32[]{:S(2)}) async-start(), calls=%async_computation.14 | async-start | bytes 1966080 | tf_op jit(solution)/shard_map/reduce_scatter | solution.py:278
  456.6 86.7 %reduce-scatter.20.cloned.1.call-start = ((), (), s32[]{:S(2)}) async-start(), calls=%async_computation.17 | async-start | bytes 1966080 | tf_op jit(solution)/shard_map/reduce_scatter | solution.py:278
  494.1 95.1 %all-gather.14.cloned.1.call-start = ((), (), s32[]{:S(2)}) async-start(), calls=%async_computation.16 | async-start | bytes 1966080 | tf_op jit(solution)/shard_map/all_gather | solution.py:283
  511.7 106.0 %all-gather.16.cloned.1.call-start = ((), (), s32[]{:S(2)}) async-start(), calls=%async_computation.18 | async-start | bytes 1966080 | tf_op jit(solution)/shard_map/all_gather | solution.py:283
  554.7 126.2 %reduce-scatter.30.cloned.1.call-start = ((), (), s32[]{:S(2)}) async-start(), calls=%async_computation.26 | async-start | bytes 1966080
  638.1 71.4 %reduce-scatter.28.cloned.1.call-start = ((), (), s32[]{:S(2)}) async-start(), calls=%async_computation.25 | async-start | bytes 1966080
  660.1 131.0 %reduce-scatter.22.cloned.1.call-start = ((), (), s32[]{:S(2)}) async-start(), calls=%async_computation.19 | async-start | bytes 1966080 | tf_op jit(solution)/shard_map/reduce_scatter | solution.py:278
  734.6 73.9 %reduce-scatter.24.cloned.1.call-start = ((), (), s32[]{:S(2)}) async-start(), calls=%async_computation.20 | async-start | bytes 1966080 | tf_op jit(solution)/shard_map/reduce_scatter | solution.py:278
  765.6 145.3 %all-reduce.14.cloned.1.call-start = ((), (), s32[]{:S(2)}) async-start(), calls=%async_computation.21 | async-start | bytes 3244032 | tf_op jit(solution)/shard_map/psum | solution.py:625
  830.3 183.3 %all-gather.18.cloned.1.call-start = ((), (), s32[]{:S(2)}) async-start(), calls=%async_computation.22 | async-start | bytes 3932160 | tf_op jit(solution)/shard_map/all_gather | solution.py:283
  949.4 125.9 %reduce-scatter.26.cloned.1.call-start = ((), (), s32[]{:S(2)}) async-start(), calls=%async_computation.23 | async-start | bytes 3932160 | tf_op jit(solution)/shard_map/reduce_scatter | solution.py:278
  958.9 58.1 %collective-permute-start.47 = (f32[101760]{0:T(1024)}, f32[101760]{0:T(1024)}, u32[]{:S(2)}, u32[]{:S(2)}) collective-permute-start(f32[101760]{0:T(1024)} %pad_maximum_fusion.74), channel_id=1, source_target_pairs={{0,4},{4,0},{8,12},{12,8},{1,5},{5,1},{9,13},{13,9},{2,6},{6,2},{1... | collective-permute-start | bytes 1221128 | tf_op jit(solution)/shard_map/ppermute | solution.py:28
  973.3 65.8 %collective-permute-start.70 = (bf16[2,2,192,1024]{3,2,0,1:T(8,128)(2,1)}, bf16[2,2,192,1024]{3,2,0,1:T(8,128)(2,1)}, u32[]{:S(2)}, u32[]{:S(2)}) collective-permute-start(bf16[2,2,192,1024]{3,2,0,1:T(8,128)(2,1)} %pad_maximum_fusion.22), channel_id=1, source_target_pairs={{0,4},{4,0},{8,12},{12,8},{1,5},{5,1},{9,13},{13,9},{2,6},{6,2},{1... | collective-permute-start | bytes 4718600 | tf_op jit(solution)/shard_map/ppermute | solution.py:28
  1013.7 131.0 %all-gather.20.cloned.1.call-start = ((), (), s32[]{:S(2)}) async-start(), calls=%async_computation.24 | async-start | bytes 3932160 | tf_op jit(solution)/shard_map/all_gather | solution.py:283
  (329 other events, 4647.2 us)
Sparse Core Ops, SparseCore 0:
  122.4 69.2 all-reduce.11
  245.3 63.9 all-gather.7
  324.5 33.7 reduce-scatter.13
  361.1 34.2 reduce-scatter.15
  396.8 35.3 all-gather.9
  433.7 35.8 all-gather.11
  471.9 34.7 reduce-scatter.17
  509.0 34.2 reduce-scatter.19
  544.9 35.3 all-gather.13
  581.7 35.8 all-gather.15
  638.2 34.7 reduce-scatter.29
  675.2 34.2 reduce-scatter.27
  734.7 36.5 reduce-scatter.21
  774.0 34.4 reduce-scatter.23
  830.5 80.3 all-reduce.13
  949.5 64.1 all-gather.17
  1016.4 58.8 reduce-scatter.25
  1079.4 64.0 all-gather.19

commit v8 on v7

--- a/solution.py
+++ b/solution.py
@@ -524,9 +524,9 @@
         )
         one.grad_mixed = collected(one.grad_hidden)
 
-    def branch_out(one):
-        activ = after(one.activ, whole.grad_retrieved)
-        one.branch = scattered(matmul(activ, weights["down"]))
+    def branch_part(one):
+        activ = after(one.activ, last_stream.partial)
+        return matmul(activ, weights["down"]).astype(NARROW)
 
     def rank_major(array):
         array = array.reshape(STREAMS, ranks, -1, width)
@@ -569,7 +569,10 @@
     def remember_back(one):
         later = [0.0] * blocks_each
         pending = {}
+        branches = [item.branch for item in streams]
         for turn in range(parts):
+            if turn == parts // 2:
+                later, branches[0] = lax.optimization_barrier((later, branches[0]))
             for hop in range(1, reach + 1):
                 if (turn - hop, hop) in pending:
                     arrived = pending[(turn - hop, hop)].astype(WIDE)
@@ -617,7 +620,6 @@
             one, grad_mixing[..., SPAN:], grad_mixing[:, :, :CORNER, SPAN - CORNER : SPAN]
         )
         grad_mixing = packed(square.astype(NARROW), corner.astype(NARROW))
-        branches = [item.branch for item in streams]
         grad_mixing, branches = lax.optimization_barrier((grad_mixing, branches))
         for item, branch in zip(streams, branches):
             item.branch = branch
@@ -680,6 +682,8 @@
                     from_reads = jnp.pad(from_reads, ((0, 0), (0, rest), (0, 0)))
                     from_writes = jnp.pad(from_writes, ((0, 0), (rest, 0), (0, 0)))
                 total = total + decays[lag] * (from_reads + from_writes)
+            if own == 0:
+                total, one.output = lax.optimization_barrier((total, one.output))
             grad_features.append(total)
         grad_features = jnp.stack(grad_features, 1).reshape(rows, local_units)
         grad_features = grad_features - (one.key_scale * one.key_scale * one.scale_sum)[
@@ -691,15 +695,8 @@
         one.grad_input = (one.early + by_rows(one.grad_pre, feature_cols)).astype(NARROW)
 
     def input_early(one):
-        queries, keys, values, targets, _ = lax.optimization_barrier(
-            (one.grad_queries, one.key_token, one.value_token, one.grad_targets, one.packed_back)
-        )
-        one.early = (
-            by_rows(queries, query_w)
-            + by_rows(keys, key_w)
-            + by_rows(values, value_w)
-            + by_rows(targets, value_cols)
-        )
+        targets = after(one.grad_targets, one.packed_back)
+        one.early = one.early + by_rows(targets, value_cols)
 
     def tokens_back(one):
         grad_input = one.grad_input
@@ -789,7 +786,11 @@
         )
 
     begin(whole, 0)
-    (qkv_other,) = fetched(whole, ["mixing"], whole.products, w_qkv)
+    qkv_fetch = Holder(flipped(after(w_qkv, whole.products), "shard", 1))
+    next_features = Holder(whole.around[1])
+    tied(whole, ["mixing"], qkv_fetch, next_features)
+    qkv_other = qkv_fetch.array
+    whole.around[1] = next_features.array
     qkv_cols = joined(w_qkv, qkv_other, 1)
     query_w = qkv_cols[0]
     key_w = qkv_cols[1]
@@ -871,24 +872,35 @@
     )
     for item in feed_reductions:
         item.apart()
-    tied(whole, ["grad_retrieved"], *feed_reductions, *mix_reductions)
-    every(branch_out)
+    early = Holder(
+        by_rows(whole.grad_queries, query_w)
+        + by_rows(whole.key_token, key_w)
+        + by_rows(whole.value_token, value_w)
+    )
+    branch_parts = [Holder(branch_part(one)) for one in streams]
+    tied(
+        whole,
+        ["grad_retrieved"],
+        *feed_reductions,
+        *mix_reductions,
+        early,
+        *branch_parts,
+    )
+    whole.early = early.array
+    for one, part_sum in zip(streams, branch_parts):
+        one.branch = scattered(part_sum.array)
     heads_back(whole)
     remember_back(whole)
     persist_sum = Holder(summed_over_ranks(after(grad_persist, whole.packed_back), NARROW))
     input_early(whole)
     grad_targets = after(whole.grad_targets, whole.packed_back)
     target_reduction = Reduction(over_rows(whole.input_low, grad_targets), True)
-    for item in feed_reductions + mix_reductions:
+    for item in mix_reductions:
         item.array = after(item.array, whole.packed_back)
-    for item in feed_reductions:
-        item.together()
-    for item in mix_reductions:
         item.across()
     tied(
         whole,
         ["grad_mixing", "scale_sum", "early"],
-        *feed_reductions,
         *mix_reductions,
         target_reduction,
         persist_sum,
@@ -896,10 +908,8 @@
     finish_output(whole)
     features_back(whole)
     inputs_back(whole)
-    grad_input, whole.output = lax.optimization_barrier(
-        (rank_major(whole.grad_input), whole.output)
-    )
-    whole.grad_input = scattered(grad_input)
+    whole.grad_input_low = rank_major(whole.grad_input)
+    whole.grad_input = scattered(whole.grad_input_low)
     merged("residual")
     merged("grad_hidden")
 
@@ -925,11 +935,21 @@
     small = Holder(summed([persist_sum.array, whole.grad_gain_memory, grad_rates]))
     feature_reduction = Reduction(over_rows(whole.input_low, whole.grad_pre), True)
     late_reductions = [feature_reduction, target_reduction]
+    for item in feed_reductions:
+        item.array = after(item.array, whole.grad_input_low)
+        item.together()
     for item in mix_reductions:
         item.apart()
     for item in late_reductions:
         item.across()
-    tied(whole, ["grad_input"], small, *mix_reductions, *late_reductions)
+    tied(
+        whole,
+        ["grad_input"],
+        small,
+        *feed_reductions,
+        *mix_reductions,
+        *late_reductions,
+    )
     tokens_back(whole)
     for item in mix_reductions:
         item.together()

time: 1170 us -> 1200 us (1.026)
  local copies, waits for them, and re-layouts: 114 us -> 131 us
    ppermute x59, waiting for transfers between devices: 198 us -> 224 us  [flipped(): lax.ppermute(value, axis, [(i, i ^ bit) for i in range(lax.axis_size(axis...]
    reduce_scatter x7, waiting for transfers between devices: 87.5 us -> 63.3 us  [scattered(): lax.psum_scatter(array.astype(NARROW), 'tp', scatter_dimension=0, tiled=T...]
    all_gather x6, waiting for transfers between devices: 35.9 us -> 58 us  [collected(): return lax.all_gather(array.astype(NARROW), 'tp', axis=0, tiled=True)]
    unnamed x20, waiting for transfers between devices: 27.7 us -> 13.4 us
    unnamed x539 -> x559, local copies, waits for them, and re-layouts: 48.3 us -> 54.1 us
  transfers between devices with their start and end apart: 90 -> 90, of which waited for: 41 -> 39; matrix products, arithmetic and copies ran while one was open for 36% -> 35% of each run, Pallas kernels for 1% -> 1%
where the time goes in v8:
time: 1200 us; the launch traced here: 1180 us
  waiting for transfers between devices  477 us (40%)
  matrix products  264 us (22%)
  other arithmetic  177 us (15%)
  local copies, waits for them, and re-layouts  131 us (11%)
  starting transfers between devices  83.9 us (7%)
  Pallas kernels  32.4 us (3%)
  between operations  18.4 us (2%)
    ppermute x59, waiting for transfers between devices, flipped(): lax.ppermute(value, axis, [(i, i ^ bit) for i in range(lax.axis_size(axis...  224 us
    dot_general x25, matrix products, matmul(): return jnp.dot(left, right, preferred_element_type=WIDE)  79.4 us
    dot_general x41, matrix products, batched(): return jnp.einsum(spec, left, right, preferred_element_type=WIDE)  65.8 us
    reduce_scatter x7, waiting for transfers between devices, scattered(): lax.psum_scatter(array.astype(NARROW), 'tp', scatter_dimension=0, tiled=T...  63.3 us
    ppermute x59, starting transfers between devices, flipped(): lax.ppermute(value, axis, [(i, i ^ bit) for i in range(lax.axis_size(axis...  58.8 us
    psum x1, waiting for transfers between devices, begin(): one.mixing = lax.psum(one.products, 'tp')  58.7 us
    all_gather x6, waiting for transfers between devices, collected(): return lax.all_gather(array.astype(NARROW), 'tp', axis=0, tiled=True)  58 us
    dot_general x17, matrix products, by_rows(): lax.dot_general(left, right, (((1,), (1,)), ((), ())), preferred_element_...  58 us
  transfers between devices with their start and end apart: 90, of which 39 were waited for; matrix products, arithmetic and copies ran while one was open for 35% of the time, Pallas kernels for 1%

profile of v8, /device:TPU:1, one launch (start us, length us, event | category | flops | bytes accessed | tf_op | source)
XLA Modules:
  0.0 1183.2 jit_solution(1950400281296722168)
XLA Ops:
  25.4 21.4 %collective-permute-done.6 = bf16[384,1536]{1,0:T(8,128)(2,1)} collective-permute-done((bf16[384,1536]{1,0:T(8,128)(2,1)}, bf16[384,1536]{1,0:T(8,128)(2,1)}, u32[]{:S(2)}, u32[]{:S(2)}) %collective-permute-start.6) | collective-permute-done | bytes 1179680 | tf_op jit(solution)/shard_map/ppermute | solution.py:28
  142.5 10.0 multiply_convert_fusion
  152.5 58.7 %all-reduce.12.cloned.1.call-done = bf16[1056,768]{1,0:T(8,128)(2,1)} async-done(((bf16[1056,768]{1,0:T(8,128)(2,1)}), bf16[1056,768]{1,0:T(8,128)(2,1)}) %all-reduce.12.cloned.1.call-update) | async-done | bytes 1622032 | tf_op jit(solution)/shard_map/psum | solution.py:426
  231.5 10.7 collective-permute-done.16
  282.1 35.7 %collective-permute-done.18 = bf16[384,768]{1,0:T(8,128)(2,1)S(1)} collective-permute-done((bf16[384,768]{1,0:T(8,128)(2,1)S(1)}, bf16[384,768]{1,0:T(8,128)(2,1)S(1)}, u32[]{:S(2)}, u32[]{:S(2)}) %collective-permute-start.18) | collective-permute-done | bytes 589856 | tf_op jit(solution)/shard_map/ppermute | solution.py:28
  318.6 10.4 all-gather.8.cloned.1.call-done
  389.5 25.6 %reduce-scatter.16.cloned.1.call-done = bf16[128,1536]{1,0:T(8,128)(2,1)} async-done(((bf16[512,1536]{1,0:T(8,128)(2,1)}), bf16[128,1536]{1,0:T(8,128)(2,1)}) %reduce-scatter.16.cloned.1.call-update) | async-done | bytes 393232 | tf_op jit(solution)/shard_map/reduce_scatter | solution.py:278
  418.5 22.2 %collective-permute-done.20 = bf16[768,1024]{1,0:T(8,128)(2,1)} collective-permute-done((bf16[768,1024]{1,0:T(8,128)(2,1)}, bf16[768,1024]{1,0:T(8,128)(2,1)}, u32[]{:S(2)}, u32[]{:S(2)}) %collective-permute-start.20) | collective-permute-done | bytes 1572896 | tf_op jit(solution)/shard_map/ppermute | solution.py:28
  440.7 11.2 all-gather.10.cloned.1.call-done
  472.9 16.4 %all-gather.12.cloned.1.call-done = bf16[512,1536]{1,0:T(8,128)(2,1)} async-done(((bf16[128,1536]{1,0:T(8,128)(2,1)}), bf16[512,1536]{1,0:T(8,128)(2,1)}) %all-gather.12.cloned.1.call-update) | async-done | bytes 1572880 | tf_op jit(solution)/shard_map/all_gather | solution.py:283
  555.4 7.6 reduce-scatter.20.cloned.1.call-done
  566.8 35.0 %collective-permute-done.23 = bf16[2,256,768]{2,1,0:T(8,128)(2,1)} collective-permute-done((bf16[2,256,768]{2,1,0:T(8,128)(2,1)}, bf16[2,256,768]{2,1,0:T(8,128)(2,1)}, u32[]{:S(2)}, u32[]{:S(2)}) %collective-permute-start.23) | collective-permute-done | bytes 786464 | tf_op jit(solution)/shard_map/ppermute | solution.py:28
  611.0 10.7 shard_map.239
  640.8 10.3 shard_map.240
  716.4 13.1 %reduce-scatter.28.cloned.1.call-done = bf16[384,512]{1,0:T(8,128)(2,1)} async-done(((bf16[1536,512]{1,0:T(8,128)(2,1)}), bf16[384,512]{1,0:T(8,128)(2,1)}) %reduce-scatter.28.cloned.1.call-update) | async-done | bytes 393232
  786.9 16.2 %reduce-scatter.24.cloned.1.call-done = bf16[128,1536]{1,0:T(8,128)(2,1)} async-done(((bf16[512,1536]{1,0:T(8,128)(2,1)}), bf16[128,1536]{1,0:T(8,128)(2,1)}) %reduce-scatter.24.cloned.1.call-update) | async-done | bytes 393232 | tf_op jit(solution)/shard_map/reduce_scatter | solution.py:278
  852.2 9.1 collective-permute-done.40
  863.2 17.6 %collective-permute-done.41 = bf16[64,1536]{1,0:T(8,128)(2,1)S(1)} collective-permute-done((bf16[64,1536]{1,0:T(8,128)(2,1)S(1)}, bf16[64,1536]{1,0:T(8,128)(2,1)S(1)}, u32[]{:S(2)}, u32[]{:S(2)}) %collective-permute-start.41) | collective-permute-done | bytes 196640 | tf_op jit(solution)/shard_map/ppermute | solution.py:28
  886.2 28.2 %all-reduce.14.cloned.1.call-done = bf16[1056,768]{1,0:T(8,128)(2,1)} async-done(((bf16[1056,768]{1,0:T(8,128)(2,1)}), bf16[1056,768]{1,0:T(8,128)(2,1)}) %all-reduce.14.cloned.1.call-update) | async-done | bytes 1622032 | tf_op jit(solution)/shard_map/psum | solution.py:627
  983.3 25.3 %all-gather.18.cloned.1.call-done = bf16[1024,1536]{1,0:T(8,128)(2,1)} async-done(((bf16[256,1536]{1,0:T(8,128)(2,1)}), bf16[1024,1536]{1,0:T(8,128)(2,1)}) %all-gather.18.cloned.1.call-update) | async-done | bytes 3145744 | tf_op jit(solution)/shard_map/all_gather | solution.py:283
  1066.7 15.8 %collective-permute-done.49 = bf16[2,192,1024]{2,1,0:T(8,128)(2,1)S(1)} collective-permute-done((bf16[2,192,1024]{2,1,0:T(8,128)(2,1)S(1)}, bf16[2,192,1024]{2,1,0:T(8,128)(2,1)S(1)}, u32[]{:S(2)}, u32[]{:S(2)}) %collective-permute-start.49) | collective-permute-done | bytes 786464 | tf_op jit(solution)/shard_map/ppermute | solution.py:28
  1084.2 8.3 reduce-scatter.26.cloned.1.call-done
  1108.1 11.2 collective-permute-done.57
  1145.2 12.1 %collective-permute-done.68 = bf16[192,1536]{1,0:T(8,128)(2,1)S(1)} collective-permute-done((bf16[192,1536]{1,0:T(8,128)(2,1)S(1)}, bf16[192,1536]{1,0:T(8,128)(2,1)S(1)}, u32[]{:S(2)}, u32[]{:S(2)}) %collective-permute-start.68) | collective-permute-done | bytes 589856 | tf_op jit(solution)/shard_map/ppermute | solution.py:28
  (1136 shorter events, 722.0 us)
Async XLA Ops:
  7.2 204.0 %all-reduce.12.cloned.1.call-start = ((), (), s32[]{:S(2)}) async-start(), calls=%async_computation.9 | async-start | bytes 3244032 | tf_op jit(solution)/shard_map/psum | solution.py:426
  7.2 70.2 %collective-permute-start = (bf16[2,512,1536]{2,1,0:T(8,128)(2,1)}, bf16[2,512,1536]{2,1,0:T(8,128)(2,1)}, u32[]{:S(2)}, u32[]{:S(2)}) collective-permute-start(bf16[2,512,1536]{2,1,0:T(8,128)(2,1)} %param.14), channel_id=1, source_target_pairs={{0,8},{4,12},{8,0},{12,4},{1,9},{5,13},{9,1},{13,5},{2,10},{6,14},... | collective-permute-start | bytes 9437192 | tf_op jit(solution)/shard_map/ppermute | solution.py:28
  9.3 68.1 %collective-permute-start.4 = (bf16[2,512,1536]{2,1,0:T(8,128)(2,1)}, bf16[2,512,1536]{2,1,0:T(8,128)(2,1)}, u32[]{:S(2)}, u32[]{:S(2)}) collective-permute-start(bf16[2,512,1536]{2,1,0:T(8,128)(2,1)} %param.14), channel_id=1, source_target_pairs={{0,4},{4,0},{8,12},{12,8},{1,5},{5,1},{9,13},{13,9},{2,6},{6,2},{1... | collective-permute-start | bytes 9437192 | tf_op jit(solution)/shard_map/ppermute | solution.py:28
  141.2 187.8 %all-gather.8.cloned.1.call-start = ((), (), s32[]{:S(2)}) async-start(), calls=%async_computation.10 | async-start | bytes 3932160 | tf_op jit(solution)/shard_map/all_gather | solution.py:473
  141.2 70.0 %collective-permute-start.11 = (bf16[3,768,384]{2,1,0:T(8,128)(2,1)}, bf16[3,768,384]{2,1,0:T(8,128)(2,1)S(1)}, u32[]{:S(2)}, u32[]{:S(2)}) collective-permute-start(bf16[3,768,384]{2,1,0:T(8,128)(2,1)} %param.21), channel_id=1, source_target_pairs={{0,16},{16,0},{1,17},{17,1},{2,18},{18,2},{3,19},{19,3},{4,20},{20... | collective-permute-start | bytes 5308424 | tf_op jit(solution)/shard_map/ppermute | solution.py:28
  264.6 113.5 %reduce-scatter.14.cloned.1.call-start = ((), (), s32[]{:S(2)}) async-start(), calls=%async_computation.11 | async-start | bytes 1966080 | tf_op jit(solution)/shard_map/reduce_scatter | solution.py:278
  344.1 71.0 %reduce-scatter.16.cloned.1.call-start = ((), (), s32[]{:S(2)}) async-start(), calls=%async_computation.13 | async-start | bytes 1966080 | tf_op jit(solution)/shard_map/reduce_scatter | solution.py:278
  365.4 86.6 %all-gather.10.cloned.1.call-start = ((), (), s32[]{:S(2)}) async-start(), calls=%async_computation.12 | async-start | bytes 1966080 | tf_op jit(solution)/shard_map/all_gather | solution.py:283
  381.2 108.1 %all-gather.12.cloned.1.call-start = ((), (), s32[]{:S(2)}) async-start(), calls=%async_computation.15 | async-start | bytes 1966080 | tf_op jit(solution)/shard_map/all_gather | solution.py:283
  381.3 59.4 %collective-permute-start.20 = (bf16[768,1024]{1,0:T(8,128)(2,1)}, bf16[768,1024]{1,0:T(8,128)(2,1)}, u32[]{:S(2)}, u32[]{:S(2)}) collective-permute-start(bf16[768,1024]{1,0:T(8,128)(2,1)} %get-tuple-element.110), channel_id=1, source_target_pairs={{0,16},{16,0},{1,17},{17,1},{2,18},{18,2},{3,19},{19,3},{4,20},{20... | collective-permute-start | bytes 4718600 | tf_op jit(solution)/shard_map/ppermute | solution.py:28
  418.4 119.5 %reduce-scatter.18.cloned.1.call-start = ((), (), s32[]{:S(2)}) async-start(), calls=%async_computation.14 | async-start | bytes 1966080 | tf_op jit(solution)/shard_map/reduce_scatter | solution.py:278
  467.1 95.9 %reduce-scatter.20.cloned.1.call-start = ((), (), s32[]{:S(2)}) async-start(), calls=%async_computation.17 | async-start | bytes 1966080 | tf_op jit(solution)/shard_map/reduce_scatter | solution.py:278
  512.0 95.4 %all-gather.14.cloned.1.call-start = ((), (), s32[]{:S(2)}) async-start(), calls=%async_computation.16 | async-start | bytes 1966080 | tf_op jit(solution)/shard_map/all_gather | solution.py:283
  542.8 94.5 %all-gather.16.cloned.1.call-start = ((), (), s32[]{:S(2)}) async-start(), calls=%async_computation.18 | async-start | bytes 1966080 | tf_op jit(solution)/shard_map/all_gather | solution.py:283
  566.8 148.4 %reduce-scatter.30.cloned.1.call-start = ((), (), s32[]{:S(2)}) async-start(), calls=%async_computation.26 | async-start | bytes 1966080
  658.1 71.4 %reduce-scatter.28.cloned.1.call-start = ((), (), s32[]{:S(2)}) async-start(), calls=%async_computation.25 | async-start | bytes 1966080
  688.5 79.6 %reduce-scatter.22.cloned.1.call-start = ((), (), s32[]{:S(2)}) async-start(), calls=%async_computation.19 | async-start | bytes 1966080 | tf_op jit(solution)/shard_map/reduce_scatter | solution.py:278
  730.8 72.3 %reduce-scatter.24.cloned.1.call-start = ((), (), s32[]{:S(2)}) async-start(), calls=%async_computation.20 | async-start | bytes 1966080 | tf_op jit(solution)/shard_map/reduce_scatter | solution.py:278
  745.4 168.9 %all-reduce.14.cloned.1.call-start = ((), (), s32[]{:S(2)}) async-start(), calls=%async_computation.21 | async-start | bytes 3244032 | tf_op jit(solution)/shard_map/psum | solution.py:627
  835.5 173.0 %all-gather.18.cloned.1.call-start = ((), (), s32[]{:S(2)}) async-start(), calls=%async_computation.22 | async-start | bytes 3932160 | tf_op jit(solution)/shard_map/all_gather | solution.py:283
  944.9 147.6 %reduce-scatter.26.cloned.1.call-start = ((), (), s32[]{:S(2)}) async-start(), calls=%async_computation.23 | async-start | bytes 3932160 | tf_op jit(solution)/shard_map/reduce_scatter | solution.py:278
  959.6 77.0 %collective-permute-start.45 = (f32[101760]{0:T(1024)}, f32[101760]{0:T(1024)}, u32[]{:S(2)}, u32[]{:S(2)}) collective-permute-start(f32[101760]{0:T(1024)} %pad_maximum_fusion.74), channel_id=1, source_target_pairs={{0,4},{4,0},{8,12},{12,8},{1,5},{5,1},{9,13},{13,9},{2,6},{6,2},{1... | collective-permute-start | bytes 1221128 | tf_op jit(solution)/shard_map/ppermute | solution.py:28
  963.0 77.6 %collective-permute-start.50 = (bf16[96,768]{1,0:T(8,128)(2,1)}, bf16[96,768]{1,0:T(8,128)(2,1)}, u32[]{:S(2)}, u32[]{:S(2)}) collective-permute-start(bf16[96,768]{1,0:T(8,128)(2,1)} %dynamic-slice_bitcast_fusion.15), channel_id=1, source_target_pairs={{0,8},{4,12},{8,0},{12,4},{1,9},{5,13},{9,1},{13,5},{2,10},{6,14},... | collective-permute-start | bytes 442376 | tf_op jit(solution)/shard_map/ppermute | solution.py:28
  1033.5 136.8 %all-gather.20.cloned.1.call-start = ((), (), s32[]{:S(2)}) async-start(), calls=%async_computation.24 | async-start | bytes 3932160 | tf_op jit(solution)/shard_map/all_gather | solution.py:283
  (338 other events, 4218.4 us)
Sparse Core Ops, SparseCore 0:
  141.3 69.8 all-reduce.11
  264.7 64.2 all-gather.7
  344.2 33.7 reduce-scatter.13
  380.8 34.2 reduce-scatter.15
  416.5 35.3 all-gather.9
  453.4 35.8 all-gather.11
  491.6 34.7 reduce-scatter.17
  528.7 34.2 reduce-scatter.19
  564.6 35.3 all-gather.13
  601.4 35.8 all-gather.15
  658.2 34.7 reduce-scatter.29
  695.2 34.2 reduce-scatter.27
  731.8 34.2 reduce-scatter.21
  768.9 34.2 reduce-scatter.23
  835.6 78.7 all-reduce.13
  945.0 63.4 all-gather.17
  1033.6 58.8 reduce-scatter.25
  1096.7 64.0 all-gather.19

commit v9 on v8

--- a/solution.py
+++ b/solution.py
@@ -396,12 +396,12 @@
         )
         close = [pair, flipped(far, "ctx", 1)]
         one.around = {0: shaped(one.features)}
-        for delta, piece in (
-            (-1, jnp.where(odd_part, close[0], close[1])),
-            (1, jnp.where(odd_part, close[1], close[0])),
-            (2, far),
-        ):
-            one.around[delta] = shaped(jax.nn.silu(features_of(piece)[1]).astype(NARROW))
+        one.features_around = lambda piece: shaped(
+            jax.nn.silu(features_of(piece)[1]).astype(NARROW)
+        )
+        one.next_piece = jnp.where(odd_part, close[1], close[0])
+        one.around[-1] = one.features_around(jnp.where(odd_part, close[0], close[1]))
+        one.around[2] = one.features_around(far)
         one.around[-2] = one.around[2]
         one.targets = matmul(one.input_low, value_cols).reshape(
             count, blocks_each, SPAN, local_width
@@ -569,10 +569,11 @@
     def remember_back(one):
         later = [0.0] * blocks_each
         pending = {}
-        branches = [item.branch for item in streams]
         for turn in range(parts):
             if turn == parts // 2:
-                later, branches[0] = lax.optimization_barrier((later, branches[0]))
+                later, first_stream.branch = lax.optimization_barrier(
+                    (later, first_stream.branch)
+                )
             for hop in range(1, reach + 1):
                 if (turn - hop, hop) in pending:
                     arrived = pending[(turn - hop, hop)].astype(WIDE)
@@ -620,9 +621,6 @@
             one, grad_mixing[..., SPAN:], grad_mixing[:, :, :CORNER, SPAN - CORNER : SPAN]
         )
         grad_mixing = packed(square.astype(NARROW), corner.astype(NARROW))
-        grad_mixing, branches = lax.optimization_barrier((grad_mixing, branches))
-        for item, branch in zip(streams, branches):
-            item.branch = branch
         one.packed_back = grad_mixing
         one.grad_mixing = lax.psum(grad_mixing, "tp")
 
@@ -682,8 +680,6 @@
                     from_reads = jnp.pad(from_reads, ((0, 0), (0, rest), (0, 0)))
                     from_writes = jnp.pad(from_writes, ((0, 0), (rest, 0), (0, 0)))
                 total = total + decays[lag] * (from_reads + from_writes)
-            if own == 0:
-                total, one.output = lax.optimization_barrier((total, one.output))
             grad_features.append(total)
         grad_features = jnp.stack(grad_features, 1).reshape(rows, local_units)
         grad_features = grad_features - (one.key_scale * one.key_scale * one.scale_sum)[
@@ -787,10 +783,8 @@
 
     begin(whole, 0)
     qkv_fetch = Holder(flipped(after(w_qkv, whole.products), "shard", 1))
-    next_features = Holder(whole.around[1])
-    tied(whole, ["mixing"], qkv_fetch, next_features)
+    tied(whole, ["mixing"], qkv_fetch)
     qkv_other = qkv_fetch.array
-    whole.around[1] = next_features.array
     qkv_cols = joined(w_qkv, qkv_other, 1)
     query_w = qkv_cols[0]
     key_w = qkv_cols[1]
@@ -798,6 +792,9 @@
     fixed_keys = matmul(persist, key_w).astype(NARROW)
     fixed_values = matmul(persist, value_w).astype(NARROW)
     remember(whole)
+    next_features = Holder(whole.features_around(after(whole.next_piece, whole.recall)))
+    tied(whole, ["retrieved_full"], next_features)
+    whole.around[1] = next_features.array
     out_other, down_other = fetched(whole, ["retrieved_full"], whole.recall, w_out, w_down)
     weights["out"] = joined(w_out, out_other, 1)
     weights["down"] = joined(w_down, down_other, 1)
@@ -887,14 +884,12 @@
         *branch_parts,
     )
     whole.early = early.array
-    for one, part_sum in zip(streams, branch_parts):
-        one.branch = scattered(part_sum.array)
+    first_stream.branch = scattered(branch_parts[0].array)
     heads_back(whole)
     remember_back(whole)
+    last_branch = Holder(scattered(branch_parts[-1].array))
     persist_sum = Holder(summed_over_ranks(after(grad_persist, whole.packed_back), NARROW))
     input_early(whole)
-    grad_targets = after(whole.grad_targets, whole.packed_back)
-    target_reduction = Reduction(over_rows(whole.input_low, grad_targets), True)
     for item in mix_reductions:
         item.array = after(item.array, whole.packed_back)
         item.across()
@@ -902,13 +897,16 @@
         whole,
         ["grad_mixing", "scale_sum", "early"],
         *mix_reductions,
-        target_reduction,
         persist_sum,
-    )
+        last_branch,
+    )
+    last_stream.branch = last_branch.array
     finish_output(whole)
     features_back(whole)
     inputs_back(whole)
-    whole.grad_input_low = rank_major(whole.grad_input)
+    whole.grad_input_low, whole.output = lax.optimization_barrier(
+        (rank_major(whole.grad_input), whole.output)
+    )
     whole.grad_input = scattered(whole.grad_input_low)
     merged("residual")
     merged("grad_hidden")
@@ -934,6 +932,8 @@
 
     small = Holder(summed([persist_sum.array, whole.grad_gain_memory, grad_rates]))
     feature_reduction = Reduction(over_rows(whole.input_low, whole.grad_pre), True)
+    grad_targets = after(whole.grad_targets, whole.grad_input_low)
+    target_reduction = Reduction(over_rows(whole.input_low, grad_targets), True)
     late_reductions = [feature_reduction, target_reduction]
     for item in feed_reductions:
         item.array = after(item.array, whole.grad_input_low)

time: 1200 us -> 1150 us (0.958)
  waiting for transfers between devices: 477 us -> 441 us
    ppermute x59, waiting for transfers between devices: 224 us -> 162 us  [flipped(): lax.ppermute(value, axis, [(i, i ^ bit) for i in range(lax.axis_size(axis...]
    all_gather x1, waiting for transfers between devices: 10.4 us -> 43.7 us  [remember(): one.retrieved_full = lax.all_gather(retrieved, 'tp', axis=1, tiled=True)]
    all_gather x6, waiting for transfers between devices: 58 us -> 39.5 us  [collected(): return lax.all_gather(array.astype(NARROW), 'tp', axis=0, tiled=True)]
    psum x1, waiting for transfers between devices: 28.2 us -> 41.7 us  [remember_back(): one.grad_mixing = lax.psum(grad_mixing, 'tp')]
    unnamed x559 -> x551, local copies, waits for them, and re-layouts: 54.1 us -> 55.6 us
  transfers between devices with their start and end apart: 90 -> 90, of which waited for: 39 -> 37; matrix products, arithmetic and copies ran while one was open for 35% -> 38% of each run, Pallas kernels for 1% -> 1%
where the time goes in v9:
time: 1150 us; the launch traced here: 1140 us
  waiting for transfers between devices  441 us (38%)
  matrix products  263 us (23%)
  other arithmetic  169 us (15%)
  local copies, waits for them, and re-layouts  130 us (11%)
  starting transfers between devices  86.7 us (8%)
  Pallas kernels  32.6 us (3%)
  between operations  18.3 us (2%)
    ppermute x59, waiting for transfers between devices, flipped(): lax.ppermute(value, axis, [(i, i ^ bit) for i in range(lax.axis_size(axis...  162 us
    dot_general x25, matrix products, matmul(): return jnp.dot(left, right, preferred_element_type=WIDE)  80.7 us
    psum x1, waiting for transfers between devices, begin(): one.mixing = lax.psum(one.products, 'tp')  66.1 us
    dot_general x41, matrix products, batched(): return jnp.einsum(spec, left, right, preferred_element_type=WIDE)  62.7 us
    reduce_scatter x7, waiting for transfers between devices, scattered(): lax.psum_scatter(array.astype(NARROW), 'tp', scatter_dimension=0, tiled=T...  62 us
    ppermute x59, starting transfers between devices, flipped(): lax.ppermute(value, axis, [(i, i ^ bit) for i in range(lax.axis_size(axis...  61.8 us
    dot_general x17, matrix products, by_rows(): lax.dot_general(left, right, (((1,), (1,)), ((), ())), preferred_element_...  61.4 us
    unnamed x551, local copies, waits for them, and re-layouts  55.6 us
  transfers between devices with their start and end apart: 90, of which 37 were waited for; matrix products, arithmetic and copies ran while one was open for 38% of the time, Pallas kernels for 1%

profile of v9, /device:TPU:1, one launch (start us, length us, event | category | flops | bytes accessed | tf_op | source)
XLA Modules:
  0.0 1140.7 jit_solution(9647348859894133618)
XLA Ops:
  31.4 15.5 %collective-permute-done.6 = bf16[384,1536]{1,0:T(8,128)(2,1)} collective-permute-done((bf16[384,1536]{1,0:T(8,128)(2,1)}, bf16[384,1536]{1,0:T(8,128)(2,1)}, u32[]{:S(2)}, u32[]{:S(2)}) %collective-permute-start.6) | collective-permute-done | bytes 1179680 | tf_op jit(solution)/shard_map/ppermute | solution.py:28
  68.5 9.0 collective-permute-done
  125.7 66.1 %all-reduce.12.cloned.1.call-done = bf16[1056,768]{1,0:T(8,128)(2,1)} async-done(((bf16[1056,768]{1,0:T(8,128)(2,1)}), bf16[1056,768]{1,0:T(8,128)(2,1)}) %all-reduce.12.cloned.1.call-update) | async-done | bytes 1622032 | tf_op jit(solution)/shard_map/psum | solution.py:426
  253.1 7.0 multiply_convert_fusion
  260.1 43.7 %all-gather.8.cloned.1.call-done = bf16[1024,1536]{1,0:T(8,128)(2,1)} async-done(((bf16[1024,384]{1,0:T(8,128)(2,1)}), bf16[1024,1536]{1,0:T(8,128)(2,1)}) %all-gather.8.cloned.1.call-update) | async-done | bytes 3145744 | tf_op jit(solution)/shard_map/all_gather | solution.py:473
  365.4 25.7 %reduce-scatter.16.cloned.1.call-done = bf16[128,1536]{1,0:T(8,128)(2,1)} async-done(((bf16[512,1536]{1,0:T(8,128)(2,1)}), bf16[128,1536]{1,0:T(8,128)(2,1)}) %reduce-scatter.16.cloned.1.call-update) | async-done | bytes 393232 | tf_op jit(solution)/shard_map/reduce_scatter | solution.py:278
  394.9 21.8 %collective-permute-done.20 = bf16[768,1024]{1,0:T(8,128)(2,1)} collective-permute-done((bf16[768,1024]{1,0:T(8,128)(2,1)}, bf16[768,1024]{1,0:T(8,128)(2,1)}, u32[]{:S(2)}, u32[]{:S(2)}) %collective-permute-start.20) | collective-permute-done | bytes 1572896 | tf_op jit(solution)/shard_map/ppermute | solution.py:28
  416.7 11.2 all-gather.10.cloned.1.call-done
  448.9 16.4 %all-gather.12.cloned.1.call-done = bf16[512,1536]{1,0:T(8,128)(2,1)} async-done(((bf16[128,1536]{1,0:T(8,128)(2,1)}), bf16[512,1536]{1,0:T(8,128)(2,1)}) %all-gather.12.cloned.1.call-update) | async-done | bytes 1572880 | tf_op jit(solution)/shard_map/all_gather | solution.py:283
  543.4 34.9 %collective-permute-done.23 = bf16[2,256,768]{2,1,0:T(8,128)(2,1)} collective-permute-done((bf16[2,256,768]{2,1,0:T(8,128)(2,1)}, bf16[2,256,768]{2,1,0:T(8,128)(2,1)}, u32[]{:S(2)}, u32[]{:S(2)}) %collective-permute-start.23) | collective-permute-done | bytes 786464 | tf_op jit(solution)/shard_map/ppermute | solution.py:28
  587.6 10.7 shard_map.239
  616.8 10.3 shard_map.240
  692.5 13.0 %reduce-scatter.28.cloned.1.call-done = bf16[384,512]{1,0:T(8,128)(2,1)} async-done(((bf16[1536,512]{1,0:T(8,128)(2,1)}), bf16[384,512]{1,0:T(8,128)(2,1)}) %reduce-scatter.28.cloned.1.call-update) | async-done | bytes 393232
  767.2 11.4 reduce-scatter.24.cloned.1.call-done
  808.9 7.9 convolution_add_fusion
  819.8 21.1 %collective-permute-done.40 = bf16[64,1536]{1,0:T(8,128)(2,1)S(1)} collective-permute-done((bf16[64,1536]{1,0:T(8,128)(2,1)S(1)}, bf16[64,1536]{1,0:T(8,128)(2,1)S(1)}, u32[]{:S(2)}, u32[]{:S(2)}) %collective-permute-start.40) | collective-permute-done | bytes 196640 | tf_op jit(solution)/shard_map/ppermute | solution.py:28
  844.1 41.7 %all-reduce.14.cloned.1.call-done = bf16[1056,768]{1,0:T(8,128)(2,1)} async-done(((bf16[1056,768]{1,0:T(8,128)(2,1)}), bf16[1056,768]{1,0:T(8,128)(2,1)}) %all-reduce.14.cloned.1.call-update) | async-done | bytes 1622032 | tf_op jit(solution)/shard_map/psum | solution.py:625
  925.2 7.2 multiply_reduce_fusion.3
  962.9 7.2 add_convert_fusion
  980.9 7.4 all-gather.18.cloned.1.call-done
  1016.5 8.7 collective-permute-done.52
  1037.6 12.3 %reduce-scatter.26.cloned.1.call-done = bf16[256,1536]{1,0:T(8,128)(2,1)} async-done(((bf16[1024,1536]{1,0:T(8,128)(2,1)}), bf16[256,1536]{1,0:T(8,128)(2,1)}) %reduce-scatter.26.cloned.1.call-update) | async-done | bytes 786448 | tf_op jit(solution)/shard_map/reduce_scatter | solution.py:278
  1065.5 11.2 collective-permute-done.57
  1102.6 12.1 %collective-permute-done.68 = bf16[192,1536]{1,0:T(8,128)(2,1)S(1)} collective-permute-done((bf16[192,1536]{1,0:T(8,128)(2,1)S(1)}, bf16[192,1536]{1,0:T(8,128)(2,1)S(1)}, u32[]{:S(2)}, u32[]{:S(2)}) %collective-permute-start.68) | collective-permute-done | bytes 589856 | tf_op jit(solution)/shard_map/ppermute | solution.py:28
  (1129 shorter events, 688.8 us)
Async XLA Ops:
  7.2 184.7 %all-reduce.12.cloned.1.call-start = ((), (), s32[]{:S(2)}) async-start(), calls=%async_computation.9 | async-start | bytes 3244032 | tf_op jit(solution)/shard_map/psum | solution.py:426
  7.2 70.2 %collective-permute-start = (bf16[2,512,1536]{2,1,0:T(8,128)(2,1)}, bf16[2,512,1536]{2,1,0:T(8,128)(2,1)}, u32[]{:S(2)}, u32[]{:S(2)}) collective-permute-start(bf16[2,512,1536]{2,1,0:T(8,128)(2,1)} %param.14), channel_id=1, source_target_pairs={{0,8},{4,12},{8,0},{12,4},{1,9},{5,13},{9,1},{13,5},{2,10},{6,14},... | collective-permute-start | bytes 9437192 | tf_op jit(solution)/shard_map/ppermute | solution.py:28
  9.3 68.1 %collective-permute-start.4 = (bf16[2,512,1536]{2,1,0:T(8,128)(2,1)}, bf16[2,512,1536]{2,1,0:T(8,128)(2,1)}, u32[]{:S(2)}, u32[]{:S(2)}) collective-permute-start(bf16[2,512,1536]{2,1,0:T(8,128)(2,1)} %param.14), channel_id=1, source_target_pairs={{0,4},{4,0},{8,12},{12,8},{1,5},{5,1},{9,13},{13,9},{2,6},{6,2},{1... | collective-permute-start | bytes 9437192 | tf_op jit(solution)/shard_map/ppermute | solution.py:28
  121.2 70.6 %collective-permute-start.11 = (bf16[3,768,384]{2,1,0:T(8,128)(2,1)}, bf16[3,768,384]{2,1,0:T(8,128)(2,1)}, u32[]{:S(2)}, u32[]{:S(2)}) collective-permute-start(bf16[3,768,384]{2,1,0:T(8,128)(2,1)} %param.21), channel_id=1, source_target_pairs={{0,16},{16,0},{1,17},{17,1},{2,18},{18,2},{3,19},{19,3},{4,20},{20... | collective-permute-start | bytes 5308424 | tf_op jit(solution)/shard_map/ppermute | solution.py:28
  122.4 181.4 %all-gather.8.cloned.1.call-start = ((), (), s32[]{:S(2)}) async-start(), calls=%async_computation.10 | async-start | bytes 3932160 | tf_op jit(solution)/shard_map/all_gather | solution.py:473
  240.2 113.8 %reduce-scatter.14.cloned.1.call-start = ((), (), s32[]{:S(2)}) async-start(), calls=%async_computation.11 | async-start | bytes 1966080 | tf_op jit(solution)/shard_map/reduce_scatter | solution.py:278
  320.1 71.0 %reduce-scatter.16.cloned.1.call-start = ((), (), s32[]{:S(2)}) async-start(), calls=%async_computation.13 | async-start | bytes 1966080 | tf_op jit(solution)/shard_map/reduce_scatter | solution.py:278
  341.3 86.7 %all-gather.10.cloned.1.call-start = ((), (), s32[]{:S(2)}) async-start(), calls=%async_computation.12 | async-start | bytes 1966080 | tf_op jit(solution)/shard_map/all_gather | solution.py:283
  357.2 108.1 %all-gather.12.cloned.1.call-start = ((), (), s32[]{:S(2)}) async-start(), calls=%async_computation.15 | async-start | bytes 1966080 | tf_op jit(solution)/shard_map/all_gather | solution.py:283
  357.3 59.4 %collective-permute-start.20 = (bf16[768,1024]{1,0:T(8,128)(2,1)}, bf16[768,1024]{1,0:T(8,128)(2,1)}, u32[]{:S(2)}, u32[]{:S(2)}) collective-permute-start(bf16[768,1024]{1,0:T(8,128)(2,1)} %get-tuple-element.112), channel_id=1, source_target_pairs={{0,16},{16,0},{1,17},{17,1},{2,18},{18,2},{3,19},{19,3},{4,20},{20... | collective-permute-start | bytes 4718600 | tf_op jit(solution)/shard_map/ppermute | solution.py:28
  394.4 119.6 %reduce-scatter.18.cloned.1.call-start = ((), (), s32[]{:S(2)}) async-start(), calls=%async_computation.14 | async-start | bytes 1966080 | tf_op jit(solution)/shard_map/reduce_scatter | solution.py:278
  443.2 95.8 %reduce-scatter.20.cloned.1.call-start = ((), (), s32[]{:S(2)}) async-start(), calls=%async_computation.17 | async-start | bytes 1966080 | tf_op jit(solution)/shard_map/reduce_scatter | solution.py:278
  488.0 96.0 %all-gather.14.cloned.1.call-start = ((), (), s32[]{:S(2)}) async-start(), calls=%async_computation.16 | async-start | bytes 1966080 | tf_op jit(solution)/shard_map/all_gather | solution.py:283
  519.5 93.9 %all-gather.16.cloned.1.call-start = ((), (), s32[]{:S(2)}) async-start(), calls=%async_computation.18 | async-start | bytes 1966080 | tf_op jit(solution)/shard_map/all_gather | solution.py:283
  543.4 147.9 %reduce-scatter.30.cloned.1.call-start = ((), (), s32[]{:S(2)}) async-start(), calls=%async_computation.26 | async-start | bytes 1966080
  634.1 71.4 %reduce-scatter.28.cloned.1.call-start = ((), (), s32[]{:S(2)}) async-start(), calls=%async_computation.25 | async-start | bytes 1966080
  664.6 84.4 %reduce-scatter.22.cloned.1.call-start = ((), (), s32[]{:S(2)}) async-start(), calls=%async_computation.19 | async-start | bytes 1966080 | tf_op jit(solution)/shard_map/reduce_scatter | solution.py:278
  706.9 71.8 %reduce-scatter.24.cloned.1.call-start = ((), (), s32[]{:S(2)}) async-start(), calls=%async_computation.21 | async-start | bytes 1966080 | tf_op jit(solution)/shard_map/reduce_scatter | solution.py:278
  726.3 159.5 %all-reduce.14.cloned.1.call-start = ((), (), s32[]{:S(2)}) async-start(), calls=%async_computation.20 | async-start | bytes 3244032 | tf_op jit(solution)/shard_map/psum | solution.py:625
  806.0 182.4 %all-gather.18.cloned.1.call-start = ((), (), s32[]{:S(2)}) async-start(), calls=%async_computation.22 | async-start | bytes 3932160 | tf_op jit(solution)/shard_map/all_gather | solution.py:283
  924.0 125.9 %reduce-scatter.26.cloned.1.call-start = ((), (), s32[]{:S(2)}) async-start(), calls=%async_computation.23 | async-start | bytes 3932160 | tf_op jit(solution)/shard_map/reduce_scatter | solution.py:278
  935.9 65.4 %collective-permute-start.49 = (bf16[96,768]{1,0:T(8,128)(2,1)}, bf16[96,768]{1,0:T(8,128)(2,1)}, u32[]{:S(2)}, u32[]{:S(2)}) collective-permute-start(bf16[96,768]{1,0:T(8,128)(2,1)} %dynamic-slice_bitcast_fusion.15), channel_id=1, source_target_pairs={{0,8},{4,12},{8,0},{12,4},{1,9},{5,13},{9,1},{13,5},{2,10},{6,14},... | collective-permute-start | bytes 442376 | tf_op jit(solution)/shard_map/ppermute | solution.py:28
  943.0 59.9 %collective-permute-start.50 = (bf16[3,192,384]{2,1,0:T(8,128)(2,1)}, bf16[3,192,384]{2,1,0:T(8,128)(2,1)}, u32[]{:S(2)}, u32[]{:S(2)}) collective-permute-start(bf16[3,192,384]{2,1,0:T(8,128)(2,1)} %dynamic-slice_bitcast_fusion.11), channel_id=1, source_target_pairs={{0,8},{4,12},{8,0},{12,4},{1,9},{5,13},{9,1},{13,5},{2,10},{6,14},... | collective-permute-start | bytes 1327112 | tf_op jit(solution)/shard_map/ppermute | solution.py:28
  988.3 139.4 %all-gather.20.cloned.1.call-start = ((), (), s32[]{:S(2)}) async-start(), calls=%async_computation.24 | async-start | bytes 3932160 | tf_op jit(solution)/shard_map/all_gather | solution.py:283
  (334 other events, 5254.1 us)
Sparse Core Ops, SparseCore 0:
  122.6 69.2 all-reduce.11
  240.3 63.5 all-gather.7
  320.2 33.7 reduce-scatter.13
  356.8 34.2 reduce-scatter.15
  392.5 35.3 all-gather.9
  429.4 35.8 all-gather.11
  467.6 34.7 reduce-scatter.17
  504.7 34.2 reduce-scatter.19
  540.6 35.3 all-gather.13
  577.4 35.8 all-gather.15
  634.2 34.7 reduce-scatter.29
  671.2 34.2 reduce-scatter.27
  707.8 34.2 reduce-scatter.21
  744.3 34.2 reduce-scatter.23
  806.1 79.6 all-reduce.13
  924.1 64.1 all-gather.17
  991.0 58.8 reduce-scatter.25
  1054.1 64.0 all-gather.19
